TPU v7x, 32 devices: a whole 2x2x4 slice. The times are simulated.
32 devices in a mesh: outer: 4 (over y, x), inner: 8 (over z, core).
Axes of the slice: x: 2, y: 2, z: 4, core: 2. Of those that a mesh axis runs over, the one named last changes fastest.
Arguments:
- p_factor: bfloat16 [56, 56, 16384], P('outer', None, 'inner'), may hold values from -24 to 24
- q_factor: bfloat16 [56, 56, 16384], P(None, None, 'inner'), may hold values from -6 to 6
- truncation: bfloat16 [3136, 56], P('outer'), may hold values from -0.109375 to 0.109375
Outputs:
- gram: float32 [3136, 3136], P('outer', 'inner')
- coarse: float32 [56, 16384], P(None, 'inner')
All inputs are finite; a program needn't handle non-finite values.
Results may differ from a plain program's by a relative error of at most 0.003.
Values may be sent and summed in bfloat16 or wider, within the bound.
No kernel may reach another device: no remote copies, remote signals or barrier semaphores. Data moves between devices by JAX's collectives and lax.ppermute only.
A program may use at most 128 MiB of HBM per device.

v0:
```python
import math

import jax
import jax.numpy as jnp
from jax import lax
from jax.sharding import PartitionSpec as P


def contract(factor, q_factor):
    bond_size = q_factor.shape[0]
    paired = jnp.einsum("imc,jmc->ijc", factor, q_factor, preferred_element_type=jnp.float32)
    paired = paired / math.sqrt(q_factor.shape[1])
    return paired.reshape(factor.shape[0] * bond_size, factor.shape[2]).astype(jnp.bfloat16)


def body(p_factor, q_factor, truncation):
    columns = p_factor.shape[2]
    own_rows = contract(p_factor, q_factor)
    gathered = lax.all_gather(own_rows, "outer", axis=0, tiled=True)
    partial_value = lax.dot_general(
        own_rows, gathered, (((1,), (1,)), ((), ())), preferred_element_type=jnp.float32
    )
    total_columns = columns * lax.axis_size("inner")
    gram = lax.psum_scatter(partial_value, "inner", scatter_dimension=1, tiled=True) / total_columns
    local_term = lax.dot_general(
        truncation, own_rows, (((0,), (0,)), ((), ())), preferred_element_type=jnp.float32
    )
    absorbed = lax.psum(local_term, "outer")
    squares = lax.psum(jnp.sum(absorbed * absorbed), "inner")
    norm_scale = jnp.sqrt(squares / (absorbed.shape[0] * total_columns) + 1e-06)
    return (gram, absorbed / norm_scale)


def solution(mesh):
    return jax.shard_map(
        body,
        mesh=mesh,
        in_specs=(P("outer", None, "inner"), P(None, None, "inner"), P("outer", None)),
        out_specs=(P("outer", "inner"), P(None, "inner")),
        check_vma=False,
    )
```

profile of v0, /device:TPU:8, one launch (start us, length us, event | category | flops | bytes accessed | tf_op | source)
XLA Modules:
  0.0 380.9 jit_solution(4690721399324301520)
XLA Ops:
  7.2 0.0 copy-start
  7.2 0.0 all-gather.2.cloned.1.call-start
  7.2 10.5 %copy.11 = bf16[14,56,2048]{1,0,2:T(8,128)(2,1)} copy(bf16[14,56,2048]{2,1,0:T(8,128)(2,1)} %param.3) | data formatting | bytes 6422528 | tf_op args[0]
  17.7 31.2 %copy.10 = bf16[56,56,2048]{1,0,2:T(8,128)(2,1)} copy(bf16[56,56,2048]{2,1,0:T(8,128)(2,1)} %param.4) | data formatting | bytes 25690112 | tf_op args[1]
  48.9 22.2 %fusion = bf16[14,56,2048]{1,0,2:T(8,128)(2,1)} fusion(bf16[56,56,2048]{1,0,2:T(8,128)(2,1)} %copy.10, bf16[14,56,2048]{1,0,2:T(8,128)(2,1)} %copy.11), kind=kOutput, calls=%fused_computation.1 | convolution fusion | flops 183042048 | bytes 19267584 | tf_op jit(solution)/shard_map/imc,jmc->ijc/dot_general | solution.py:11
  71.1 9.8 %copy.12 = bf16[14,56,2048]{2,1,0:T(8,128)(2,1)} copy(bf16[14,56,2048]{1,0,2:T(8,128)(2,1)} %fusion) | data formatting | bytes 6422528 | tf_op jit(solution)/shard_map/convert_element_type | solution.py:13
  80.9 0.0 copy-start.2
  80.9 0.0 all-gather.2.cloned.1.call-update
  80.9 0.0 all-reduce.3.cloned.1.call-start
  81.0 0.0 copy-done
  81.0 3.6 convolution_bitcast_fusion
  84.6 0.0 all-reduce.3.cloned.1.call-update
  84.6 0.0 reduce-scatter.4.cloned.1.call-start
  84.6 122.3 %all-gather.2.cloned.1.call-done = bf16[3136,2048]{1,0:T(8,128)(2,1)} async-done(((bf16[784,2048]{1,0:T(8,128)(2,1)}), bf16[3136,2048]{1,0:T(8,128)(2,1)}) %all-gather.2.cloned.1.call-update) | async-done | bytes 12845072 | tf_op jit(solution)/shard_map/all_gather | solution.py:19
  207.0 0.0 copy-done.2
  207.0 18.3 %fusion.1 = f32[784,3136]{0,1:T(8,128)} fusion(bf16[784,2048]{1,0:T(8,128)(2,1)S(1)} %bitcast.14, bf16[3136,2048]{1,0:T(8,128)(2,1)} %all-gather.2.cloned.1.call-done), kind=kOutput, calls=%fused_computation.6 | convolution fusion | flops 10070523904 | bytes 25890816 | tf_op jit(solution)/shard_map/dot_general | solution.py:20
  225.2 0.0 reduce-scatter.4.cloned.1.call-update
  225.2 30.0 %all-reduce.3.cloned.1.call-done = f32[56,2048]{1,0:T(8,128)} async-done(((f32[56,2048]{1,0:T(8,128)}), f32[56,2048]{1,0:T(8,128)}) %all-reduce.3.cloned.1.call-update) | async-done | bytes 458768 | tf_op jit(solution)/shard_map/psum | solution.py:28
  255.2 1.7 multiply_reduce_fusion
  257.0 13.2 %psum.15 = f32[]{:T(128)} all-reduce(f32[]{:T(128)} %multiply_reduce_fusion), channel_id=1, replica_groups=mesh['outer'=4,'inner'=8] {'inner'}, use_global_device_ids=true, to_apply=%region_3.0 | all-reduce | flops 1 | bytes 8 | tf_op jit(solution)/shard_map/psum | solution.py:29
  270.8 1.8 broadcast_divide_fusion
  272.7 99.1 %reduce-scatter.4.cloned.1.call-done = f32[784,392]{0,1:T(8,128)} async-done(((f32[784,3136]{0,1:T(8,128)}), f32[784,392]{0,1:T(8,128)}) %reduce-scatter.4.cloned.1.call-update) | async-done | bytes 1229328
  371.8 2.5 broadcast_multiply_fusion
  374.3 0.0 copy-done.1
  (1 shorter events, 0.0 us)
Async XLA Ops:
  7.2 73.8 %copy-start = (bf16[784,56]{0,1:T(8,128)(2,1)S(1)}, bf16[784,56]{0,1:T(8,128)(2,1)}, u32[]{:S(2)}) copy-start(bf16[784,56]{0,1:T(8,128)(2,1)} %param.5) | copy-start | bytes 263428
  7.2 199.8 %all-gather.2.cloned.1.call-start = ((), (), s32[]{:S(2)}) async-start(), calls=%async_computation.1 | async-start | bytes 16056320 | tf_op jit(solution)/shard_map/all_gather | solution.py:19
  80.9 126.0 %copy-start.2 = (bf16[14,56,2048]{2,1,0:T(8,128)(2,1)S(1)}, bf16[14,56,2048]{2,1,0:T(8,128)(2,1)}, u32[]{:S(2)}) copy-start(bf16[14,56,2048]{2,1,0:T(8,128)(2,1)} %copy.12) | copy-start | bytes 9633796
  80.9 174.3 %all-reduce.3.cloned.1.call-start = ((), (), s32[]{:S(2)}) async-start(), calls=%async_computation.2 | async-start | bytes 917504 | tf_op jit(solution)/shard_map/psum | solution.py:28
  84.6 287.2 %reduce-scatter.4.cloned.1.call-start = ((), (), s32[]{:S(2)}) async-start(), calls=%async_computation.3 | async-start | bytes 12644352
  207.0 167.4 %copy-start.1 = (bf16[784,56]{0,1:T(8,128)(2,1)S(1)}, bf16[784,56]{0,1:T(8,128)(2,1)}, u32[]{:S(2)}) copy-start(bf16[784,56]{0,1:T(8,128)(2,1)} %param.5) | copy-start | bytes 263428
Sparse Core Ops, SparseCore 0:
  81.1 125.8 all-gather.1
  210.5 44.6 all-reduce.2
  257.7 114.0 reduce-scatter.3
where the time goes:
time: 387 us; the launch traced here: 381 us
  waiting for transfers between devices  251 us (65%)
  local copies, waits for them, and re-layouts  51.5 us (13%)
  matrix products  44 us (11%)
  between operations  14.5 us (4%)
  blocking collectives  13.2 us (3%)
  other arithmetic  6.09 us (2%)
    all_gather x1, waiting for transfers between devices, body(): gathered = lax.all_gather(own_rows, 'outer', axis=0, tiled=True)  122 us
    unnamed x4, waiting for transfers between devices  99.2 us
    unnamed x8, local copies, waits for them, and re-layouts  41.7 us
    psum x1, waiting for transfers between devices, body(): absorbed = lax.psum(local_term, 'outer')  30 us
    dot_general x1, matrix products, contract(): jnp.einsum('imc,jmc->ijc', factor, q_factor, preferred_element_type=jnp.f...  22.2 us
    dot_general x1, matrix products, body(): lax.dot_general(own_rows, gathered, (((1,), (1,)), ((), ())), preferred_e...  18.3 us
    psum x1, blocking collectives, body(): squares = lax.psum(jnp.sum(absorbed * absorbed), 'inner')  13.2 us
    convert_element_type x1, local copies, waits for them, and re-layouts, contract(): paired.reshape(factor.shape[0] * bond_size, factor.shape[2])  9.78 us
  transfers between devices with their start and end apart: 3, of which 3 were waited for; matrix products, arithmetic and copies ran while one was open for 7% of the time, Pallas kernels for 0%

commit v1 on v0

v1 whole, which is shorter than its diff:
```python
import functools
import math

import jax
import jax.numpy as jnp
from jax import lax
from jax.experimental import pallas as pl
from jax.experimental.pallas import tpu as pltpu
from jax.sharding import PartitionSpec as P

F32 = jnp.float32
BF16 = jnp.bfloat16
AXES = ("outer", "inner")
VMEM_LIMIT = 56 << 20
COLUMN_TILE = 256


def product_rows(p_ref, q_ref, rows, cols, scale, store):
    bond = q_ref.shape[0]

    def step(group, carry):
        base = pl.multiple_of(group * 8, 8)
        q_rows = [q_ref[base + u, :, cols].astype(F32) for u in range(8)]
        for half, i in rows:
            p_row = p_ref[half, i, :, cols].astype(F32)
            sums = [jnp.sum(p_row * q_row, axis=0, keepdims=True) for q_row in q_rows]
            store(half, i, base, (jnp.concatenate(sums, axis=0) * scale).astype(BF16))
        return carry

    lax.fori_loop(0, bond // 8, step, 0)


def first_kernel(lo, hi, scale, p_ref, q_ref, left_ref, right_ref):
    column = pl.program_id(0)
    bond = q_ref.shape[0]
    rows = [(h, i) for h in range(2) for i in range(lo, hi)]

    def run(out_ref):
        for c in range(0, p_ref.shape[3], 128):
            cols = slice(c, c + 128)

            def store(half, i, base, value):
                out_ref[half, pl.ds((i - lo) * bond + base, 8), cols] = value

            product_rows(p_ref, q_ref, rows, cols, scale, store)

    middle = pl.num_programs(0) // 2

    @pl.when(column < middle)
    def _():
        run(left_ref)

    @pl.when(column >= middle)
    def _():
        run(right_ref)


def contract_chunk(p4, q_factor, lo, hi):
    _, half_rows, bonds, columns = p4.shape
    bond = q_factor.shape[0]
    tile = COLUMN_TILE
    steps = columns // tile
    middle = steps // 2
    rows = (hi - lo) * bond
    scale = 1.0 / math.sqrt(bonds)
    out = jax.ShapeDtypeStruct((2, rows, columns // 2), BF16)
    return pl.pallas_call(
        functools.partial(first_kernel, lo, hi, scale),
        grid=(steps,),
        in_specs=[
            pl.BlockSpec((2, half_rows, bonds, tile), lambda c: (0, 0, 0, c)),
            pl.BlockSpec((bond, bonds, tile), lambda c: (0, 0, c)),
        ],
        out_specs=[
            pl.BlockSpec((2, rows, tile), lambda c: (0, 0, jnp.minimum(c, middle - 1))),
            pl.BlockSpec((2, rows, tile), lambda c: (0, 0, jnp.maximum(c - middle, 0))),
        ],
        out_shape=[out, out],
        compiler_params=pltpu.CompilerParams(vmem_limit_bytes=VMEM_LIMIT),
        cost_estimate=pl.CostEstimate(flops=60_000_000_000, bytes_accessed=16 << 20, transcendentals=0),
        name="contract",
    )(p4, q_factor)


def gram_kernel(core_ref, own0, own1, x0, x1, y0, y1, d0, d1, s_ref, keep_ref, send_ref):
    core = core_ref[0]
    half_cols = own0.shape[2]
    for k, (left, right) in enumerate(((own0, own1), (x0, x1), (y0, y1), (d0, d1))):
        for h in range(2):
            acc = lax.dot_general(
                left[h], s_ref[:, :half_cols], (((1,), (1,)), ((), ())), preferred_element_type=F32
            )
            acc += lax.dot_general(
                right[h], s_ref[:, half_cols:], (((1,), (1,)), ((), ())), preferred_element_type=F32
            )
            value = acc.astype(BF16)

            @pl.when(core == h)
            def _():
                keep_ref[k] = value

            @pl.when(core != h)
            def _():
                send_ref[k] = value


def gram_chunk(core, blocks, slab):
    rows = blocks[0].shape[1]
    total = slab.shape[0]
    out = jax.ShapeDtypeStruct((4, rows, total), BF16)
    vmem = pl.BlockSpec(memory_space=pltpu.VMEM)
    return pl.pallas_call(
        gram_kernel,
        in_specs=[pl.BlockSpec(memory_space=pltpu.SMEM)] + [vmem] * 9,
        out_specs=[vmem, vmem],
        out_shape=[out, out],
        compiler_params=pltpu.CompilerParams(vmem_limit_bytes=VMEM_LIMIT),
        cost_estimate=pl.CostEstimate(
            flops=2 * 8 * rows * total * slab.shape[1], bytes_accessed=12 << 20, transcendentals=0
        ),
        name="gram",
    )(core, *blocks, slab)


def merge_kernel(o_ref, keep_ref, recv_ref, out_ref):
    out_ref[...] = (keep_ref[...].astype(F32) + recv_ref[...].astype(F32)).astype(BF16)


def merge_chunk(outer_index, keep, recv):
    _, rows, total = keep.shape
    spec = pl.BlockSpec((1, rows, total), lambda d, o: (d ^ o[0], 0, 0))
    return pl.pallas_call(
        merge_kernel,
        grid_spec=pltpu.PrefetchScalarGridSpec(
            num_scalar_prefetch=1,
            grid=(4,),
            in_specs=[spec, spec],
            out_specs=pl.BlockSpec((1, rows, total), lambda d, o: (d, 0, 0)),
        ),
        out_shape=jax.ShapeDtypeStruct(keep.shape, BF16),
        name="merge",
    )(outer_index, keep, recv)


def pairs(target, keep):
    found = []
    for o in range(4):
        for z in range(4):
            for c in range(2):
                t = target(o, z, c)
                if keep(*t):
                    found.append((o * 8 + z * 2 + c, t[0] * 8 + t[1] * 2 + t[2]))
    return found


def move(value, target, keep=lambda o, z, c: True):
    return lax.ppermute(value, AXES, pairs(target, keep))


def low_rule(o, z, c):
    return (o & 1) == c


def high_rule(o, z, c):
    return (o >> 1) == c


def off_diagonal(o, z, c):
    return o != z


def to_x(o, z, c):
    return (o ^ 1, z, c)


def to_y(o, z, c):
    return (o ^ 2, z, c)


def other_core(o, z, c):
    return (o, z, 1 - c)


def paired_body(p_factor, q_factor, truncation):
    own_i, bonds, columns = p_factor.shape
    bond = q_factor.shape[0]
    half_i = own_i // 2
    half_rows = half_i * bond
    total_columns = columns * lax.axis_size("inner")
    outer = lax.axis_index("outer")
    inner = lax.axis_index("inner")
    core = inner % 2
    cut = (half_i + 1) // 2
    p4 = p_factor.reshape(2, half_i, bonds, columns)

    chunks = [contract_chunk(p4, q_factor, lo, hi) for lo, hi in ((0, cut), (cut, half_i))]
    slab = jnp.concatenate([jnp.concatenate([left, right], axis=2) for left, right in chunks], axis=1)
    slab = slab.reshape(2 * half_rows, columns)

    local_term = lax.dot_general(truncation, slab, (((0,), (0,)), ((), ())), preferred_element_type=F32)

    core_vec = core.astype(jnp.int32).reshape(1)
    outer_vec = outer.astype(jnp.int32).reshape(1)
    sums = []
    for left, right in chunks:
        x0 = move(left, to_x, low_rule)
        y1 = move(right, to_y, high_rule)
        x1 = move(right, to_x, low_rule)
        y0 = move(left, to_y, high_rule)
        d0 = move(x0, to_y, low_rule)
        d1 = move(y1, to_x, high_rule)
        keep, send = gram_chunk(core_vec, (left, right, x0, x1, y0, y1, d0, d1), slab)
        merged = merge_chunk(outer_vec, keep, move(send, other_core))
        got = lax.all_to_all(
            merged, "inner", 0, 0, axis_index_groups=[[0, 2, 4, 6], [1, 3, 5, 7]], tiled=True
        )
        sums.append(jnp.sum(got.astype(F32), axis=0))
    value = jnp.concatenate(sums, axis=0) / total_columns

    first, second = value[:, :half_rows], value[:, half_rows:]
    same = jnp.where(core == 0, first, second).astype(BF16).T
    cross = jnp.where(core == 0, second, first).astype(BF16).T
    same = move(same, lambda o, z, c: (z, o, c), off_diagonal).astype(F32)
    cross = move(cross, lambda o, z, c: (z, o, 1 - c), off_diagonal).astype(F32)
    mirror = jnp.concatenate(
        [jnp.where(core == 0, same, cross), jnp.where(core == 0, cross, same)], axis=1
    )
    gram = (value + mirror).T

    absorbed = local_term + move(local_term, to_x)
    absorbed = absorbed + move(absorbed, to_y)
    squares = lax.psum(jnp.sum(absorbed * absorbed), "inner")
    norm_scale = jnp.sqrt(squares / (absorbed.shape[0] * total_columns) + 1e-06)
    return (gram, absorbed / norm_scale)


def general_body(p_factor, q_factor, truncation):
    own_i, bonds, columns = p_factor.shape
    bond = q_factor.shape[0]
    paired = jnp.einsum("imc,jmc->ijc", p_factor, q_factor, preferred_element_type=F32)
    paired = paired / math.sqrt(bonds)
    own_rows = paired.reshape(own_i * bond, columns).astype(BF16)
    gathered = lax.all_gather(own_rows, "outer", axis=0, tiled=True)
    partial = lax.dot_general(own_rows, gathered, (((1,), (1,)), ((), ())), preferred_element_type=F32)
    total_columns = columns * lax.axis_size("inner")
    gram = lax.psum_scatter(partial, "inner", scatter_dimension=1, tiled=True) / total_columns
    local_term = lax.dot_general(truncation, own_rows, (((0,), (0,)), ((), ())), preferred_element_type=F32)
    absorbed = lax.psum(local_term, "outer")
    squares = lax.psum(jnp.sum(absorbed * absorbed), "inner")
    norm_scale = jnp.sqrt(squares / (absorbed.shape[0] * total_columns) + 1e-06)
    return (gram, absorbed / norm_scale)


def solution(mesh):
    paired = mesh.shape["outer"] == 4 and mesh.shape["inner"] == 8
    return jax.shard_map(
        paired_body if paired else general_body,
        mesh=mesh,
        in_specs=(P("outer", None, "inner"), P(None, None, "inner"), P("outer", None)),
        out_specs=(P("outer", "inner"), P(None, "inner")),
        check_vma=False,
    )
```

time: 387 us -> 257 us (0.66)
  waiting for transfers between devices: 251 us -> 86.6 us
  Pallas kernels: 0 us -> 85.7 us
  starting transfers between devices: 0.12 us -> 49.1 us
  local copies, waits for them, and re-layouts: 51.5 us -> 3.69 us
  matrix products: 44 us -> 0.75 us
  between operations: 14.5 us -> 1.65 us
    all_gather x1 -> x0, waiting for transfers between devices: 122 us -> none  [body(): gathered = lax.all_gather(own_rows, 'outer', axis=0, tiled=True)]
    unnamed x4 -> x0, waiting for transfers between devices: 99.2 us -> none
    ppermute x0 -> x18, waiting for transfers between devices: none -> 86.6 us  [move(): return lax.ppermute(value, AXES, pairs(target, keep))]
    pallas_call x0 -> x6, Pallas kernels: none -> 85.7 us  [the longest x2 45.2 us: contract_chunk(): pl.pallas_call(functools.partial(first_kernel, lo, hi, scale), grid=(step...]
    dot_general x3 -> x1, matrix products: 44 us -> 0.75 us  [paired_body(): lax.dot_general(truncation, slab, (((0,), (0,)), ((), ())), preferred_ele...]
    unnamed x8 -> x24, local copies, waits for them, and re-layouts: 41.7 us -> 3.49 us
    ppermute x0 -> x18, starting transfers between devices: none -> 38.2 us  [move(): return lax.ppermute(value, AXES, pairs(target, keep))]
    psum x1 -> x0, waiting for transfers between devices: 30 us -> none  [body(): absorbed = lax.psum(local_term, 'outer')]
  transfers between devices with their start and end apart: 3 -> 20, of which waited for: 3 -> 7; matrix products, arithmetic and copies ran while one was open for 7% -> 3% of each run, Pallas kernels for 0% -> 26%
where the time goes in v1:
time: 257 us; the launch traced here: 254 us
  waiting for transfers between devices  86.6 us (34%)
  Pallas kernels  85.7 us (33%)
  starting transfers between devices  49.1 us (19%)
  blocking collectives  16.6 us (6%)
  other arithmetic  9.78 us (4%)
  local copies, waits for them, and re-layouts  3.69 us (1%)
    ppermute x18, waiting for transfers between devices, move(): return lax.ppermute(value, AXES, pairs(target, keep))  86.6 us
    pallas_call x2, Pallas kernels, contract_chunk(): pl.pallas_call(functools.partial(first_kernel, lo, hi, scale), grid=(step...  45.2 us
    ppermute x18, starting transfers between devices, move(): return lax.ppermute(value, AXES, pairs(target, keep))  38.2 us
    pallas_call x2, Pallas kernels, gram_chunk(): pl.pallas_call(gram_kernel, in_specs=[pl.BlockSpec(memory_space=pltpu.SME...  32.7 us
    psum x1, blocking collectives, paired_body(): squares = lax.psum(jnp.sum(absorbed * absorbed), 'inner')  16.6 us
    all_to_all x2, starting transfers between devices, paired_body(): lax.all_to_all(merged, 'inner', 0, 0, axis_index_groups=[[0, 2, 4, 6], [1...  10.9 us
    pallas_call x2, Pallas kernels, merge_chunk(): pl.pallas_call(merge_kernel, grid_spec=pltpu.PrefetchScalarGridSpec(num_s...  7.75 us
  transfers between devices with their start and end apart: 20, of which 7 were waited for; matrix products, arithmetic and copies ran while one was open for 3% of the time, Pallas kernels for 26%

profile of v1, /device:TPU:8, one launch (start us, length us, event | category | flops | bytes accessed | tf_op | source)
XLA Modules:
  0.0 253.8 jit_solution(17017885640120579398)
XLA Ops:
  0.6 20.1 %contract.3 = (bf16[2,168,1024]{2,1,0:T(8,128)(2,1)}, bf16[2,168,1024]{2,1,0:T(8,128)(2,1)}) custom-call(bf16[2,7,56,2048]{3,2,1,0:T(8,128)(2,1)} %bitcast.17, bf16[56,56,2048]{2,1,0:T(8,128)(2,1)} %q_ref.3), custom_call_target="tpu_custom_call" | custom-call | flops 60000002048 | bytes 16777216 | tf_op jit(solution)/shard_map/contract/pallas_call | solution.py:67
  26.1 7.7 %collective-permute-done.7.x0 = bf16[2,168,1024]{2,1,0:T(8,128)(2,1)S(1)} collective-permute-done((bf16[2,168,1024]{2,1,0:T(8,128)(2,1)}, bf16[2,168,1024]{2,1,0:T(8,128)(2,1)S(1)}, u32[]{:S(2)}, u32[]{:S(2)}) %collective-permute-start.7) | collective-permute-done | bytes 688160 | tf_op jit(solution)/shard_map/ppermute | solution.py:157
  33.8 3.4 %collective-permute-start.11 = (bf16[2,168,1024]{2,1,0:T(8,128)(2,1)S(1)}, bf16[2,168,1024]{2,1,0:T(8,128)(2,1)}, u32[]{:S(2)}, u32[]{:S(2)}) collective-permute-start(bf16[2,168,1024]{2,1,0:T(8,128)(2,1)S(1)} %collective-permute-done.7.x0), channel_id=1, source_target_pairs={{0,16},{2,18},{4,20},{6,22},{9,25},{11,27},{13,29},{15,31},{16,0},... | collective-permute-start | bytes 2064392 | tf_op jit(solution)/shard_map/ppermute | solution.py:157
  37.2 2.6 %collective-permute-start.12 = (bf16[2,168,1024]{2,1,0:T(8,128)(2,1)S(1)}, bf16[2,168,1024]{2,1,0:T(8,128)(2,1)}, u32[]{:S(2)}, u32[]{:S(2)}) collective-permute-start(bf16[2,168,1024]{2,1,0:T(8,128)(2,1)S(1)} %collective-permute-done.10.y1), channel_id=1, source_target_pairs={{0,8},{2,10},{4,12},{6,14},{8,0},{10,2},{12,4},{14,6},{17,25},{19,... | collective-permute-start | bytes 2064392 | tf_op jit(solution)/shard_map/ppermute | solution.py:157
  39.8 25.1 %contract.2 = (bf16[2,224,1024]{2,1,0:T(8,128)(2,1)}, bf16[2,224,1024]{2,1,0:T(8,128)(2,1)}) custom-call(bf16[2,7,56,2048]{3,2,1,0:T(8,128)(2,1)} %bitcast.18, bf16[56,56,2048]{2,1,0:T(8,128)(2,1)} %q_ref.3), custom_call_target="tpu_custom_call" | custom-call | flops 60000002048 | bytes 16777216 | tf_op jit(solution)/shard_map/contract/pallas_call | solution.py:67
  67.6 3.1 %maximum_maximum_fusion = bf16[2,392,2048]{2,1,0:T(8,128)(2,1)} fusion(bf16[2,168,1024]{2,1,0:T(8,128)(2,1)S(1)} %copy-done.7, bf16[2,168,1024]{2,1,0:T(8,128)(2,1)S(1)} %copy-done.6, bf16[2,224,1024]{2,1,0:T(8,128)(2,1)} %get-tuple-element.11.own1, bf16[2,224,1024]{2,1,0:T(8,128)(2,1)} %get-tuple-element.10.own0), kind=kLoop, calls=%fused_computation | loop fusion | flops 12845056 | bytes 6422528 | tf_op jit(solution)/shard_map/concatenate | solution.py:197
  71.5 16.1 %gram.3 = (bf16[4,168,784]{2,1,0:T(8,128)(2,1)}, bf16[4,168,784]{2,1,0:T(8,128)(2,1)}) custom-call(s32[1]{0:T(128)} %bitcast.1.core_ref, bf16[2,168,1024]{2,1,0:T(8,128)(2,1)} %get-tuple-element.12.own0, bf16[2,168,1024]{2,1,0:T(8,128)(2,1)} %get-tuple-element.13.own1, bf16[2,168,1024]{2,1,0:T(8,128)(2,1)} %copy-done.8, ...), custom_call_target="tpu_custom_call" | custom-call | flops 4315938816 | bytes 12582912 | tf_op jit(solution)/shard_map/gram/pallas_call | solution.py:112
  87.7 4.1 %collective-permute-start.13 = (bf16[4,168,784]{2,1,0:T(8,128)(2,1)}, bf16[4,168,784]{2,1,0:T(8,128)(2,1)S(1)}, u32[]{:S(2)}, u32[]{:S(2)}) collective-permute-start(bf16[4,168,784]{2,1,0:T(8,128)(2,1)} %get-tuple-element.17), channel_id=1, source_target_pairs={{0,1},{1,0},{2,3},{3,2},{4,5},{5,4},{6,7},{7,6},{8,9},{9,8},{10,11... | collective-permute-start | bytes 3161096 | tf_op jit(solution)/shard_map/ppermute | solution.py:157
  94.4 5.5 %collective-permute-start.4 = (bf16[2,224,1024]{2,1,0:T(8,128)(2,1)}, bf16[2,224,1024]{2,1,0:T(8,128)(2,1)}, u32[]{:S(2)}, u32[]{:S(2)}) collective-permute-start(bf16[2,224,1024]{2,1,0:T(8,128)(2,1)} %collective-permute-done.x0), channel_id=1, source_target_pairs={{0,16},{2,18},{4,20},{6,22},{9,25},{11,27},{13,29},{15,31},{16,0},... | collective-permute-start | bytes 2752520 | tf_op jit(solution)/shard_map/ppermute | solution.py:157
  102.9 3.7 %merge.3 = bf16[4,168,784]{2,1,0:T(8,128)(2,1)} custom-call(s32[1]{0:T(128)} %bitcast.o_ref, bf16[4,168,784]{2,1,0:T(8,128)(2,1)} %get-tuple-element.16.keep_ref, bf16[4,168,784]{2,1,0:T(8,128)(2,1)} %copy-done.3), custom_call_target="tpu_custom_call" | custom-call | tf_op jit(solution)/shard_map/merge/pallas_call | solution.py:132
  106.6 5.3 %all-to-all-start.1 = ((bf16[4,168,784]{2,1,0:T(8,128)(2,1)}), bf16[4,168,784]{2,1,0:T(8,128)(2,1)}, u32[]{:S(2)}, u32[]{:S(2)}) async-start(bf16[4,168,784]{2,1,0:T(8,128)(2,1)} %merge.3), calls=%async_computation.1 | async-start | bytes 2408448 | tf_op jit(solution)/shard_map/all_to_all | solution.py:214
  111.9 7.7 %collective-permute-done.4.d0 = bf16[2,224,1024]{2,1,0:T(8,128)(2,1)} collective-permute-done((bf16[2,224,1024]{2,1,0:T(8,128)(2,1)}, bf16[2,224,1024]{2,1,0:T(8,128)(2,1)}, u32[]{:S(2)}, u32[]{:S(2)}) %collective-permute-start.4) | collective-permute-done | bytes 917536 | tf_op jit(solution)/shard_map/ppermute | solution.py:157
  119.6 16.6 %gram.2 = (bf16[4,224,784]{2,1,0:T(8,128)(2,1)}, bf16[4,224,784]{2,1,0:T(8,128)(2,1)}) custom-call(s32[1]{0:T(128)} %bitcast.1.core_ref, bf16[2,224,1024]{2,1,0:T(8,128)(2,1)} %get-tuple-element.10.own0, bf16[2,224,1024]{2,1,0:T(8,128)(2,1)} %get-tuple-element.11.own1, bf16[2,224,1024]{2,1,0:T(8,128)(2,1)} %collective-permute-done.x0, ...), custom_call_target="tpu_custom_call" | custom-call | flops 5754585088 | bytes 12582912 | tf_op jit(solution)/shard_map/gram/pallas_call | solution.py:112
  136.2 3.7 %collective-permute-done.6.recv_ref = bf16[4,224,784]{2,1,0:T(8,128)(2,1)S(1)} collective-permute-done((bf16[4,224,784]{2,1,0:T(8,128)(2,1)}, bf16[4,224,784]{2,1,0:T(8,128)(2,1)S(1)}, u32[]{:S(2)}, u32[]{:S(2)}) %collective-permute-start.6) | collective-permute-done | bytes 1404960 | tf_op jit(solution)/shard_map/ppermute | solution.py:157
  141.1 4.0 %merge.2 = bf16[4,224,784]{2,1,0:T(8,128)(2,1)} custom-call(s32[1]{0:T(128)} %bitcast.o_ref, bf16[4,224,784]{2,1,0:T(8,128)(2,1)} %get-tuple-element.14.keep_ref, bf16[4,224,784]{2,1,0:T(8,128)(2,1)} %copy-done.2), custom_call_target="tpu_custom_call" | custom-call | tf_op jit(solution)/shard_map/merge/pallas_call | solution.py:132
  145.1 5.6 %all-to-all-start = ((bf16[4,224,784]{2,1,0:T(8,128)(2,1)}), bf16[4,224,784]{2,1,0:T(8,128)(2,1)}, u32[]{:S(2)}, u32[]{:S(2)}) async-start(bf16[4,224,784]{2,1,0:T(8,128)(2,1)} %merge.2), calls=%async_computation | async-start | bytes 3211264 | tf_op jit(solution)/shard_map/all_to_all | solution.py:214
  153.5 10.5 %collective-permute-done.16 = f32[56,2048]{1,0:T(8,128)S(1)} collective-permute-done((f32[56,2048]{1,0:T(8,128)S(1)}, f32[56,2048]{1,0:T(8,128)S(1)}, u32[]{:S(2)}, u32[]{:S(2)}) %collective-permute-start.16) | collective-permute-done | bytes 458784 | tf_op jit(solution)/shard_map/ppermute | solution.py:157
  164.0 2.1 collective-permute-start.17
  166.2 9.6 %collective-permute-done.17 = f32[56,2048]{1,0:T(8,128)S(1)} collective-permute-done((f32[56,2048]{1,0:T(8,128)S(1)}, f32[56,2048]{1,0:T(8,128)S(1)}, u32[]{:S(2)}, u32[]{:S(2)}) %collective-permute-start.17) | collective-permute-done | bytes 458784 | tf_op jit(solution)/shard_map/ppermute | solution.py:157
  176.5 16.6 %psum.7 = f32[]{:T(128)} all-reduce(f32[]{:T(128)} %get-tuple-element.18), channel_id=1, replica_groups=mesh['outer'=4,'inner'=8] {'inner'}, use_global_device_ids=true, to_apply=%region_3.4 | all-reduce | flops 1 | bytes 8 | tf_op jit(solution)/shard_map/psum | solution.py:232
  197.8 2.8 %collective-permute-start.15 = (bf16[392,392]{1,0:T(8,128)(2,1)S(1)}, bf16[392,392]{1,0:T(8,128)(2,1)S(1)}, u32[]{:S(2)}, u32[]{:S(2)}) collective-permute-start(bf16[392,392]{1,0:T(8,128)(2,1)S(1)} %get-tuple-element.23), channel_id=1, source_target_pairs={{2,9},{3,8},{4,17},{5,16},{6,25},{7,24},{8,3},{9,2},{12,19},{13,18... | collective-permute-start | bytes 921992 | tf_op jit(solution)/shard_map/ppermute | solution.py:157
  200.5 3.4 %collective-permute-start.14 = (bf16[392,392]{1,0:T(8,128)(2,1)S(1)}, bf16[392,392]{1,0:T(8,128)(2,1)S(1)}, u32[]{:S(2)}, u32[]{:S(2)}) collective-permute-start(bf16[392,392]{1,0:T(8,128)(2,1)S(1)} %get-tuple-element.22), channel_id=1, source_target_pairs={{2,8},{3,9},{4,16},{5,17},{6,24},{7,25},{8,2},{9,3},{12,18},{13,19... | collective-permute-start | bytes 921992 | tf_op jit(solution)/shard_map/ppermute | solution.py:157
  204.7 39.8 %collective-permute-done.15 = bf16[392,392]{1,0:T(8,128)(2,1)S(1)} collective-permute-done((bf16[392,392]{1,0:T(8,128)(2,1)S(1)}, bf16[392,392]{1,0:T(8,128)(2,1)S(1)}, u32[]{:S(2)}, u32[]{:S(2)}) %collective-permute-start.15) | collective-permute-done | bytes 307360 | tf_op jit(solution)/shard_map/ppermute | solution.py:157
  244.5 7.7 %collective-permute-done.14 = bf16[392,392]{1,0:T(8,128)(2,1)S(1)} collective-permute-done((bf16[392,392]{1,0:T(8,128)(2,1)S(1)}, bf16[392,392]{1,0:T(8,128)(2,1)S(1)}, u32[]{:S(2)}, u32[]{:S(2)}) %collective-permute-start.14) | collective-permute-done | bytes 307360 | tf_op jit(solution)/shard_map/ppermute | solution.py:157
  (59 shorter events, 25.5 us)
Async XLA Ops:
  0.6 150.1 %copy-start = (bf16[784,56]{0,1:T(8,128)(2,1)S(1)}, bf16[784,56]{0,1:T(8,128)(2,1)}, u32[]{:S(2)}) copy-start(bf16[784,56]{0,1:T(8,128)(2,1)} %param.5) | copy-start | bytes 263428
  20.7 13.0 %collective-permute-start.7 = (bf16[2,168,1024]{2,1,0:T(8,128)(2,1)}, bf16[2,168,1024]{2,1,0:T(8,128)(2,1)S(1)}, u32[]{:S(2)}, u32[]{:S(2)}) collective-permute-start(bf16[2,168,1024]{2,1,0:T(8,128)(2,1)} %get-tuple-element.12.own0), channel_id=1, source_target_pairs={{1,9},{3,11},{5,13},{7,15},{8,0},{10,2},{12,4},{14,6},{17,25},{19,... | collective-permute-start | bytes 2064392 | tf_op jit(solution)/shard_map/ppermute | solution.py:157
  22.0 45.5 %copy-start.6 = (bf16[2,168,1024]{2,1,0:T(8,128)(2,1)S(1)}, bf16[2,168,1024]{2,1,0:T(8,128)(2,1)}, u32[]{:S(2)}) copy-start(bf16[2,168,1024]{2,1,0:T(8,128)(2,1)} %get-tuple-element.12.own0) | copy-start | bytes 2064388
  22.0 45.5 %copy-start.7 = (bf16[2,168,1024]{2,1,0:T(8,128)(2,1)S(1)}, bf16[2,168,1024]{2,1,0:T(8,128)(2,1)}, u32[]{:S(2)}) copy-start(bf16[2,168,1024]{2,1,0:T(8,128)(2,1)} %get-tuple-element.13.own1) | copy-start | bytes 2064388
  22.0 15.2 %collective-permute-start.10 = (bf16[2,168,1024]{2,1,0:T(8,128)(2,1)}, bf16[2,168,1024]{2,1,0:T(8,128)(2,1)S(1)}, u32[]{:S(2)}, u32[]{:S(2)}) collective-permute-start(bf16[2,168,1024]{2,1,0:T(8,128)(2,1)} %get-tuple-element.13.own1), channel_id=1, source_target_pairs={{1,17},{3,19},{5,21},{7,23},{9,25},{11,27},{13,29},{15,31},{16,0},... | collective-permute-start | bytes 2064392 | tf_op jit(solution)/shard_map/ppermute | solution.py:157
  23.5 42.7 %collective-permute-start.8 = (bf16[2,168,1024]{2,1,0:T(8,128)(2,1)}, bf16[2,168,1024]{2,1,0:T(8,128)(2,1)}, u32[]{:S(2)}, u32[]{:S(2)}) collective-permute-start(bf16[2,168,1024]{2,1,0:T(8,128)(2,1)} %get-tuple-element.13.own1), channel_id=1, source_target_pairs={{1,9},{3,11},{5,13},{7,15},{8,0},{10,2},{12,4},{14,6},{17,25},{19,... | collective-permute-start | bytes 2064392 | tf_op jit(solution)/shard_map/ppermute | solution.py:157
  24.8 45.9 %collective-permute-start.9 = (bf16[2,168,1024]{2,1,0:T(8,128)(2,1)}, bf16[2,168,1024]{2,1,0:T(8,128)(2,1)S(1)}, u32[]{:S(2)}, u32[]{:S(2)}) collective-permute-start(bf16[2,168,1024]{2,1,0:T(8,128)(2,1)} %get-tuple-element.12.own0), channel_id=1, source_target_pairs={{1,17},{3,19},{5,21},{7,23},{9,25},{11,27},{13,29},{15,31},{16,0},... | collective-permute-start | bytes 2064392 | tf_op jit(solution)/shard_map/ppermute | solution.py:157
  33.8 31.1 %copy-start.8 = (bf16[2,168,1024]{2,1,0:T(8,128)(2,1)}, bf16[2,168,1024]{2,1,0:T(8,128)(2,1)S(1)}, u32[]{:S(2)}) copy-start(bf16[2,168,1024]{2,1,0:T(8,128)(2,1)S(1)} %collective-permute-done.7.x0) | copy-start | bytes 2064388
  33.8 36.9 %collective-permute-start.11 = (bf16[2,168,1024]{2,1,0:T(8,128)(2,1)S(1)}, bf16[2,168,1024]{2,1,0:T(8,128)(2,1)}, u32[]{:S(2)}, u32[]{:S(2)}) collective-permute-start(bf16[2,168,1024]{2,1,0:T(8,128)(2,1)S(1)} %collective-permute-done.7.x0), channel_id=1, source_target_pairs={{0,16},{2,18},{4,20},{6,22},{9,25},{11,27},{13,29},{15,31},{16,0},... | collective-permute-start | bytes 2064392 | tf_op jit(solution)/shard_map/ppermute | solution.py:157
  37.2 33.5 %collective-permute-start.12 = (bf16[2,168,1024]{2,1,0:T(8,128)(2,1)S(1)}, bf16[2,168,1024]{2,1,0:T(8,128)(2,1)}, u32[]{:S(2)}, u32[]{:S(2)}) collective-permute-start(bf16[2,168,1024]{2,1,0:T(8,128)(2,1)S(1)} %collective-permute-done.10.y1), channel_id=1, source_target_pairs={{0,8},{2,10},{4,12},{6,14},{8,0},{10,2},{12,4},{14,6},{17,25},{19,... | collective-permute-start | bytes 2064392 | tf_op jit(solution)/shard_map/ppermute | solution.py:157
  64.9 29.4 %collective-permute-start = (bf16[2,224,1024]{2,1,0:T(8,128)(2,1)}, bf16[2,224,1024]{2,1,0:T(8,128)(2,1)}, u32[]{:S(2)}, u32[]{:S(2)}) collective-permute-start(bf16[2,224,1024]{2,1,0:T(8,128)(2,1)} %get-tuple-element.10.own0), channel_id=1, source_target_pairs={{1,9},{3,11},{5,13},{7,15},{8,0},{10,2},{12,4},{14,6},{17,25},{19,... | collective-permute-start | bytes 2752520 | tf_op jit(solution)/shard_map/ppermute | solution.py:157
  66.2 33.6 %collective-permute-start.3 = (bf16[2,224,1024]{2,1,0:T(8,128)(2,1)}, bf16[2,224,1024]{2,1,0:T(8,128)(2,1)}, u32[]{:S(2)}, u32[]{:S(2)}) collective-permute-start(bf16[2,224,1024]{2,1,0:T(8,128)(2,1)} %get-tuple-element.11.own1), channel_id=1, source_target_pairs={{1,17},{3,19},{5,21},{7,23},{9,25},{11,27},{13,29},{15,31},{16,0},... | collective-permute-start | bytes 2752520 | tf_op jit(solution)/shard_map/ppermute | solution.py:157
  87.7 14.1 %collective-permute-start.13 = (bf16[4,168,784]{2,1,0:T(8,128)(2,1)}, bf16[4,168,784]{2,1,0:T(8,128)(2,1)S(1)}, u32[]{:S(2)}, u32[]{:S(2)}) collective-permute-start(bf16[4,168,784]{2,1,0:T(8,128)(2,1)} %get-tuple-element.17), channel_id=1, source_target_pairs={{0,1},{1,0},{2,3},{3,2},{4,5},{5,4},{6,7},{7,6},{8,9},{9,8},{10,11... | collective-permute-start | bytes 3161096 | tf_op jit(solution)/shard_map/ppermute | solution.py:157
  91.8 20.2 %collective-permute-start.1 = (bf16[2,224,1024]{2,1,0:T(8,128)(2,1)S(1)}, bf16[2,224,1024]{2,1,0:T(8,128)(2,1)}, u32[]{:S(2)}, u32[]{:S(2)}) collective-permute-start(bf16[2,224,1024]{2,1,0:T(8,128)(2,1)S(1)} %copy-done.5), channel_id=1, source_target_pairs={{1,9},{3,11},{5,13},{7,15},{8,0},{10,2},{12,4},{14,6},{17,25},{19,... | collective-permute-start | bytes 2752520 | tf_op jit(solution)/shard_map/ppermute | solution.py:157
  93.1 18.9 %collective-permute-start.2 = (bf16[2,224,1024]{2,1,0:T(8,128)(2,1)S(1)}, bf16[2,224,1024]{2,1,0:T(8,128)(2,1)}, u32[]{:S(2)}, u32[]{:S(2)}) collective-permute-start(bf16[2,224,1024]{2,1,0:T(8,128)(2,1)S(1)} %copy-done.4), channel_id=1, source_target_pairs={{1,17},{3,19},{5,21},{7,23},{9,25},{11,27},{13,29},{15,31},{16,0},... | collective-permute-start | bytes 2752520 | tf_op jit(solution)/shard_map/ppermute | solution.py:157
  94.4 25.3 %collective-permute-start.4 = (bf16[2,224,1024]{2,1,0:T(8,128)(2,1)}, bf16[2,224,1024]{2,1,0:T(8,128)(2,1)}, u32[]{:S(2)}, u32[]{:S(2)}) collective-permute-start(bf16[2,224,1024]{2,1,0:T(8,128)(2,1)} %collective-permute-done.x0), channel_id=1, source_target_pairs={{0,16},{2,18},{4,20},{6,22},{9,25},{11,27},{13,29},{15,31},{16,0},... | collective-permute-start | bytes 2752520 | tf_op jit(solution)/shard_map/ppermute | solution.py:157
  99.8 19.8 %collective-permute-start.5 = (bf16[2,224,1024]{2,1,0:T(8,128)(2,1)}, bf16[2,224,1024]{2,1,0:T(8,128)(2,1)}, u32[]{:S(2)}, u32[]{:S(2)}) collective-permute-start(bf16[2,224,1024]{2,1,0:T(8,128)(2,1)} %collective-permute-done.3.y1), channel_id=1, source_target_pairs={{0,8},{2,10},{4,12},{6,14},{8,0},{10,2},{12,4},{14,6},{17,25},{19,... | collective-permute-start | bytes 2752520 | tf_op jit(solution)/shard_map/ppermute | solution.py:157
  106.6 38.5 %all-to-all-start.1 = ((bf16[4,168,784]{2,1,0:T(8,128)(2,1)}), bf16[4,168,784]{2,1,0:T(8,128)(2,1)}, u32[]{:S(2)}, u32[]{:S(2)}) async-start(bf16[4,168,784]{2,1,0:T(8,128)(2,1)} %merge.3), calls=%async_computation.1 | async-start | bytes 2408448 | tf_op jit(solution)/shard_map/all_to_all | solution.py:214
  136.2 3.7 %collective-permute-start.6 = (bf16[4,224,784]{2,1,0:T(8,128)(2,1)}, bf16[4,224,784]{2,1,0:T(8,128)(2,1)S(1)}, u32[]{:S(2)}, u32[]{:S(2)}) collective-permute-start(bf16[4,224,784]{2,1,0:T(8,128)(2,1)} %get-tuple-element.15), channel_id=1, source_target_pairs={{0,1},{1,0},{2,3},{3,2},{4,5},{5,4},{6,7},{7,6},{8,9},{9,8},{10,11... | collective-permute-start | bytes 4214792 | tf_op jit(solution)/shard_map/ppermute | solution.py:157
  145.1 50.2 %all-to-all-start = ((bf16[4,224,784]{2,1,0:T(8,128)(2,1)}), bf16[4,224,784]{2,1,0:T(8,128)(2,1)}, u32[]{:S(2)}, u32[]{:S(2)}) async-start(bf16[4,224,784]{2,1,0:T(8,128)(2,1)} %merge.2), calls=%async_computation | async-start | bytes 3211264 | tf_op jit(solution)/shard_map/all_to_all | solution.py:214
  151.5 12.5 %collective-permute-start.16 = (f32[56,2048]{1,0:T(8,128)S(1)}, f32[56,2048]{1,0:T(8,128)S(1)}, u32[]{:S(2)}, u32[]{:S(2)}) collective-permute-start(f32[56,2048]{1,0:T(8,128)S(1)} %convolution_bitcast_fusion), channel_id=1, source_target_pairs={{0,8},{1,9},{2,10},{3,11},{4,12},{5,13},{6,14},{7,15},{8,0},{9,1},... | collective-permute-start | bytes 1376264 | tf_op jit(solution)/shard_map/ppermute | solution.py:157
  164.0 11.7 %collective-permute-start.17 = (f32[56,2048]{1,0:T(8,128)S(1)}, f32[56,2048]{1,0:T(8,128)S(1)}, u32[]{:S(2)}, u32[]{:S(2)}) collective-permute-start(f32[56,2048]{1,0:T(8,128)S(1)} %add.20), channel_id=1, source_target_pairs={{0,16},{1,17},{2,18},{3,19},{4,20},{5,21},{6,22},{7,23},{8,24},{9,... | collective-permute-start | bytes 1376264 | tf_op jit(solution)/shard_map/ppermute | solution.py:157
  197.8 46.7 %collective-permute-start.15 = (bf16[392,392]{1,0:T(8,128)(2,1)S(1)}, bf16[392,392]{1,0:T(8,128)(2,1)S(1)}, u32[]{:S(2)}, u32[]{:S(2)}) collective-permute-start(bf16[392,392]{1,0:T(8,128)(2,1)S(1)} %get-tuple-element.23), channel_id=1, source_target_pairs={{2,9},{3,8},{4,17},{5,16},{6,25},{7,24},{8,3},{9,2},{12,19},{13,18... | collective-permute-start | bytes 921992 | tf_op jit(solution)/shard_map/ppermute | solution.py:157
  200.5 51.6 %collective-permute-start.14 = (bf16[392,392]{1,0:T(8,128)(2,1)S(1)}, bf16[392,392]{1,0:T(8,128)(2,1)S(1)}, u32[]{:S(2)}, u32[]{:S(2)}) collective-permute-start(bf16[392,392]{1,0:T(8,128)(2,1)S(1)} %get-tuple-element.22), channel_id=1, source_target_pairs={{2,8},{3,9},{4,16},{5,17},{6,24},{7,25},{8,2},{9,3},{12,18},{13,19... | collective-permute-start | bytes 921992 | tf_op jit(solution)/shard_map/ppermute | solution.py:157
  (7 other events, 78.2 us)

commit v2 on v1

v2 whole, which is shorter than its diff:
```python
import functools
import math

import jax
import jax.numpy as jnp
from jax import lax
from jax.experimental import pallas as pl
from jax.experimental.pallas import tpu as pltpu
from jax.sharding import PartitionSpec as P

F32 = jnp.float32
BF16 = jnp.bfloat16
AXES = ("outer", "inner")
COLUMN_TILE = 256
CUTS = (0, 2, 5, 7)


def product_rows(p_ref, q_ref, rows, cols, scale, store):
    bond = q_ref.shape[0]

    def step(group, carry):
        base = pl.multiple_of(group * 8, 8)
        q_rows = [q_ref[base + u, :, cols].astype(F32) for u in range(8)]
        for half, i in rows:
            p_row = p_ref[half, i, :, cols].astype(F32)
            sums = [jnp.sum(p_row * q_row, axis=0, keepdims=True) for q_row in q_rows]
            store(half, i, base, (jnp.concatenate(sums, axis=0) * scale).astype(BF16))
        return carry

    lax.fori_loop(0, bond // 8, step, 0)


def head_kernel(hi, scale, p_ref, q_ref, out_ref):
    bond = q_ref.shape[0]
    rows = [(h, i) for h in range(2) for i in range(hi)]
    for c in range(0, p_ref.shape[3], 128):
        cols = slice(c, c + 128)

        def store(half, i, base, value):
            out_ref[half, pl.ds(i * bond + base, 8), cols] = value

        product_rows(p_ref, q_ref, rows, cols, scale, store)


def tail_kernel(cuts, scale, p_ref, q_ref, head_ref, slab_ref, *out_refs):
    bond = q_ref.shape[0]
    rows = [(h, i) for h in range(2) for i in range(cuts[0], cuts[-1])]
    slab_ref[:, : cuts[0] * bond, :] = head_ref[...]
    for c in range(0, p_ref.shape[3], 128):
        cols = slice(c, c + 128)

        def store(half, i, base, value):
            slab_ref[half, pl.ds(i * bond + base, 8), cols] = value
            for part, out_ref in enumerate(out_refs):
                if cuts[part] <= i < cuts[part + 1]:
                    out_ref[half, pl.ds((i - cuts[part]) * bond + base, 8), cols] = value

        product_rows(p_ref, q_ref, rows, cols, scale, store)


def factor_specs(p4, q_factor):
    tile = COLUMN_TILE
    _, half_i, bonds, _ = p4.shape
    return [
        pl.BlockSpec((2, half_i, bonds, tile), lambda c: (0, 0, 0, c)),
        pl.BlockSpec((q_factor.shape[0], bonds, tile), lambda c: (0, 0, c)),
    ]


def row_spec(rows):
    return pl.BlockSpec((2, rows, COLUMN_TILE), lambda c: (0, 0, c))


def product_cost(p4, q_factor, share):
    flops = 1400 * share * p4.size * q_factor.shape[0]
    return pl.CostEstimate(flops=int(flops), bytes_accessed=2 * (p4.size + q_factor.size), transcendentals=0)


def contract(p4, q_factor, cuts):
    _, half_i, bonds, columns = p4.shape
    bond = q_factor.shape[0]
    scale = 1.0 / math.sqrt(bonds)
    params = pltpu.CompilerParams(vmem_limit_bytes=52 << 20)
    head_rows = cuts[1] * bond
    head = pl.pallas_call(
        functools.partial(head_kernel, cuts[1], scale),
        grid=(columns // COLUMN_TILE,),
        in_specs=factor_specs(p4, q_factor),
        out_specs=row_spec(head_rows),
        out_shape=jax.ShapeDtypeStruct((2, head_rows, columns), BF16),
        compiler_params=params,
        cost_estimate=product_cost(p4, q_factor, cuts[1] / half_i),
        name="contract_head",
    )(p4, q_factor)
    sizes = [half_i * bond] + [(b - a) * bond for a, b in zip(cuts[1:-1], cuts[2:])]
    slab, *rest = pl.pallas_call(
        functools.partial(tail_kernel, cuts[1:], scale),
        grid=(columns // COLUMN_TILE,),
        in_specs=factor_specs(p4, q_factor) + [row_spec(head_rows)],
        out_specs=[row_spec(s) for s in sizes],
        out_shape=[jax.ShapeDtypeStruct((2, s, columns), BF16) for s in sizes],
        compiler_params=params,
        cost_estimate=product_cost(p4, q_factor, 1 - cuts[1] / half_i),
        name="contract_tail",
    )(p4, q_factor, head)
    return slab, [head, *rest]


def gram_kernel(row0, core_ref, x_ref, y_ref, d_ref, s_ref, t_ref, *refs):
    keep_ref, send_ref, sum_ref = refs[-3:]
    core = core_ref[0]
    rows = x_ref.shape[1]
    half_rows = s_ref.shape[0] // 2
    total = jnp.zeros(sum_ref.shape, F32) if len(refs) == 3 else refs[0][...]
    for k, block in enumerate((None, x_ref, y_ref, d_ref)):
        for h in range(2):
            if block is None:
                left = s_ref[h * half_rows + row0 : h * half_rows + row0 + rows, :]
            else:
                left = block[h]
            value = lax.dot_general(
                left, s_ref[...], (((1,), (1,)), ((), ())), preferred_element_type=F32
            ).astype(BF16)
            total = total + jnp.dot(t_ref[k, h], left, preferred_element_type=F32)

            @pl.when(core == h)
            def _():
                keep_ref[k] = value

            @pl.when(core != h)
            def _():
                send_ref[k] = value

    sum_ref[...] = total


def gram_chunk(core, row0, blocks, slab, maps, running):
    rows = blocks[0].shape[1]
    total, columns = slab.shape
    out = jax.ShapeDtypeStruct((4, rows, total), BF16)
    vmem = pl.BlockSpec(memory_space=pltpu.VMEM)
    args = (*blocks, slab, maps) + (() if running is None else (running,))
    return pl.pallas_call(
        functools.partial(gram_kernel, row0),
        in_specs=[pl.BlockSpec(memory_space=pltpu.SMEM)] + [vmem] * len(args),
        out_specs=[vmem] * 3,
        out_shape=[out, out, jax.ShapeDtypeStruct((maps.shape[2], columns), F32)],
        compiler_params=pltpu.CompilerParams(vmem_limit_bytes=40 << 20),
        cost_estimate=pl.CostEstimate(
            flops=2 * 8 * 2 * rows * total * columns, bytes_accessed=12 << 20, transcendentals=0
        ),
        name="gram",
    )(core, *args)


def merge_kernel(o_ref, keep_ref, recv_ref, out_ref):
    out_ref[...] = (keep_ref[...].astype(F32) + recv_ref[...].astype(F32)).astype(BF16)


def merge_chunk(outer_index, keep, recv):
    _, rows, total = keep.shape
    spec = pl.BlockSpec((1, rows, total), lambda d, o: (d ^ o[0], 0, 0))
    return pl.pallas_call(
        merge_kernel,
        grid_spec=pltpu.PrefetchScalarGridSpec(
            num_scalar_prefetch=1,
            grid=(4,),
            in_specs=[spec, spec],
            out_specs=pl.BlockSpec((1, rows, total), lambda d, o: (d, 0, 0)),
        ),
        out_shape=jax.ShapeDtypeStruct(keep.shape, BF16),
        name="merge",
    )(outer_index, keep, recv)


def pairs(target):
    found = []
    for o in range(4):
        for z in range(4):
            for c in range(2):
                t = target(o, z, c)
                found.append((o * 8 + z * 2 + c, t[0] * 8 + t[1] * 2 + t[2]))
    return found


def move(value, target):
    return lax.ppermute(value, AXES, pairs(target))


def to_x(o, z, c):
    return (o ^ 1, z, c)


def to_y(o, z, c):
    return (o ^ 2, z, c)


def other_core(o, z, c):
    return (o, z, 1 - c)


def paired_body(p_factor, q_factor, truncation):
    own_i, bonds, columns = p_factor.shape
    bond = q_factor.shape[0]
    half_i = own_i // 2
    half_rows = half_i * bond
    total_columns = columns * lax.axis_size("inner")
    outer = lax.axis_index("outer")
    core = lax.axis_index("inner") % 2
    core_vec = core.astype(jnp.int32).reshape(1)
    outer_vec = outer.astype(jnp.int32).reshape(1)
    p4 = p_factor.reshape(2, half_i, bonds, columns)

    maps = lax.all_gather(truncation, "outer", axis=0, tiled=False)
    maps = jnp.stack([maps[outer ^ k] for k in range(4)])
    maps = maps.reshape(4, 2, half_rows, truncation.shape[1]).swapaxes(2, 3)

    slab, chunks = contract(p4, q_factor, CUTS)
    slab = slab.reshape(2 * half_rows, columns)

    sums = []
    absorbed = None
    for t, own in enumerate(chunks):
        row0, row1 = CUTS[t] * bond, CUTS[t + 1] * bond
        x = move(own, to_x)
        y = move(own, to_y)
        d = move(x, to_y) if t % 2 == 0 else move(y, to_x)
        keep, send, absorbed = gram_chunk(
            core_vec, row0, (x, y, d), slab, maps[:, :, :, row0:row1], absorbed
        )
        merged = merge_chunk(outer_vec, keep, move(send, other_core))
        got = lax.all_to_all(
            merged, "inner", 0, 0, axis_index_groups=[[0, 2, 4, 6], [1, 3, 5, 7]], tiled=True
        )
        sums.append(jnp.sum(got.astype(F32), axis=0))
    gram = (jnp.concatenate(sums, axis=0) / total_columns).T

    squares = lax.psum(jnp.sum(absorbed * absorbed), "inner")
    norm_scale = jnp.sqrt(squares / (absorbed.shape[0] * total_columns) + 1e-06)
    return (gram, absorbed / norm_scale)


def general_body(p_factor, q_factor, truncation):
    own_i, bonds, columns = p_factor.shape
    bond = q_factor.shape[0]
    paired = jnp.einsum("imc,jmc->ijc", p_factor, q_factor, preferred_element_type=F32)
    paired = paired / math.sqrt(bonds)
    own_rows = paired.reshape(own_i * bond, columns).astype(BF16)
    gathered = lax.all_gather(own_rows, "outer", axis=0, tiled=True)
    partial = lax.dot_general(own_rows, gathered, (((1,), (1,)), ((), ())), preferred_element_type=F32)
    total_columns = columns * lax.axis_size("inner")
    gram = lax.psum_scatter(partial, "inner", scatter_dimension=1, tiled=True) / total_columns
    local_term = lax.dot_general(truncation, own_rows, (((0,), (0,)), ((), ())), preferred_element_type=F32)
    absorbed = lax.psum(local_term, "outer")
    squares = lax.psum(jnp.sum(absorbed * absorbed), "inner")
    norm_scale = jnp.sqrt(squares / (absorbed.shape[0] * total_columns) + 1e-06)
    return (gram, absorbed / norm_scale)


def solution(mesh):
    paired = mesh.shape["outer"] == 4 and mesh.shape["inner"] == 8
    return jax.shard_map(
        paired_body if paired else general_body,
        mesh=mesh,
        in_specs=(P("outer", None, "inner"), P(None, None, "inner"), P("outer", None)),
        out_specs=(P("outer", "inner"), P(None, "inner")),
        check_vma=False,
    )
```

time: 257 us -> 275 us (1.070)
  blocking collectives: 16.6 us -> 103 us
  waiting for transfers between devices: 86.6 us -> 28.3 us
  starting transfers between devices: 49.1 us -> 27.6 us
  Pallas kernels: 85.7 us -> 95.6 us
  local copies, waits for them, and re-layouts: 3.69 us -> 13.1 us
  other arithmetic: 9.78 us -> 4.35 us
    ppermute x18 -> x12, waiting for transfers between devices: 86.6 us -> 15.5 us  [move(): return lax.ppermute(value, AXES, pairs(target))]
    all_gather x0 -> x1, blocking collectives: none -> 70.8 us  [paired_body(): maps = lax.all_gather(truncation, 'outer', axis=0, tiled=False)]
    ppermute x18 -> x12, starting transfers between devices: 38.2 us -> 10.2 us  [move(): return lax.ppermute(value, AXES, pairs(target))]
    psum x1, blocking collectives: 16.6 us -> 32 us  [paired_body(): squares = lax.psum(jnp.sum(absorbed * absorbed), 'inner')]
    all_to_all x2 -> x3, waiting for transfers between devices: 0.01 us -> 12.7 us  [paired_body(): lax.all_to_all(merged, 'inner', 0, 0, axis_index_groups=[[0, 2, 4, 6], [1...]
    unnamed x24 -> x22, local copies, waits for them, and re-layouts: 3.49 us -> 10.6 us
    pallas_call x4 -> x5, Pallas kernels: 77.9 us -> 84.8 us  [the longest x3 40.1 us: gram_chunk(): pl.pallas_call(functools.partial(gram_kernel, row0), in_specs=[pl.BlockSp...]
    all_to_all x2 -> x3, starting transfers between devices: 10.9 us -> 17.4 us  [paired_body(): lax.all_to_all(merged, 'inner', 0, 0, axis_index_groups=[[0, 2, 4, 6], [1...]
  transfers between devices with their start and end apart: 20 -> 15, of which waited for: 7 -> 5; matrix products, arithmetic and copies ran while one was open for 3% -> 2% of each run, Pallas kernels for 26% -> 30%
where the time goes in v2:
time: 275 us; the launch traced here: 273 us
  blocking collectives  103 us (37%)
  Pallas kernels  95.6 us (35%)
  waiting for transfers between devices  28.3 us (10%)
  starting transfers between devices  27.6 us (10%)
  local copies, waits for them, and re-layouts  13.1 us (5%)
  other arithmetic  4.35 us (2%)
    all_gather x1, blocking collectives, paired_body(): maps = lax.all_gather(truncation, 'outer', axis=0, tiled=False)  70.8 us
    pallas_call x3, Pallas kernels, gram_chunk(): pl.pallas_call(functools.partial(gram_kernel, row0), in_specs=[pl.BlockSp...  40.1 us
    psum x1, blocking collectives, paired_body(): squares = lax.psum(jnp.sum(absorbed * absorbed), 'inner')  32 us
    pallas_call x1, Pallas kernels, contract(): pl.pallas_call(functools.partial(tail_kernel, cuts[1:], scale), grid=(col...  30 us
    all_to_all x3, starting transfers between devices, paired_body(): lax.all_to_all(merged, 'inner', 0, 0, axis_index_groups=[[0, 2, 4, 6], [1...  17.4 us
    ppermute x12, waiting for transfers between devices, move(): return lax.ppermute(value, AXES, pairs(target))  15.5 us
    pallas_call x1, Pallas kernels, contract(): pl.pallas_call(functools.partial(head_kernel, cuts[1], scale), grid=(colu...  14.7 us
    all_to_all x3, waiting for transfers between devices, paired_body(): lax.all_to_all(merged, 'inner', 0, 0, axis_index_groups=[[0, 2, 4, 6], [1...  12.7 us
  transfers between devices with their start and end apart: 15, of which 5 were waited for; matrix products, arithmetic and copies ran while one was open for 2% of the time, Pallas kernels for 30%

profile of v2, /device:TPU:8, one launch (start us, length us, event | category | flops | bytes accessed | tf_op | source)
XLA Modules:
  0.0 273.2 jit_solution(5868044647138485304)
XLA Ops:
  0.6 14.7 %contract_head.1.head_ref = bf16[2,112,2048]{2,1,0:T(8,128)(2,1)} custom-call(bf16[2,7,56,2048]{3,2,1,0:T(8,128)(2,1)} %bitcast.18, bf16[56,56,2048]{2,1,0:T(8,128)(2,1)} %q_ref.3), custom_call_target="tpu_custom_call" | custom-call | flops 35966156800 | bytes 16056320 | tf_op jit(solution)/shard_map/contract_head/pallas_call | solution.py:85
  15.3 1.5 collective-permute-start
  16.8 30.0 %contract_tail.1 = (bf16[2,392,2048]{2,1,0:T(8,128)(2,1)}, bf16[2,168,2048]{2,1,0:T(8,128)(2,1)}, bf16[2,112,2048]{2,1,0:T(8,128)(2,1)}) custom-call(bf16[2,7,56,2048]{3,2,1,0:T(8,128)(2,1)} %bitcast.19, bf16[56,56,2048]{2,1,0:T(8,128)(2,1)} %q_ref.3, bf16[2,112,2048]{2,1,0:T(8,128)(2,1)} %contract_head.1.head_ref), custom_call_target="tpu_custom_call" | custom-call | flops 89915392000 | bytes 16056320 | tf_op jit(solution)/shard_map/contract_tail/pallas_call | solution.py:96
  46.8 1.5 collective-permute-start.5
  48.9 1.5 collective-permute-start.2
  50.9 1.5 collective-permute-start.8
  52.4 70.8 %all-gather.1 = bf16[4,784,56]{1,2,0:T(8,128)(2,1)S(1)} all-gather(bf16[1,784,56]{1,2,0:T(8,128)(2,1)S(1)} %bitcast.17), channel_id=2, replica_groups=mesh['outer'=4,'inner'=8] {'outer'}, dimensions={0}, use_global_device_ids=true | all-gather | bytes 439040 | tf_op jit(solution)/shard_map/all_gather | solution.py:214
  126.4 1.9 copy-done.3
  128.3 12.9 %gram.3 = (bf16[4,112,784]{2,1,0:T(8,128)(2,1)S(1)}, bf16[4,112,784]{2,1,0:T(8,128)(2,1)S(1)}, f32[56,2048]{1,0:T(8,128)S(1)}) custom-call(s32[1]{0:T(128)} %bitcast.1.core_ref, bf16[2,112,2048]{2,1,0:T(8,128)(2,1)} %collective-permute-done.x_ref, bf16[2,112,2048]{2,1,0:T(8,128)(2,1)} %collective-permute-done.1.y_ref, ...), custom_call_target="tpu_custom_call" | custom-call | flops 5754585088 | bytes 12582912 | tf_op jit(solution)/shard_map/gram/pallas_call | solution.py:143
  142.2 1.5 collective-permute-start.9
  145.4 3.5 %merge.3 = bf16[4,112,784]{2,1,0:T(8,128)(2,1)} custom-call(s32[1]{0:T(128)} %bitcast.o_ref, bf16[4,112,784]{2,1,0:T(8,128)(2,1)} %copy-done.1, bf16[4,112,784]{2,1,0:T(8,128)(2,1)} %copy-done.8), custom_call_target="tpu_custom_call" | custom-call | tf_op jit(solution)/shard_map/merge/pallas_call | solution.py:163
  149.0 5.3 %all-to-all-start = ((bf16[4,112,784]{2,1,0:T(8,128)(2,1)}), bf16[4,112,784]{2,1,0:T(8,128)(2,1)}, u32[]{:S(2)}, u32[]{:S(2)}) async-start(bf16[4,112,784]{2,1,0:T(8,128)(2,1)} %merge.3), calls=%async_computation | async-start | bytes 1605632 | tf_op jit(solution)/shard_map/all_to_all | solution.py:232
  154.3 1.8 collective-permute-done.6.d_ref
  156.1 1.9 copy-done.4
  159.0 14.2 %gram.4 = (bf16[4,168,784]{2,1,0:T(8,128)(2,1)S(1)}, bf16[4,168,784]{2,1,0:T(8,128)(2,1)}, f32[56,2048]{1,0:T(8,128)S(1)}) custom-call(s32[1]{0:T(128)} %bitcast.1.core_ref, bf16[2,168,2048]{2,1,0:T(8,128)(2,1)S(1)} %collective-permute-done.4.x_ref, bf16[2,168,2048]{2,1,0:T(8,128)(2,1)S(1)} %collective-permute-done.5.y_ref, ...), custom_call_target="tpu_custom_call" | custom-call | flops 8631877632 | bytes 12582912 | tf_op jit(solution)/shard_map/gram/pallas_call | solution.py:143
  174.3 10.7 %collective-permute-done.10.d_ref = bf16[2,112,2048]{2,1,0:T(8,128)(2,1)} collective-permute-done((bf16[2,112,2048]{2,1,0:T(8,128)(2,1)}, bf16[2,112,2048]{2,1,0:T(8,128)(2,1)}, u32[]{:S(2)}, u32[]{:S(2)}) %collective-permute-start.10) | collective-permute-done | bytes 917536 | tf_op jit(solution)/shard_map/ppermute | solution.py:187
  184.9 13.0 %gram.5 = (bf16[4,112,784]{2,1,0:T(8,128)(2,1)S(1)}, bf16[4,112,784]{2,1,0:T(8,128)(2,1)S(1)}, f32[56,2048]{1,0:T(8,128)S(1)}) custom-call(s32[1]{0:T(128)} %bitcast.1.core_ref, bf16[2,112,2048]{2,1,0:T(8,128)(2,1)} %collective-permute-done.8.x_ref, bf16[2,112,2048]{2,1,0:T(8,128)(2,1)} %collective-permute-done.9.y_ref, ...), custom_call_target="tpu_custom_call" | custom-call | flops 5754585088 | bytes 12582912 | tf_op jit(solution)/shard_map/gram/pallas_call | solution.py:143
  199.3 2.9 %collective-permute-done.11.recv_ref = bf16[4,112,784]{2,1,0:T(8,128)(2,1)S(1)} collective-permute-done((bf16[4,112,784]{2,1,0:T(8,128)(2,1)S(1)}, bf16[4,112,784]{2,1,0:T(8,128)(2,1)S(1)}, u32[]{:S(2)}, u32[]{:S(2)}) %collective-permute-start.11) | collective-permute-done | bytes 702496 | tf_op jit(solution)/shard_map/ppermute | solution.py:187
  203.1 3.5 %merge.5 = bf16[4,112,784]{2,1,0:T(8,128)(2,1)} custom-call(s32[1]{0:T(128)} %bitcast.o_ref, bf16[4,112,784]{2,1,0:T(8,128)(2,1)} %copy-done.2, bf16[4,112,784]{2,1,0:T(8,128)(2,1)} %copy-done.9), custom_call_target="tpu_custom_call" | custom-call | tf_op jit(solution)/shard_map/merge/pallas_call | solution.py:163
  206.7 5.3 %all-to-all-start.2 = ((bf16[4,112,784]{2,1,0:T(8,128)(2,1)}), bf16[4,112,784]{2,1,0:T(8,128)(2,1)S(1)}, u32[]{:S(2)}, u32[]{:S(2)}) async-start(bf16[4,112,784]{2,1,0:T(8,128)(2,1)} %merge.5), calls=%async_computation.2 | async-start | bytes 1605632 | tf_op jit(solution)/shard_map/all_to_all | solution.py:232
  213.0 3.7 %merge.4 = bf16[4,168,784]{2,1,0:T(8,128)(2,1)} custom-call(s32[1]{0:T(128)} %bitcast.o_ref, bf16[4,168,784]{2,1,0:T(8,128)(2,1)} %copy-done, bf16[4,168,784]{2,1,0:T(8,128)(2,1)} %copy-done.7), custom_call_target="tpu_custom_call" | custom-call | tf_op jit(solution)/shard_map/merge/pallas_call | solution.py:163
  216.7 12.7 %all-to-all-done.2 = bf16[4,112,784]{2,1,0:T(8,128)(2,1)S(1)} async-done(((bf16[4,112,784]{2,1,0:T(8,128)(2,1)}), bf16[4,112,784]{2,1,0:T(8,128)(2,1)S(1)}, u32[]{:S(2)}, u32[]{:S(2)}) %all-to-all-start.2) | async-done | bytes 702496 | tf_op jit(solution)/shard_map/all_to_all | solution.py:232
  229.5 6.8 %all-to-all-start.1 = ((bf16[4,168,784]{2,1,0:T(8,128)(2,1)}), bf16[4,168,784]{2,1,0:T(8,128)(2,1)S(1)}, u32[]{:S(2)}, u32[]{:S(2)}) async-start(bf16[4,168,784]{2,1,0:T(8,128)(2,1)} %merge.4), calls=%async_computation.1 | async-start | bytes 2408448 | tf_op jit(solution)/shard_map/all_to_all | solution.py:232
  237.0 32.0 %psum.7 = f32[]{:T(128)} all-reduce(f32[]{:T(128)} %multiply_reduce_fusion), channel_id=1, replica_groups=mesh['outer'=4,'inner'=8] {'inner'}, use_global_device_ids=true, to_apply=%region_4.5 | all-reduce | flops 1 | bytes 8 | tf_op jit(solution)/shard_map/psum | solution.py:238
  (50 shorter events, 16.5 us)
Async XLA Ops:
  15.3 37.1 %copy-start.10 = (bf16[784,56]{0,1:T(8,128)(2,1)S(1)}, bf16[784,56]{0,1:T(8,128)(2,1)}, u32[]{:S(2)}) copy-start(bf16[784,56]{0,1:T(8,128)(2,1)} %param.5) | copy-start | bytes 263428
  15.3 33.6 %collective-permute-start = (bf16[2,112,2048]{2,1,0:T(8,128)(2,1)}, bf16[2,112,2048]{2,1,0:T(8,128)(2,1)}, u32[]{:S(2)}, u32[]{:S(2)}) collective-permute-start(bf16[2,112,2048]{2,1,0:T(8,128)(2,1)} %contract_head.1.head_ref), channel_id=1, source_target_pairs={{0,8},{1,9},{2,10},{3,11},{4,12},{5,13},{6,14},{7,15},{8,0},{9,1},... | collective-permute-start | bytes 2752520 | tf_op jit(solution)/shard_map/ppermute | solution.py:187
  46.8 78.8 %collective-permute-start.5 = (bf16[2,168,2048]{2,1,0:T(8,128)(2,1)}, bf16[2,168,2048]{2,1,0:T(8,128)(2,1)S(1)}, u32[]{:S(2)}, u32[]{:S(2)}) collective-permute-start(bf16[2,168,2048]{2,1,0:T(8,128)(2,1)} %get-tuple-element.17), channel_id=1, source_target_pairs={{0,16},{1,17},{2,18},{3,19},{4,20},{5,21},{6,22},{7,23},{8,24},{9,... | collective-permute-start | bytes 4128776 | tf_op jit(solution)/shard_map/ppermute | solution.py:187
  48.3 78.0 %collective-permute-start.1 = (bf16[2,112,2048]{2,1,0:T(8,128)(2,1)}, bf16[2,112,2048]{2,1,0:T(8,128)(2,1)}, u32[]{:S(2)}, u32[]{:S(2)}) collective-permute-start(bf16[2,112,2048]{2,1,0:T(8,128)(2,1)} %contract_head.1.head_ref), channel_id=1, source_target_pairs={{0,16},{1,17},{2,18},{3,19},{4,20},{5,21},{6,22},{7,23},{8,24},{9,... | collective-permute-start | bytes 2752520 | tf_op jit(solution)/shard_map/ppermute | solution.py:187
  48.9 77.5 %collective-permute-start.2 = (bf16[2,112,2048]{2,1,0:T(8,128)(2,1)}, bf16[2,112,2048]{2,1,0:T(8,128)(2,1)}, u32[]{:S(2)}, u32[]{:S(2)}) collective-permute-start(bf16[2,112,2048]{2,1,0:T(8,128)(2,1)} %collective-permute-done.x_ref), channel_id=1, source_target_pairs={{0,16},{1,17},{2,18},{3,19},{4,20},{5,21},{6,22},{7,23},{8,24},{9,... | collective-permute-start | bytes 2752520 | tf_op jit(solution)/shard_map/ppermute | solution.py:187
  50.4 103.9 %collective-permute-start.4 = (bf16[2,168,2048]{2,1,0:T(8,128)(2,1)}, bf16[2,168,2048]{2,1,0:T(8,128)(2,1)S(1)}, u32[]{:S(2)}, u32[]{:S(2)}) collective-permute-start(bf16[2,168,2048]{2,1,0:T(8,128)(2,1)} %get-tuple-element.17), channel_id=1, source_target_pairs={{0,8},{1,9},{2,10},{3,11},{4,12},{5,13},{6,14},{7,15},{8,0},{9,1},... | collective-permute-start | bytes 4128776 | tf_op jit(solution)/shard_map/ppermute | solution.py:187
  50.9 92.8 %collective-permute-start.8 = (bf16[2,112,2048]{2,1,0:T(8,128)(2,1)}, bf16[2,112,2048]{2,1,0:T(8,128)(2,1)}, u32[]{:S(2)}, u32[]{:S(2)}) collective-permute-start(bf16[2,112,2048]{2,1,0:T(8,128)(2,1)} %get-tuple-element.21), channel_id=1, source_target_pairs={{0,8},{1,9},{2,10},{3,11},{4,12},{5,13},{6,14},{7,15},{8,0},{9,1},... | collective-permute-start | bytes 2752520 | tf_op jit(solution)/shard_map/ppermute | solution.py:187
  125.7 30.4 %collective-permute-start.6 = (bf16[2,168,2048]{2,1,0:T(8,128)(2,1)S(1)}, bf16[2,168,2048]{2,1,0:T(8,128)(2,1)}, u32[]{:S(2)}, u32[]{:S(2)}) collective-permute-start(bf16[2,168,2048]{2,1,0:T(8,128)(2,1)S(1)} %collective-permute-done.5.y_ref), channel_id=1, source_target_pairs={{0,8},{1,9},{2,10},{3,11},{4,12},{5,13},{6,14},{7,15},{8,0},{9,1},... | collective-permute-start | bytes 4128776 | tf_op jit(solution)/shard_map/ppermute | solution.py:187
  126.4 1.9 copy-start.3
  141.2 1.0 copy-start.1
  142.2 2.3 copy-start.5
  142.2 2.3 collective-permute-start.3
  142.2 32.1 %collective-permute-start.9 = (bf16[2,112,2048]{2,1,0:T(8,128)(2,1)}, bf16[2,112,2048]{2,1,0:T(8,128)(2,1)}, u32[]{:S(2)}, u32[]{:S(2)}) collective-permute-start(bf16[2,112,2048]{2,1,0:T(8,128)(2,1)} %get-tuple-element.21), channel_id=1, source_target_pairs={{0,16},{1,17},{2,18},{3,19},{4,20},{5,21},{6,22},{7,23},{8,24},{9,... | collective-permute-start | bytes 2752520 | tf_op jit(solution)/shard_map/ppermute | solution.py:187
  143.7 41.2 %collective-permute-start.10 = (bf16[2,112,2048]{2,1,0:T(8,128)(2,1)}, bf16[2,112,2048]{2,1,0:T(8,128)(2,1)}, u32[]{:S(2)}, u32[]{:S(2)}) collective-permute-start(bf16[2,112,2048]{2,1,0:T(8,128)(2,1)} %collective-permute-done.8.x_ref), channel_id=1, source_target_pairs={{0,16},{1,17},{2,18},{3,19},{4,20},{5,21},{6,22},{7,23},{8,24},{9,... | collective-permute-start | bytes 2752520 | tf_op jit(solution)/shard_map/ppermute | solution.py:187
  144.5 0.9 copy-start.8
  149.0 57.7 %all-to-all-start = ((bf16[4,112,784]{2,1,0:T(8,128)(2,1)}), bf16[4,112,784]{2,1,0:T(8,128)(2,1)}, u32[]{:S(2)}, u32[]{:S(2)}) async-start(bf16[4,112,784]{2,1,0:T(8,128)(2,1)} %merge.3), calls=%async_computation | async-start | bytes 1605632 | tf_op jit(solution)/shard_map/all_to_all | solution.py:232
  156.1 1.9 copy-start.4
  158.0 1.0 copy-start.6
  173.2 1.0 copy-start
  198.8 3.4 %collective-permute-start.11 = (bf16[4,112,784]{2,1,0:T(8,128)(2,1)S(1)}, bf16[4,112,784]{2,1,0:T(8,128)(2,1)S(1)}, u32[]{:S(2)}, u32[]{:S(2)}) collective-permute-start(bf16[4,112,784]{2,1,0:T(8,128)(2,1)S(1)} %get-tuple-element.24), channel_id=1, source_target_pairs={{0,1},{1,0},{2,3},{3,2},{4,5},{5,4},{6,7},{7,6},{8,9},{9,8},{10,11... | collective-permute-start | bytes 2107400 | tf_op jit(solution)/shard_map/ppermute | solution.py:187
  198.8 13.2 %collective-permute-start.7 = (bf16[4,168,784]{2,1,0:T(8,128)(2,1)}, bf16[4,168,784]{2,1,0:T(8,128)(2,1)S(1)}, u32[]{:S(2)}, u32[]{:S(2)}) collective-permute-start(bf16[4,168,784]{2,1,0:T(8,128)(2,1)} %get-tuple-element.20), channel_id=1, source_target_pairs={{0,1},{1,0},{2,3},{3,2},{4,5},{5,4},{6,7},{7,6},{8,9},{9,8},{10,11... | collective-permute-start | bytes 3161096 | tf_op jit(solution)/shard_map/ppermute | solution.py:187
  206.7 22.8 %all-to-all-start.2 = ((bf16[4,112,784]{2,1,0:T(8,128)(2,1)}), bf16[4,112,784]{2,1,0:T(8,128)(2,1)S(1)}, u32[]{:S(2)}, u32[]{:S(2)}) async-start(bf16[4,112,784]{2,1,0:T(8,128)(2,1)} %merge.5), calls=%async_computation.2 | async-start | bytes 1605632 | tf_op jit(solution)/shard_map/all_to_all | solution.py:232
  212.0 1.0 copy-start.7
  229.5 42.4 %all-to-all-start.1 = ((bf16[4,168,784]{2,1,0:T(8,128)(2,1)}), bf16[4,168,784]{2,1,0:T(8,128)(2,1)S(1)}, u32[]{:S(2)}, u32[]{:S(2)}) async-start(bf16[4,168,784]{2,1,0:T(8,128)(2,1)} %merge.4), calls=%async_computation.1 | async-start | bytes 2408448 | tf_op jit(solution)/shard_map/all_to_all | solution.py:232
  (2 other events, 1.8 us)

commit v3 on v2

v3 whole, which is shorter than its diff:
```python
import functools
import math

import jax
import jax.numpy as jnp
from jax import lax
from jax.experimental import pallas as pl
from jax.experimental.pallas import tpu as pltpu
from jax.sharding import PartitionSpec as P

F32 = jnp.float32
BF16 = jnp.bfloat16
AXES = ("outer", "inner")
COLUMN_TILE = 256
CUTS = (0, 2, 5, 7)


def product_rows(p_ref, q_ref, rows, cols, scale, store):
    bond = q_ref.shape[0]

    def step(group, carry):
        base = pl.multiple_of(group * 8, 8)
        q_rows = [q_ref[base + u, :, cols].astype(F32) for u in range(8)]
        for half, i in rows:
            p_row = p_ref[half, i, :, cols].astype(F32)
            sums = [jnp.sum(p_row * q_row, axis=0, keepdims=True) for q_row in q_rows]
            store(half, i, base, (jnp.concatenate(sums, axis=0) * scale).astype(BF16))
        return carry

    lax.fori_loop(0, bond // 8, step, 0)


def chunk_kernel(lo, hi, scale, p_ref, q_ref, out_ref):
    bond = q_ref.shape[0]
    rows = [(h, i) for h in range(2) for i in range(lo, hi)]
    for c in range(0, p_ref.shape[3], 128):
        cols = slice(c, c + 128)

        def store(half, i, base, value):
            out_ref[half, pl.ds((i - lo) * bond + base, 8), cols] = value

        product_rows(p_ref, q_ref, rows, cols, scale, store)


def last_kernel(cuts, scale, p_ref, q_ref, *refs):
    bond = q_ref.shape[0]
    earlier, (out_ref, slab_ref) = refs[:-2], refs[-2:]
    lo, hi = cuts[-2:]
    rows = [(h, i) for h in range(2) for i in range(lo, hi)]
    for part, ref in enumerate(earlier):
        slab_ref[:, cuts[part] * bond : cuts[part + 1] * bond, :] = ref[...]
    for c in range(0, p_ref.shape[3], 128):
        cols = slice(c, c + 128)

        def store(half, i, base, value):
            out_ref[half, pl.ds((i - lo) * bond + base, 8), cols] = value
            slab_ref[half, pl.ds(i * bond + base, 8), cols] = value

        product_rows(p_ref, q_ref, rows, cols, scale, store)


def contract(p4, q_factor, cuts):
    _, half_i, bonds, columns = p4.shape
    bond = q_factor.shape[0]
    scale = 1.0 / math.sqrt(bonds)
    tile = COLUMN_TILE

    def row_spec(rows):
        return pl.BlockSpec((2, rows, tile), lambda c: (0, 0, c))

    def row_shape(rows):
        return jax.ShapeDtypeStruct((2, rows, columns), BF16)

    factor_specs = [
        pl.BlockSpec((2, half_i, bonds, tile), lambda c: (0, 0, 0, c)),
        pl.BlockSpec((bond, bonds, tile), lambda c: (0, 0, c)),
    ]
    chunks = []
    for lo, hi in zip(cuts, cuts[1:]):
        last = hi == cuts[-1]
        rows = (hi - lo) * bond
        flops = 1400 * 2 * (hi - lo) * bonds * columns * bond
        earlier = chunks if last else []
        found = pl.pallas_call(
            functools.partial(last_kernel, cuts, scale) if last else functools.partial(chunk_kernel, lo, hi, scale),
            grid=(columns // tile,),
            in_specs=factor_specs + [row_spec(e.shape[1]) for e in earlier],
            out_specs=[row_spec(rows)] + ([row_spec(half_i * bond)] if last else []),
            out_shape=[row_shape(rows)] + ([row_shape(half_i * bond)] if last else []),
            compiler_params=pltpu.CompilerParams(vmem_limit_bytes=52 << 20),
            cost_estimate=pl.CostEstimate(flops=30_000_000_000, bytes_accessed=1000, transcendentals=0),
            name="contract",
        )(p4, q_factor, *earlier)
        own = found[0]
        if not last:
            q_factor, own = lax.optimization_barrier((q_factor, own))
        chunks.append(own)
    return found[1], chunks


def gram_kernel(core_ref, own_ref, x_ref, y_ref, d_ref, s_ref, t_ref, *refs):
    keep_ref, send_ref, sum_ref = refs[-3:]
    core = core_ref[0]
    rows = x_ref.shape[1]
    terms = []
    for k, block in enumerate((own_ref, x_ref, y_ref, d_ref)):
        left = block[...].reshape(2 * rows, block.shape[2])
        value = lax.dot_general(
            left, s_ref[...], (((1,), (1,)), ((), ())), preferred_element_type=F32
        ).astype(BF16)
        terms.append(jnp.dot(t_ref[k], left, preferred_element_type=F32))

        @pl.when(core == 0)
        def _():
            keep_ref[k] = value[:rows]
            send_ref[k] = value[rows:]

        @pl.when(core != 0)
        def _():
            keep_ref[k] = value[rows:]
            send_ref[k] = value[:rows]

    total = (terms[0] + terms[1]) + (terms[2] + terms[3])
    sum_ref[...] = total if len(refs) == 3 else refs[0][...] + total


def gram_chunk(core, blocks, slab, maps, running):
    rows = blocks[0].shape[1]
    total, columns = slab.shape
    out = jax.ShapeDtypeStruct((4, rows, total), BF16)
    vmem = pl.BlockSpec(memory_space=pltpu.VMEM)
    args = (*blocks, slab, maps) + (() if running is None else (running,))
    return pl.pallas_call(
        gram_kernel,
        in_specs=[pl.BlockSpec(memory_space=pltpu.SMEM)] + [vmem] * len(args),
        out_specs=[vmem] * 3,
        out_shape=[out, out, jax.ShapeDtypeStruct((maps.shape[1], columns), F32)],
        compiler_params=pltpu.CompilerParams(vmem_limit_bytes=40 << 20),
        cost_estimate=pl.CostEstimate(
            flops=1000, bytes_accessed=1000, transcendentals=0
        ),
        name="gram",
    )(core, *args)


def merge_kernel(o_ref, keep_ref, recv_ref, out_ref):
    o = o_ref[0]
    for d in range(4):
        k = d ^ o
        out_ref[d] = (keep_ref[k].astype(F32) + recv_ref[k].astype(F32)).astype(BF16)


def merge_chunk(outer_index, keep, recv):
    vmem = pl.BlockSpec(memory_space=pltpu.VMEM)
    return pl.pallas_call(
        merge_kernel,
        in_specs=[pl.BlockSpec(memory_space=pltpu.SMEM), vmem, vmem],
        out_specs=vmem,
        out_shape=jax.ShapeDtypeStruct(keep.shape, BF16),
        cost_estimate=pl.CostEstimate(flops=1000, bytes_accessed=1000, transcendentals=0),
        name="merge",
    )(outer_index, keep, recv)


def pairs(target):
    found = []
    for o in range(4):
        for z in range(4):
            for c in range(2):
                t = target(o, z, c)
                found.append((o * 8 + z * 2 + c, t[0] * 8 + t[1] * 2 + t[2]))
    return found


def move(value, target):
    return lax.ppermute(value, AXES, pairs(target))


def to_x(o, z, c):
    return (o ^ 1, z, c)


def to_y(o, z, c):
    return (o ^ 2, z, c)


def to_diagonal(o, z, c):
    return (o ^ 3, z, c)


def to_z1(o, z, c):
    return (o, z ^ 1, c)


def to_z2(o, z, c):
    return (o, z ^ 2, c)


def other_core(o, z, c):
    return (o, z, 1 - c)


def paired_body(p_factor, q_factor, truncation):
    own_i, bonds, columns = p_factor.shape
    bond = q_factor.shape[0]
    half_i = own_i // 2
    half_rows = half_i * bond
    total_columns = columns * lax.axis_size("inner")
    outer = lax.axis_index("outer")
    core = lax.axis_index("inner") % 2
    core_vec = core.astype(jnp.int32).reshape(1)
    outer_vec = outer.astype(jnp.int32).reshape(1)
    p4 = p_factor.reshape(2, half_i, bonds, columns)

    maps = [truncation] + [move(truncation, to) for to in (to_x, to_y, to_diagonal)]
    maps = jnp.stack(maps).reshape(4, 2, half_rows, truncation.shape[1])
    slab, chunks = contract(p4, q_factor, CUTS)
    slab = slab.reshape(2 * half_rows, columns)

    moved = []
    for t, own in enumerate(chunks):
        x = move(own, to_x)
        y = move(own, to_y)
        d = move(x, to_y) if t % 2 == 0 else move(y, to_x)
        moved.append([x, y, d])

    sums = []
    absorbed = None
    merged = None
    for t, own in enumerate(chunks):
        row0, row1 = CUTS[t] * bond, CUTS[t + 1] * bond
        if merged is not None:
            moved[t][2], merged = lax.optimization_barrier((moved[t][2], merged))
            sums.append(merged)
        if t + 1 < len(chunks):
            moved[t][2], moved[t + 1][0], moved[t + 1][1] = lax.optimization_barrier(
                (moved[t][2], moved[t + 1][0], moved[t + 1][1])
            )
        part = maps[:, :, row0:row1].reshape(4, 2 * (row1 - row0), -1).swapaxes(1, 2)
        keep, send, absorbed = gram_chunk(core_vec, (own, *moved[t]), slab, part, absorbed)
        merged = merge_chunk(outer_vec, keep, move(send, other_core))
    sums.append(merged)
    sums = [
        lax.all_to_all(m, "inner", 0, 0, axis_index_groups=[[0, 2, 4, 6], [1, 3, 5, 7]], tiled=True)
        for m in sums
    ]
    sums = [jnp.sum(m.astype(F32), axis=0) for m in sums]
    gram = (jnp.concatenate(sums, axis=0) / total_columns).T

    squares = jnp.full((8, 128), jnp.sum(absorbed * absorbed))
    for to in (other_core, to_z1, to_z2):
        squares = squares + move(squares, to)
    norm_scale = jnp.sqrt(squares[:1, :1] / (absorbed.shape[0] * total_columns) + 1e-06)
    return (gram, absorbed / norm_scale)


def general_body(p_factor, q_factor, truncation):
    own_i, bonds, columns = p_factor.shape
    bond = q_factor.shape[0]
    paired = jnp.einsum("imc,jmc->ijc", p_factor, q_factor, preferred_element_type=F32)
    paired = paired / math.sqrt(bonds)
    own_rows = paired.reshape(own_i * bond, columns).astype(BF16)
    gathered = lax.all_gather(own_rows, "outer", axis=0, tiled=True)
    partial = lax.dot_general(own_rows, gathered, (((1,), (1,)), ((), ())), preferred_element_type=F32)
    total_columns = columns * lax.axis_size("inner")
    gram = lax.psum_scatter(partial, "inner", scatter_dimension=1, tiled=True) / total_columns
    local_term = lax.dot_general(truncation, own_rows, (((0,), (0,)), ((), ())), preferred_element_type=F32)
    absorbed = lax.psum(local_term, "outer")
    squares = lax.psum(jnp.sum(absorbed * absorbed), "inner")
    norm_scale = jnp.sqrt(squares / (absorbed.shape[0] * total_columns) + 1e-06)
    return (gram, absorbed / norm_scale)


def solution(mesh):
    paired = mesh.shape["outer"] == 4 and mesh.shape["inner"] == 8
    return jax.shard_map(
        paired_body if paired else general_body,
        mesh=mesh,
        in_specs=(P("outer", None, "inner"), P(None, None, "inner"), P("outer", None)),
        out_specs=(P("outer", "inner"), P(None, "inner")),
        check_vma=False,
    )
```

time: 275 us -> 228 us (0.83)
  blocking collectives: 103 us -> 0 us
  waiting for transfers between devices: 28.3 us -> 74.1 us
  Pallas kernels: 95.6 us -> 83.7 us
  local copies, waits for them, and re-layouts: 13.1 us -> 23.4 us
  starting transfers between devices: 27.6 us -> 34.5 us
    all_gather x1 -> x0, blocking collectives: 70.8 us -> none  [paired_body(): maps = lax.all_gather(truncation, 'outer', axis=0, tiled=False)]
    ppermute x12 -> x18, waiting for transfers between devices: 15.5 us -> 65.8 us  [move(): return lax.ppermute(value, AXES, pairs(target))]
    psum x1 -> x0, blocking collectives: 32 us -> none  [paired_body(): squares = lax.psum(jnp.sum(absorbed * absorbed), 'inner')]
    pallas_call x8 -> x9, Pallas kernels: 95.6 us -> 83.7 us  [the longest x3 49.4 us: contract(): pl.pallas_call(functools.partial(last_kernel, cuts, scale) if last else f...]
    ppermute x12 -> x18, starting transfers between devices: 10.2 us -> 17.3 us  [move(): return lax.ppermute(value, AXES, pairs(target))]
    unnamed x22 -> x47, local copies, waits for them, and re-layouts: 10.6 us -> 15.2 us
    all_to_all x3, waiting for transfers between devices: 12.7 us -> 8.26 us  [paired_body(): lax.all_to_all(m, 'inner', 0, 0, axis_index_groups=[[0, 2, 4, 6], [1, 3,...]
    another operation x0 -> x5, local copies, waits for them, and re-layouts: none -> 3.39 us  [paired_body(): maps = jnp.stack(maps).reshape(4, 2, half_rows, truncation.shape[1])]
  transfers between devices with their start and end apart: 15 -> 21, of which waited for: 5 -> 8; matrix products, arithmetic and copies ran while one was open for 2% -> 6% of each run, Pallas kernels for 30% -> 33%
where the time goes in v3:
time: 228 us; the launch traced here: 224 us
  Pallas kernels  83.7 us (37%)
  waiting for transfers between devices  74.1 us (32%)
  starting transfers between devices  34.5 us (15%)
  local copies, waits for them, and re-layouts  23.4 us (10%)
  other arithmetic  6.76 us (3%)
    ppermute x18, waiting for transfers between devices, move(): return lax.ppermute(value, AXES, pairs(target))  65.8 us
    pallas_call x3, Pallas kernels, contract(): pl.pallas_call(functools.partial(last_kernel, cuts, scale) if last else f...  49.4 us
    pallas_call x3, Pallas kernels, gram_chunk(): pl.pallas_call(gram_kernel, in_specs=[pl.BlockSpec(memory_space=pltpu.SME...  26.4 us
    ppermute x18, starting transfers between devices, move(): return lax.ppermute(value, AXES, pairs(target))  17.3 us
    all_to_all x3, starting transfers between devices, paired_body(): lax.all_to_all(m, 'inner', 0, 0, axis_index_groups=[[0, 2, 4, 6], [1, 3,...  17.3 us
    unnamed x47, local copies, waits for them, and re-layouts  15.2 us
    all_to_all x3, waiting for transfers between devices, paired_body(): lax.all_to_all(m, 'inner', 0, 0, axis_index_groups=[[0, 2, 4, 6], [1, 3,...  8.26 us
    pallas_call x3, Pallas kernels, merge_chunk(): pl.pallas_call(merge_kernel, in_specs=[pl.BlockSpec(memory_space=pltpu.SM...  7.87 us
  transfers between devices with their start and end apart: 21, of which 8 were waited for; matrix products, arithmetic and copies ran while one was open for 6% of the time, Pallas kernels for 33%

profile of v3, /device:TPU:8, one launch (start us, length us, event | category | flops | bytes accessed | tf_op | source)
XLA Modules:
  0.0 224.1 jit_solution(7335125439399300656)
XLA Ops:
  3.7 14.7 %contract.3.refs_0_.own_ref = bf16[2,112,2048]{2,1,0:T(8,128)(2,1)} custom-call(bf16[2,7,56,2048]{3,2,1,0:T(8,128)(2,1)} %bitcast.30, bf16[56,56,2048]{2,1,0:T(8,128)(2,1)} %q_ref.3), custom_call_target="tpu_custom_call" | custom-call | flops 30000001024 | bytes 1000 | tf_op jit(solution)/shard_map/contract/pallas_call | solution.py:84
  20.4 19.2 %contract.4.refs_1_.own_ref = bf16[2,168,2048]{2,1,0:T(8,128)(2,1)S(1)} custom-call(bf16[2,7,56,2048]{3,2,1,0:T(8,128)(2,1)} %bitcast.31, bf16[56,56,2048]{2,1,0:T(8,128)(2,1)} %q_ref.3), custom_call_target="tpu_custom_call" | custom-call | flops 30000001024 | bytes 1000 | tf_op jit(solution)/shard_map/contract/pallas_call | solution.py:84
  42.2 15.5 %contract.5 = (bf16[2,112,2048]{2,1,0:T(8,128)(2,1)S(1)}, bf16[2,392,2048]{2,1,0:T(8,128)(2,1)}) custom-call(bf16[2,7,56,2048]{3,2,1,0:T(8,128)(2,1)} %bitcast.32, bf16[56,56,2048]{2,1,0:T(8,128)(2,1)} %q_ref.3, bf16[2,112,2048]{2,1,0:T(8,128)(2,1)} %contract.3.refs_0_.own_ref, bf16[2,168,2048]{2,1,0:T(8,128)(2,1)} %copy-done.4), custom_call_target="tpu_custom_call" | custom-call | flops 30000001024 | bytes 1000 | tf_op jit(solution)/shard_map/contract/pallas_call | solution.py:84
  58.9 1.6 collective-permute-start.7
  60.5 12.9 %collective-permute-done.y_ref = bf16[2,168,2048]{2,1,0:T(8,128)(2,1)} collective-permute-done((bf16[2,168,2048]{2,1,0:T(8,128)(2,1)S(1)}, bf16[2,168,2048]{2,1,0:T(8,128)(2,1)}, u32[]{:S(2)}, u32[]{:S(2)}) %collective-permute-start) | collective-permute-done | bytes 1376288 | tf_op jit(solution)/shard_map/ppermute | solution.py:176
  77.1 15.5 %collective-permute-done.7 = bf16[784,56]{0,1:T(8,128)(2,1)} collective-permute-done((bf16[784,56]{0,1:T(8,128)(2,1)S(1)}, bf16[784,56]{0,1:T(8,128)(2,1)}, u32[]{:S(2)}, u32[]{:S(2)}) %collective-permute-start.7) | collective-permute-done | bytes 87840 | tf_op jit(solution)/shard_map/ppermute | solution.py:176
  95.5 1.6 collective-permute-start.10
  97.4 1.9 copy-done
  99.3 8.5 %gram.3 = (bf16[4,112,784]{2,1,0:T(8,128)(2,1)S(1)}, bf16[4,112,784]{2,1,0:T(8,128)(2,1)}, f32[56,2048]{1,0:T(8,128)S(1)}) custom-call(s32[1]{0:T(128)} %bitcast.2.core_ref, bf16[2,112,2048]{2,1,0:T(8,128)(2,1)} %contract.3.refs_0_.own_ref, bf16[2,112,2048]{2,1,0:T(8,128)(2,1)} %collective-permute-done.2.x_ref, ...), custom_call_target="tpu_custom_call" | custom-call | flops 1000 | bytes 1000 | tf_op jit(solution)/shard_map/gram/pallas_call | solution.py:133
  109.5 2.2 slice.17
  112.8 2.5 %merge.3 = bf16[4,112,784]{2,1,0:T(8,128)(2,1)} custom-call(s32[1]{0:T(128)} %bitcast.1.o_ref, bf16[4,112,784]{2,1,0:T(8,128)(2,1)} %copy-done.11, bf16[4,112,784]{2,1,0:T(8,128)(2,1)} %collective-permute-done.9.recv_ref), custom_call_target="tpu_custom_call" | custom-call | flops 1000 | bytes 1000 | tf_op jit(solution)/shard_map/merge/pallas_call | solution.py:155
  115.3 5.1 %collective-permute-done.10.x_ref = bf16[2,112,2048]{2,1,0:T(8,128)(2,1)} collective-permute-done((bf16[2,112,2048]{2,1,0:T(8,128)(2,1)}, bf16[2,112,2048]{2,1,0:T(8,128)(2,1)}, u32[]{:S(2)}, u32[]{:S(2)}) %collective-permute-start.10) | collective-permute-done | bytes 917536 | tf_op jit(solution)/shard_map/ppermute | solution.py:176
  124.1 10.1 %gram.4 = (bf16[4,168,784]{2,1,0:T(8,128)(2,1)S(1)}, bf16[4,168,784]{2,1,0:T(8,128)(2,1)}, f32[56,2048]{1,0:T(8,128)S(1)}) custom-call(s32[1]{0:T(128)} %bitcast.2.core_ref, bf16[2,168,2048]{2,1,0:T(8,128)(2,1)S(1)} %copy-done.5, bf16[2,168,2048]{2,1,0:T(8,128)(2,1)S(1)} %copy-done.7, bf16[2,168,2048]{2,1,0:T(8,128)(2,1)} %collective-permute-done.y_ref, ...), custom_call_target="tpu_custom_call" | custom-call | flops 1000 | bytes 1000 | tf_op jit(solution)/shard_map/gram/pallas_call | solution.py:133
  135.9 5.3 %all-to-all-start = ((bf16[4,112,784]{2,1,0:T(8,128)(2,1)}), bf16[4,112,784]{2,1,0:T(8,128)(2,1)}, u32[]{:S(2)}, u32[]{:S(2)}) async-start(bf16[4,112,784]{2,1,0:T(8,128)(2,1)} %merge.3), calls=%async_computation | async-start | bytes 1605632 | tf_op jit(solution)/shard_map/all_to_all | solution.py:244
  142.8 3.0 %merge.4 = bf16[4,168,784]{2,1,0:T(8,128)(2,1)} custom-call(s32[1]{0:T(128)} %bitcast.1.o_ref, bf16[4,168,784]{2,1,0:T(8,128)(2,1)} %copy-done.8, bf16[4,168,784]{2,1,0:T(8,128)(2,1)} %collective-permute-done.13.recv_ref), custom_call_target="tpu_custom_call" | custom-call | flops 1000 | bytes 1000 | tf_op jit(solution)/shard_map/merge/pallas_call | solution.py:155
  145.7 18.0 %collective-permute-done.11.d_ref = bf16[2,112,2048]{2,1,0:T(8,128)(2,1)} collective-permute-done((bf16[2,112,2048]{2,1,0:T(8,128)(2,1)}, bf16[2,112,2048]{2,1,0:T(8,128)(2,1)}, u32[]{:S(2)}, u32[]{:S(2)}) %collective-permute-start.11) | collective-permute-done | bytes 917536 | tf_op jit(solution)/shard_map/ppermute | solution.py:176
  163.8 5.1 %all-to-all-start.1 = ((bf16[4,168,784]{2,1,0:T(8,128)(2,1)}), bf16[4,168,784]{2,1,0:T(8,128)(2,1)}, u32[]{:S(2)}, u32[]{:S(2)}) async-start(bf16[4,168,784]{2,1,0:T(8,128)(2,1)} %merge.4), calls=%async_computation.1 | async-start | bytes 2408448 | tf_op jit(solution)/shard_map/all_to_all | solution.py:244
  171.2 7.9 %gram.5 = (bf16[4,112,784]{2,1,0:T(8,128)(2,1)S(1)}, bf16[4,112,784]{2,1,0:T(8,128)(2,1)S(1)}, f32[56,2048]{1,0:T(8,128)S(1)}) custom-call(s32[1]{0:T(128)} %bitcast.2.core_ref, bf16[2,112,2048]{2,1,0:T(8,128)(2,1)S(1)} %copy-done.10, bf16[2,112,2048]{2,1,0:T(8,128)(2,1)} %collective-permute-done.10.x_ref, ...), custom_call_target="tpu_custom_call" | custom-call | flops 1000 | bytes 1000 | tf_op jit(solution)/shard_map/gram/pallas_call | solution.py:133
  183.2 2.5 %merge.5 = bf16[4,112,784]{2,1,0:T(8,128)(2,1)} custom-call(s32[1]{0:T(128)} %bitcast.1.o_ref, bf16[4,112,784]{2,1,0:T(8,128)(2,1)} %copy-done.12, bf16[4,112,784]{2,1,0:T(8,128)(2,1)} %copy-done.17), custom_call_target="tpu_custom_call" | custom-call | flops 1000 | bytes 1000 | tf_op jit(solution)/shard_map/merge/pallas_call | solution.py:155
  185.7 8.3 %all-to-all-done.1 = bf16[4,168,784]{2,1,0:T(8,128)(2,1)} async-done(((bf16[4,168,784]{2,1,0:T(8,128)(2,1)}), bf16[4,168,784]{2,1,0:T(8,128)(2,1)}, u32[]{:S(2)}, u32[]{:S(2)}) %all-to-all-start.1) | async-done | bytes 1053728 | tf_op jit(solution)/shard_map/all_to_all | solution.py:244
  193.9 6.8 %all-to-all-start.2 = ((bf16[4,112,784]{2,1,0:T(8,128)(2,1)}), bf16[4,112,784]{2,1,0:T(8,128)(2,1)S(1)}, u32[]{:S(2)}, u32[]{:S(2)}) async-start(bf16[4,112,784]{2,1,0:T(8,128)(2,1)} %merge.5), calls=%async_computation.2 | async-start | bytes 1605632 | tf_op jit(solution)/shard_map/all_to_all | solution.py:244
  201.5 12.5 %collective-permute-done.16 = f32[8,128]{1,0:T(8,128)S(1)} collective-permute-done((f32[8,128]{1,0:T(8,128)S(1)}, f32[8,128]{1,0:T(8,128)S(1)}, u32[]{:S(2)}, u32[]{:S(2)}) %collective-permute-start.16) | collective-permute-done | bytes 4128 | tf_op jit(solution)/shard_map/ppermute | solution.py:176
  214.5 1.7 collective-permute-start.17
  217.6 1.6 collective-permute-done.17
  (95 shorter events, 38.7 us)
Async XLA Ops:
  0.6 39.5 %collective-permute-start.6 = (bf16[784,56]{0,1:T(8,128)(2,1)}, bf16[784,56]{0,1:T(8,128)(2,1)S(1)}, u32[]{:S(2)}, u32[]{:S(2)}) collective-permute-start(bf16[784,56]{0,1:T(8,128)(2,1)} %param.5), channel_id=1, source_target_pairs={{0,8},{1,9},{2,10},{3,11},{4,12},{5,13},{6,14},{7,15},{8,0},{9,1},... | collective-permute-start | bytes 263432 | tf_op jit(solution)/shard_map/ppermute | solution.py:176
  2.2 56.7 %collective-permute-start.8 = (bf16[784,56]{0,1:T(8,128)(2,1)}, bf16[784,56]{0,1:T(8,128)(2,1)S(1)}, u32[]{:S(2)}, u32[]{:S(2)}) collective-permute-start(bf16[784,56]{0,1:T(8,128)(2,1)} %param.5), channel_id=1, source_target_pairs={{0,24},{1,25},{2,26},{3,27},{4,28},{5,29},{6,30},{7,31},{8,16},{9,... | collective-permute-start | bytes 263432 | tf_op jit(solution)/shard_map/ppermute | solution.py:176
  18.4 79.1 %collective-permute-start.3 = (bf16[2,112,2048]{2,1,0:T(8,128)(2,1)}, bf16[2,112,2048]{2,1,0:T(8,128)(2,1)}, u32[]{:S(2)}, u32[]{:S(2)}) collective-permute-start(bf16[2,112,2048]{2,1,0:T(8,128)(2,1)} %contract.3.refs_0_.own_ref), channel_id=1, source_target_pairs={{0,16},{1,17},{2,18},{3,19},{4,20},{5,21},{6,22},{7,23},{8,24},{9,... | collective-permute-start | bytes 2752520 | tf_op jit(solution)/shard_map/ppermute | solution.py:176
  18.9 22.8 %collective-permute-start.2 = (bf16[2,112,2048]{2,1,0:T(8,128)(2,1)}, bf16[2,112,2048]{2,1,0:T(8,128)(2,1)}, u32[]{:S(2)}, u32[]{:S(2)}) collective-permute-start(bf16[2,112,2048]{2,1,0:T(8,128)(2,1)} %contract.3.refs_0_.own_ref), channel_id=1, source_target_pairs={{0,8},{1,9},{2,10},{3,11},{4,12},{5,13},{6,14},{7,15},{8,0},{9,1},... | collective-permute-start | bytes 2752520 | tf_op jit(solution)/shard_map/ppermute | solution.py:176
  39.5 19.2 %copy-start.19 = (bf16[784,56]{0,1:T(8,128)(2,1)S(1)}, bf16[784,56]{0,1:T(8,128)(2,1)}, u32[]{:S(2)}) copy-start(bf16[784,56]{0,1:T(8,128)(2,1)} %param.5) | copy-start | bytes 263428
  39.5 55.9 %collective-permute-start.5 = (bf16[2,168,2048]{2,1,0:T(8,128)(2,1)S(1)}, bf16[2,168,2048]{2,1,0:T(8,128)(2,1)S(1)}, u32[]{:S(2)}, u32[]{:S(2)}) collective-permute-start(bf16[2,168,2048]{2,1,0:T(8,128)(2,1)S(1)} %contract.4.refs_1_.own_ref), channel_id=1, source_target_pairs={{0,8},{1,9},{2,10},{3,11},{4,12},{5,13},{6,14},{7,15},{8,0},{9,1},... | collective-permute-start | bytes 4128776 | tf_op jit(solution)/shard_map/ppermute | solution.py:176
  40.2 17.6 %copy-start.20 = (bf16[784,56]{0,1:T(8,128)(2,1)}, bf16[784,56]{0,1:T(8,128)(2,1)S(1)}, u32[]{:S(2)}) copy-start(bf16[784,56]{0,1:T(8,128)(2,1)S(1)} %collective-permute-done.6) | copy-start | bytes 263428
  40.2 33.2 %collective-permute-start = (bf16[2,168,2048]{2,1,0:T(8,128)(2,1)S(1)}, bf16[2,168,2048]{2,1,0:T(8,128)(2,1)}, u32[]{:S(2)}, u32[]{:S(2)}) collective-permute-start(bf16[2,168,2048]{2,1,0:T(8,128)(2,1)S(1)} %contract.4.refs_1_.own_ref), channel_id=1, source_target_pairs={{0,16},{1,17},{2,18},{3,19},{4,20},{5,21},{6,22},{7,23},{8,24},{9,... | collective-permute-start | bytes 4128776 | tf_op jit(solution)/shard_map/ppermute | solution.py:176
  41.7 55.7 %collective-permute-start.4 = (bf16[2,112,2048]{2,1,0:T(8,128)(2,1)}, bf16[2,112,2048]{2,1,0:T(8,128)(2,1)}, u32[]{:S(2)}, u32[]{:S(2)}) collective-permute-start(bf16[2,112,2048]{2,1,0:T(8,128)(2,1)} %collective-permute-done.2.x_ref), channel_id=1, source_target_pairs={{0,16},{1,17},{2,18},{3,19},{4,20},{5,21},{6,22},{7,23},{8,24},{9,... | collective-permute-start | bytes 2752520 | tf_op jit(solution)/shard_map/ppermute | solution.py:176
  58.9 33.7 %collective-permute-start.7 = (bf16[784,56]{0,1:T(8,128)(2,1)S(1)}, bf16[784,56]{0,1:T(8,128)(2,1)}, u32[]{:S(2)}, u32[]{:S(2)}) collective-permute-start(bf16[784,56]{0,1:T(8,128)(2,1)S(1)} %copy-done.19), channel_id=1, source_target_pairs={{0,16},{1,17},{2,18},{3,19},{4,20},{5,21},{6,22},{7,23},{8,24},{9,... | collective-permute-start | bytes 263432 | tf_op jit(solution)/shard_map/ppermute | solution.py:176
  73.4 41.9 %collective-permute-start.1 = (bf16[2,168,2048]{2,1,0:T(8,128)(2,1)}, bf16[2,168,2048]{2,1,0:T(8,128)(2,1)}, u32[]{:S(2)}, u32[]{:S(2)}) collective-permute-start(bf16[2,168,2048]{2,1,0:T(8,128)(2,1)} %collective-permute-done.y_ref), channel_id=1, source_target_pairs={{0,8},{1,9},{2,10},{3,11},{4,12},{5,13},{6,14},{7,15},{8,0},{9,1},... | collective-permute-start | bytes 4128776 | tf_op jit(solution)/shard_map/ppermute | solution.py:176
  92.6 22.7 %collective-permute-start.12 = (bf16[2,112,2048]{2,1,0:T(8,128)(2,1)}, bf16[2,112,2048]{2,1,0:T(8,128)(2,1)}, u32[]{:S(2)}, u32[]{:S(2)}) collective-permute-start(bf16[2,112,2048]{2,1,0:T(8,128)(2,1)} %copy-done.9), channel_id=1, source_target_pairs={{0,16},{1,17},{2,18},{3,19},{4,20},{5,21},{6,22},{7,23},{8,24},{9,... | collective-permute-start | bytes 2752520 | tf_op jit(solution)/shard_map/ppermute | solution.py:176
  95.5 24.9 %collective-permute-start.10 = (bf16[2,112,2048]{2,1,0:T(8,128)(2,1)}, bf16[2,112,2048]{2,1,0:T(8,128)(2,1)}, u32[]{:S(2)}, u32[]{:S(2)}) collective-permute-start(bf16[2,112,2048]{2,1,0:T(8,128)(2,1)} %copy-done.9), channel_id=1, source_target_pairs={{0,8},{1,9},{2,10},{3,11},{4,12},{5,13},{6,14},{7,15},{8,0},{9,1},... | collective-permute-start | bytes 2752520 | tf_op jit(solution)/shard_map/ppermute | solution.py:176
  109.5 3.3 %collective-permute-start.9 = (bf16[4,112,784]{2,1,0:T(8,128)(2,1)}, bf16[4,112,784]{2,1,0:T(8,128)(2,1)}, u32[]{:S(2)}, u32[]{:S(2)}) collective-permute-start(bf16[4,112,784]{2,1,0:T(8,128)(2,1)} %get-tuple-element.34), channel_id=1, source_target_pairs={{0,1},{1,0},{2,3},{3,2},{4,5},{5,4},{6,7},{7,6},{8,9},{9,8},{10,11... | collective-permute-start | bytes 2107400 | tf_op jit(solution)/shard_map/ppermute | solution.py:176
  135.9 6.8 %collective-permute-start.13 = (bf16[4,168,784]{2,1,0:T(8,128)(2,1)}, bf16[4,168,784]{2,1,0:T(8,128)(2,1)}, u32[]{:S(2)}, u32[]{:S(2)}) collective-permute-start(bf16[4,168,784]{2,1,0:T(8,128)(2,1)} %get-tuple-element.43), channel_id=1, source_target_pairs={{0,1},{1,0},{2,3},{3,2},{4,5},{5,4},{6,7},{7,6},{8,9},{9,8},{10,11... | collective-permute-start | bytes 3161096 | tf_op jit(solution)/shard_map/ppermute | solution.py:176
  135.9 27.8 %all-to-all-start = ((bf16[4,112,784]{2,1,0:T(8,128)(2,1)}), bf16[4,112,784]{2,1,0:T(8,128)(2,1)}, u32[]{:S(2)}, u32[]{:S(2)}) async-start(bf16[4,112,784]{2,1,0:T(8,128)(2,1)} %merge.3), calls=%async_computation | async-start | bytes 1605632 | tf_op jit(solution)/shard_map/all_to_all | solution.py:244
  141.3 22.5 %collective-permute-start.11 = (bf16[2,112,2048]{2,1,0:T(8,128)(2,1)}, bf16[2,112,2048]{2,1,0:T(8,128)(2,1)}, u32[]{:S(2)}, u32[]{:S(2)}) collective-permute-start(bf16[2,112,2048]{2,1,0:T(8,128)(2,1)} %collective-permute-done.10.x_ref), channel_id=1, source_target_pairs={{0,16},{1,17},{2,18},{3,19},{4,20},{5,21},{6,22},{7,23},{8,24},{9,... | collective-permute-start | bytes 2752520 | tf_op jit(solution)/shard_map/ppermute | solution.py:176
  163.8 30.2 %all-to-all-start.1 = ((bf16[4,168,784]{2,1,0:T(8,128)(2,1)}), bf16[4,168,784]{2,1,0:T(8,128)(2,1)}, u32[]{:S(2)}, u32[]{:S(2)}) async-start(bf16[4,168,784]{2,1,0:T(8,128)(2,1)} %merge.4), calls=%async_computation.1 | async-start | bytes 2408448 | tf_op jit(solution)/shard_map/all_to_all | solution.py:244
  180.0 2.3 %collective-permute-start.14 = (bf16[4,112,784]{2,1,0:T(8,128)(2,1)S(1)}, bf16[4,112,784]{2,1,0:T(8,128)(2,1)S(1)}, u32[]{:S(2)}, u32[]{:S(2)}) collective-permute-start(bf16[4,112,784]{2,1,0:T(8,128)(2,1)S(1)} %get-tuple-element.50), channel_id=1, source_target_pairs={{0,1},{1,0},{2,3},{3,2},{4,5},{5,4},{6,7},{7,6},{8,9},{9,8},{10,11... | collective-permute-start | bytes 2107400 | tf_op jit(solution)/shard_map/ppermute | solution.py:176
  182.1 18.7 %collective-permute-start.15 = (f32[8,128]{1,0:T(8,128)S(1)}, f32[8,128]{1,0:T(8,128)S(1)}, u32[]{:S(2)}, u32[]{:S(2)}) collective-permute-start(f32[8,128]{1,0:T(8,128)S(1)} %broadcast_in_dim.3), channel_id=1, source_target_pairs={{0,1},{1,0},{2,3},{3,2},{4,5},{5,4},{6,7},{7,6},{8,9},{9,8},{10,11... | collective-permute-start | bytes 12296 | tf_op jit(solution)/shard_map/ppermute | solution.py:176
  185.7 34.7 %copy-start.3 = (f32[56,2048]{1,0:T(8,128)S(1)}, f32[56,2048]{1,0:T(8,128)}, u32[]{:S(2)}) copy-start(f32[56,2048]{1,0:T(8,128)} %copy-done.2) | copy-start | bytes 1376260
  193.9 28.8 %all-to-all-start.2 = ((bf16[4,112,784]{2,1,0:T(8,128)(2,1)}), bf16[4,112,784]{2,1,0:T(8,128)(2,1)S(1)}, u32[]{:S(2)}, u32[]{:S(2)}) async-start(bf16[4,112,784]{2,1,0:T(8,128)(2,1)} %merge.5), calls=%async_computation.2 | async-start | bytes 1605632 | tf_op jit(solution)/shard_map/all_to_all | solution.py:244
  201.4 12.6 %collective-permute-start.16 = (f32[8,128]{1,0:T(8,128)S(1)}, f32[8,128]{1,0:T(8,128)S(1)}, u32[]{:S(2)}, u32[]{:S(2)}) collective-permute-start(f32[8,128]{1,0:T(8,128)S(1)} %broadcast_add_fusion), channel_id=1, source_target_pairs={{0,2},{1,3},{2,0},{3,1},{4,6},{5,7},{6,4},{7,5},{8,10},{9,11},{10,... | collective-permute-start | bytes 12296 | tf_op jit(solution)/shard_map/ppermute | solution.py:176
  214.5 4.7 %collective-permute-start.17 = (f32[8,128]{1,0:T(8,128)S(1)}, f32[8,128]{1,0:T(8,128)S(1)}, u32[]{:S(2)}, u32[]{:S(2)}) collective-permute-start(f32[8,128]{1,0:T(8,128)S(1)} %fusion.2), channel_id=1, source_target_pairs={{0,4},{1,5},{2,6},{3,7},{4,0},{5,1},{6,2},{7,3},{8,12},{9,13},{10,... | collective-permute-start | bytes 12296 | tf_op jit(solution)/shard_map/ppermute | solution.py:176
  (19 other events, 69.0 us)

commit v4 on v3

--- a/solution.py
+++ b/solution.py
@@ -13,6 +13,17 @@
 AXES = ("outer", "inner")
 COLUMN_TILE = 256
 CUTS = (0, 2, 5, 7)
+ROUTES = "yxy"
+XY_DUE = ()
+Z_DUE = ()
+Z_SEND = (1, 2)
+XY_SEND = (0,)
+D_SEND = (1,)
+GATE = True
+GRAM_VMEM = 20
+GRAM_FLOPS = 4_000_000_000
+MERGE_VMEM = 8
+CONTRACT_FLOPS = 30_000_000_000
 
 
 def product_rows(p_ref, q_ref, rows, cols, scale, store):
@@ -59,7 +70,7 @@
         product_rows(p_ref, q_ref, rows, cols, scale, store)
 
 
-def contract(p4, q_factor, cuts):
+def contract(p4, q_factor, cuts, maps):
     _, half_i, bonds, columns = p4.shape
     bond = q_factor.shape[0]
     scale = 1.0 / math.sqrt(bonds)
@@ -88,14 +99,14 @@
             out_specs=[row_spec(rows)] + ([row_spec(half_i * bond)] if last else []),
             out_shape=[row_shape(rows)] + ([row_shape(half_i * bond)] if last else []),
             compiler_params=pltpu.CompilerParams(vmem_limit_bytes=52 << 20),
-            cost_estimate=pl.CostEstimate(flops=30_000_000_000, bytes_accessed=1000, transcendentals=0),
+            cost_estimate=pl.CostEstimate(flops=CONTRACT_FLOPS, bytes_accessed=1000, transcendentals=0),
             name="contract",
         )(p4, q_factor, *earlier)
         own = found[0]
         if not last:
-            q_factor, own = lax.optimization_barrier((q_factor, own))
+            q_factor, own, maps = lax.optimization_barrier((q_factor, own, maps))
         chunks.append(own)
-    return found[1], chunks
+    return found[1], chunks, maps
 
 
 def gram_kernel(core_ref, own_ref, x_ref, y_ref, d_ref, s_ref, t_ref, *refs):
@@ -135,31 +146,31 @@
         in_specs=[pl.BlockSpec(memory_space=pltpu.SMEM)] + [vmem] * len(args),
         out_specs=[vmem] * 3,
         out_shape=[out, out, jax.ShapeDtypeStruct((maps.shape[1], columns), F32)],
-        compiler_params=pltpu.CompilerParams(vmem_limit_bytes=40 << 20),
+        compiler_params=pltpu.CompilerParams(vmem_limit_bytes=GRAM_VMEM << 20),
         cost_estimate=pl.CostEstimate(
-            flops=1000, bytes_accessed=1000, transcendentals=0
+            flops=GRAM_FLOPS, bytes_accessed=1000, transcendentals=0
         ),
         name="gram",
     )(core, *args)
 
 
-def merge_kernel(o_ref, keep_ref, recv_ref, out_ref):
-    o = o_ref[0]
-    for d in range(4):
-        k = d ^ o
-        out_ref[d] = (keep_ref[k].astype(F32) + recv_ref[k].astype(F32)).astype(BF16)
-
-
-def merge_chunk(outer_index, keep, recv):
+def merge_kernel(place_ref, keep_ref, recv_ref, *out_refs):
+    for shift, out_ref in enumerate(out_refs):
+        k = place_ref[0] ^ place_ref[1] ^ shift
+        out_ref[...] = (keep_ref[k].astype(F32) + recv_ref[k].astype(F32)).astype(BF16)
+
+
+def merge_chunk(place, keep, recv):
     vmem = pl.BlockSpec(memory_space=pltpu.VMEM)
     return pl.pallas_call(
         merge_kernel,
         in_specs=[pl.BlockSpec(memory_space=pltpu.SMEM), vmem, vmem],
-        out_specs=vmem,
-        out_shape=jax.ShapeDtypeStruct(keep.shape, BF16),
+        out_specs=[vmem] * 4,
+        out_shape=[jax.ShapeDtypeStruct(keep.shape[1:], BF16)] * 4,
+        compiler_params=pltpu.CompilerParams(vmem_limit_bytes=MERGE_VMEM << 20),
         cost_estimate=pl.CostEstimate(flops=1000, bytes_accessed=1000, transcendentals=0),
         name="merge",
-    )(outer_index, keep, recv)
+    )(place, keep, recv)
 
 
 def pairs(target):
@@ -194,6 +205,10 @@
 
 def to_z2(o, z, c):
     return (o, z ^ 2, c)
+
+
+def to_z3(o, z, c):
+    return (o, z ^ 3, c)
 
 
 def other_core(o, z, c):
@@ -209,47 +224,63 @@
     outer = lax.axis_index("outer")
     core = lax.axis_index("inner") % 2
     core_vec = core.astype(jnp.int32).reshape(1)
-    outer_vec = outer.astype(jnp.int32).reshape(1)
+    place = jnp.stack([outer, lax.axis_index("inner") // 2]).astype(jnp.int32)
     p4 = p_factor.reshape(2, half_i, bonds, columns)
 
     maps = [truncation] + [move(truncation, to) for to in (to_x, to_y, to_diagonal)]
+    slab, chunks, maps = contract(p4, q_factor, CUTS, maps)
     maps = jnp.stack(maps).reshape(4, 2, half_rows, truncation.shape[1])
-    slab, chunks = contract(p4, q_factor, CUTS)
     slab = slab.reshape(2 * half_rows, columns)
 
     moved = []
     for t, own in enumerate(chunks):
         x = move(own, to_x)
         y = move(own, to_y)
-        d = move(x, to_y) if t % 2 == 0 else move(y, to_x)
+        x, y = lax.optimization_barrier((x, y))
+        if ROUTES[t] == "y":
+            d = move(x, to_y)
+        elif ROUTES[t] == "x":
+            d = move(y, to_x)
+        else:
+            d = move(own, to_diagonal)
         moved.append([x, y, d])
 
     sums = []
     absorbed = None
-    merged = None
     for t, own in enumerate(chunks):
         row0, row1 = CUTS[t] * bond, CUTS[t + 1] * bond
-        if merged is not None:
-            moved[t][2], merged = lax.optimization_barrier((moved[t][2], merged))
-            sums.append(merged)
-        if t + 1 < len(chunks):
+        if t in XY_DUE:
             moved[t][2], moved[t + 1][0], moved[t + 1][1] = lax.optimization_barrier(
                 (moved[t][2], moved[t + 1][0], moved[t + 1][1])
             )
+        if sums:
+            due = sums[-1] if t in Z_DUE else sums[-1][:1]
+            moved[t][2], *due = lax.optimization_barrier((moved[t][2], *due))
+            sums[-1][: len(due)] = due
         part = maps[:, :, row0:row1].reshape(4, 2 * (row1 - row0), -1).swapaxes(1, 2)
         keep, send, absorbed = gram_chunk(core_vec, (own, *moved[t]), slab, part, absorbed)
-        merged = merge_chunk(outer_vec, keep, move(send, other_core))
-    sums.append(merged)
-    sums = [
-        lax.all_to_all(m, "inner", 0, 0, axis_index_groups=[[0, 2, 4, 6], [1, 3, 5, 7]], tiled=True)
-        for m in sums
-    ]
-    sums = [jnp.sum(m.astype(F32), axis=0) for m in sums]
+        if t in Z_SEND:
+            send, *sums[-1] = lax.optimization_barrier((send, *sums[-1]))
+        if t in XY_SEND:
+            send, moved[t + 1][0], moved[t + 1][1] = lax.optimization_barrier(
+                (send, moved[t + 1][0], moved[t + 1][1])
+            )
+        if t in D_SEND:
+            send, moved[t + 1][2] = lax.optimization_barrier((send, moved[t + 1][2]))
+        recv = move(send, other_core)
+        pieces = merge_chunk(place, keep, recv)
+        pieces = list(pieces)
+        sums.append(pieces[:1] + [move(v, to) for v, to in zip(pieces[1:], (to_z1, to_z2, to_z3))])
+    group = sums[-1]
+
+    squares = jnp.full((8, 128), jnp.sum(absorbed * absorbed))
+    squares = squares + move(squares, other_core)
+    if GATE:
+        squares, group[1] = lax.optimization_barrier((squares, group[1]))
+    across = [move(squares, to) for to in (to_z1, to_z2, to_z3)]
+    squares = (squares + across[0]) + (across[1] + across[2])
+    sums = [sum(v.astype(F32) for v in group) for group in sums]
     gram = (jnp.concatenate(sums, axis=0) / total_columns).T
-
-    squares = jnp.full((8, 128), jnp.sum(absorbed * absorbed))
-    for to in (other_core, to_z1, to_z2):
-        squares = squares + move(squares, to)
     norm_scale = jnp.sqrt(squares[:1, :1] / (absorbed.shape[0] * total_columns) + 1e-06)
     return (gram, absorbed / norm_scale)
 

time: 228 us -> 201 us (0.88)
  waiting for transfers between devices: 74.1 us -> 67.3 us
  starting transfers between devices: 34.5 us -> 28.6 us
  Pallas kernels: 83.7 us -> 77.9 us
  local copies, waits for them, and re-layouts: 23.4 us -> 20 us
  other arithmetic: 6.76 us -> 3.79 us
    all_to_all x3 -> x0, starting transfers between devices: 17.3 us -> none  [paired_body(): lax.all_to_all(m, 'inner', 0, 0, axis_index_groups=[[0, 2, 4, 6], [1, 3,...]
    ppermute x18 -> x28, starting transfers between devices: 17.3 us -> 28.6 us  [move(): return lax.ppermute(value, AXES, pairs(target))]
    all_to_all x3 -> x0, waiting for transfers between devices: 8.26 us -> none  [paired_body(): lax.all_to_all(m, 'inner', 0, 0, axis_index_groups=[[0, 2, 4, 6], [1, 3,...]
    pallas_call x3, Pallas kernels: 7.87 us -> 2.31 us  [merge_chunk(): pl.pallas_call(merge_kernel, in_specs=[pl.BlockSpec(memory_space=pltpu.SM...]
    reduce_sum x3 -> x0, other arithmetic: 2.93 us -> none  [paired_body(): sums = [jnp.sum(m.astype(F32), axis=0) for m in sums]]
    ppermute x18 -> x28, waiting for transfers between devices: 65.8 us -> 67.3 us  [move(): return lax.ppermute(value, AXES, pairs(target))]
    unnamed x47 -> x37, local copies, waits for them, and re-layouts: 15.2 us -> 13.9 us
  transfers between devices with their start and end apart: 21 -> 28, of which waited for: 8 -> 12; matrix products, arithmetic and copies ran while one was open for 6% -> 5% of each run, Pallas kernels for 33% -> 38%
where the time goes in v4:
time: 201 us; the launch traced here: 199 us
  Pallas kernels  77.9 us (39%)
  waiting for transfers between devices  67.3 us (33%)
  starting transfers between devices  28.6 us (14%)
  local copies, waits for them, and re-layouts  20 us (10%)
  other arithmetic  3.79 us (2%)
    ppermute x28, waiting for transfers between devices, move(): return lax.ppermute(value, AXES, pairs(target))  67.3 us
    pallas_call x3, Pallas kernels, contract(): pl.pallas_call(functools.partial(last_kernel, cuts, scale) if last else f...  49.5 us
    ppermute x28, starting transfers between devices, move(): return lax.ppermute(value, AXES, pairs(target))  28.6 us
    pallas_call x3, Pallas kernels, gram_chunk(): pl.pallas_call(gram_kernel, in_specs=[pl.BlockSpec(memory_space=pltpu.SME...  26.1 us
    unnamed x37, local copies, waits for them, and re-layouts  13.9 us
  transfers between devices with their start and end apart: 28, of which 12 were waited for; matrix products, arithmetic and copies ran while one was open for 5% of the time, Pallas kernels for 38%

profile of v4, /device:TPU:8, one launch (start us, length us, event | category | flops | bytes accessed | tf_op | source)
XLA Modules:
  0.0 199.1 jit_solution(17935079495639224162)
XLA Ops:
  4.2 14.7 %contract.3.refs_0_.own_ref = bf16[2,112,2048]{2,1,0:T(8,128)(2,1)} custom-call(bf16[2,7,56,2048]{3,2,1,0:T(8,128)(2,1)} %bitcast.31, bf16[56,56,2048]{2,1,0:T(8,128)(2,1)} %q_ref.3), custom_call_target="tpu_custom_call" | custom-call | flops 30000001024 | bytes 1000 | tf_op jit(solution)/shard_map/contract/pallas_call | solution.py:95
  22.0 19.2 %contract.4.refs_1_.own_ref = bf16[2,168,2048]{2,1,0:T(8,128)(2,1)S(1)} custom-call(bf16[2,7,56,2048]{3,2,1,0:T(8,128)(2,1)} %bitcast.32, bf16[56,56,2048]{2,1,0:T(8,128)(2,1)} %q_ref.3), custom_call_target="tpu_custom_call" | custom-call | flops 30000001024 | bytes 1000 | tf_op jit(solution)/shard_map/contract/pallas_call | solution.py:95
  44.7 15.7 %contract.5 = (bf16[2,112,2048]{2,1,0:T(8,128)(2,1)}, bf16[2,392,2048]{2,1,0:T(8,128)(2,1)}) custom-call(bf16[2,7,56,2048]{3,2,1,0:T(8,128)(2,1)} %bitcast.33, bf16[56,56,2048]{2,1,0:T(8,128)(2,1)} %q_ref.3, bf16[2,112,2048]{2,1,0:T(8,128)(2,1)} %contract.3.refs_0_.own_ref, bf16[2,168,2048]{2,1,0:T(8,128)(2,1)} %copy-done), custom_call_target="tpu_custom_call" | custom-call | flops 30000001024 | bytes 1000 | tf_op jit(solution)/shard_map/contract/pallas_call | solution.py:95
  65.2 9.1 %collective-permute-done.6.x_ref = bf16[2,168,2048]{2,1,0:T(8,128)(2,1)S(1)} collective-permute-done((bf16[2,168,2048]{2,1,0:T(8,128)(2,1)S(1)}, bf16[2,168,2048]{2,1,0:T(8,128)(2,1)S(1)}, u32[]{:S(2)}, u32[]{:S(2)}) %collective-permute-start.6) | collective-permute-done | bytes 1376288 | tf_op jit(solution)/shard_map/ppermute | solution.py:187
  77.2 1.8 fusion.1
  79.2 15.5 %collective-permute-done.5.d_ref = bf16[2,112,2048]{2,1,0:T(8,128)(2,1)} collective-permute-done((bf16[2,112,2048]{2,1,0:T(8,128)(2,1)}, bf16[2,112,2048]{2,1,0:T(8,128)(2,1)}, u32[]{:S(2)}, u32[]{:S(2)}) %collective-permute-start.5) | collective-permute-done | bytes 917536 | tf_op jit(solution)/shard_map/ppermute | solution.py:187
  95.8 1.9 copy-done.6
  97.7 7.7 %gram.3 = (bf16[4,112,784]{2,1,0:T(8,128)(2,1)S(1)}, bf16[4,112,784]{2,1,0:T(8,128)(2,1)S(1)}, f32[56,2048]{1,0:T(8,128)S(1)}) custom-call(s32[1]{0:T(128)} %bitcast.core_ref, bf16[2,112,2048]{2,1,0:T(8,128)(2,1)} %contract.3.refs_0_.own_ref, bf16[2,112,2048]{2,1,0:T(8,128)(2,1)} %collective-permute-done.3.x_ref, bf16[2,112,2048]{2,1,0:T(8,128)(2,1)S(1)} %copy-done.5, ...), custom_call_target="tpu_custom_call" | custom-call | flops 4000000000 | bytes 1000 | tf_op jit(solution)/shard_map/gram/pallas_call | solution.py:144
  106.2 5.2 %collective-permute-done.14.y_ref = bf16[2,112,2048]{2,1,0:T(8,128)(2,1)} collective-permute-done((bf16[2,112,2048]{2,1,0:T(8,128)(2,1)}, bf16[2,112,2048]{2,1,0:T(8,128)(2,1)}, u32[]{:S(2)}, u32[]{:S(2)}) %collective-permute-start.14) | collective-permute-done | bytes 917536 | tf_op jit(solution)/shard_map/ppermute | solution.py:187
  114.9 2.6 %collective-permute-start.11 = (bf16[112,784]{1,0:T(8,128)(2,1)S(1)}, bf16[112,784]{1,0:T(8,128)(2,1)S(1)}, u32[]{:S(2)}, u32[]{:S(2)}) collective-permute-start(bf16[112,784]{1,0:T(8,128)(2,1)S(1)} %get-tuple-element.92), channel_id=1, source_target_pairs={{0,4},{1,5},{2,6},{3,7},{4,0},{5,1},{6,2},{7,3},{8,12},{9,13},{10,... | collective-permute-start | bytes 526856 | tf_op jit(solution)/shard_map/ppermute | solution.py:187
  117.9 3.1 %collective-permute-done.8.d_ref = bf16[2,168,2048]{2,1,0:T(8,128)(2,1)} collective-permute-done((bf16[2,168,2048]{2,1,0:T(8,128)(2,1)}, bf16[2,168,2048]{2,1,0:T(8,128)(2,1)}, u32[]{:S(2)}, u32[]{:S(2)}) %collective-permute-start.8) | collective-permute-done | bytes 1376288 | tf_op jit(solution)/shard_map/ppermute | solution.py:187
  122.3 1.9 copy-done.7
  125.3 10.1 %gram.4 = (bf16[4,168,784]{2,1,0:T(8,128)(2,1)S(1)}, bf16[4,168,784]{2,1,0:T(8,128)(2,1)}, f32[56,2048]{1,0:T(8,128)S(1)}) custom-call(s32[1]{0:T(128)} %bitcast.core_ref, bf16[2,168,2048]{2,1,0:T(8,128)(2,1)S(1)} %copy-done.1, bf16[2,168,2048]{2,1,0:T(8,128)(2,1)S(1)} %copy-done.3, bf16[2,168,2048]{2,1,0:T(8,128)(2,1)} %collective-permute-done.7.y_ref, ...), custom_call_target="tpu_custom_call" | custom-call | flops 4000000000 | bytes 1000 | tf_op jit(solution)/shard_map/gram/pallas_call | solution.py:144
  136.3 3.0 %collective-permute-done.16.recv_ref = bf16[4,168,784]{2,1,0:T(8,128)(2,1)S(1)} collective-permute-done((bf16[4,168,784]{2,1,0:T(8,128)(2,1)}, bf16[4,168,784]{2,1,0:T(8,128)(2,1)S(1)}, u32[]{:S(2)}, u32[]{:S(2)}) %collective-permute-start.16) | collective-permute-done | bytes 1053728 | tf_op jit(solution)/shard_map/ppermute | solution.py:187
  140.6 2.6 %collective-permute-start.18 = (bf16[168,784]{1,0:T(8,128)(2,1)S(1)}, bf16[168,784]{1,0:T(8,128)(2,1)S(1)}, u32[]{:S(2)}, u32[]{:S(2)}) collective-permute-start(bf16[168,784]{1,0:T(8,128)(2,1)S(1)} %get-tuple-element.111), channel_id=1, source_target_pairs={{0,4},{1,5},{2,6},{3,7},{4,0},{5,1},{6,2},{7,3},{8,12},{9,13},{10,... | collective-permute-start | bytes 790280 | tf_op jit(solution)/shard_map/ppermute | solution.py:187
  143.7 1.9 copy-done.8
  145.6 8.3 %gram.5 = (bf16[4,112,784]{2,1,0:T(8,128)(2,1)S(1)}, bf16[4,112,784]{2,1,0:T(8,128)(2,1)S(1)}, f32[56,2048]{1,0:T(8,128)S(1)}) custom-call(s32[1]{0:T(128)} %bitcast.core_ref, bf16[2,112,2048]{2,1,0:T(8,128)(2,1)} %get-tuple-element.98.own_ref, bf16[2,112,2048]{2,1,0:T(8,128)(2,1)} %collective-permute-done.13.x_ref, ...), custom_call_target="tpu_custom_call" | custom-call | flops 4000000000 | bytes 1000 | tf_op jit(solution)/shard_map/gram/pallas_call | solution.py:144
  153.8 9.8 %collective-permute-done.18 = bf16[168,784]{1,0:T(8,128)(2,1)S(1)} collective-permute-done((bf16[168,784]{1,0:T(8,128)(2,1)S(1)}, bf16[168,784]{1,0:T(8,128)(2,1)S(1)}, u32[]{:S(2)}, u32[]{:S(2)}) %collective-permute-start.18) | collective-permute-done | bytes 263456 | tf_op jit(solution)/shard_map/ppermute | solution.py:187
  163.6 6.3 %collective-permute-done.19 = bf16[168,784]{1,0:T(8,128)(2,1)S(1)} collective-permute-done((bf16[168,784]{1,0:T(8,128)(2,1)S(1)}, bf16[168,784]{1,0:T(8,128)(2,1)S(1)}, u32[]{:S(2)}, u32[]{:S(2)}) %collective-permute-start.19) | collective-permute-done | bytes 263456 | tf_op jit(solution)/shard_map/ppermute | solution.py:187
  174.2 3.0 %collective-permute-start.23 = (bf16[112,784]{1,0:T(8,128)(2,1)S(1)}, bf16[112,784]{1,0:T(8,128)(2,1)S(1)}, u32[]{:S(2)}, u32[]{:S(2)}) collective-permute-start(bf16[112,784]{1,0:T(8,128)(2,1)S(1)} %get-tuple-element.123), channel_id=1, source_target_pairs={{0,4},{1,5},{2,6},{3,7},{4,0},{5,1},{6,2},{7,3},{8,12},{9,13},{10,... | collective-permute-start | bytes 526856 | tf_op jit(solution)/shard_map/ppermute | solution.py:187
  177.8 5.2 %collective-permute-done.22 = bf16[112,784]{1,0:T(8,128)(2,1)S(1)} collective-permute-done((bf16[112,784]{1,0:T(8,128)(2,1)S(1)}, bf16[112,784]{1,0:T(8,128)(2,1)S(1)}, u32[]{:S(2)}, u32[]{:S(2)}) %collective-permute-start.22) | collective-permute-done | bytes 175648 | tf_op jit(solution)/shard_map/ppermute | solution.py:187
  183.0 2.5 %collective-permute-start.25 = (f32[8,128]{1,0:T(8,128)S(1)}, f32[8,128]{1,0:T(8,128)S(1)}, u32[]{:S(2)}, u32[]{:S(2)}) collective-permute-start(f32[8,128]{1,0:T(8,128)S(1)} %broadcast_add_fusion), channel_id=1, source_target_pairs={{0,2},{1,3},{2,0},{3,1},{4,6},{5,7},{6,4},{7,5},{8,10},{9,11},{10,... | collective-permute-start | bytes 12296 | tf_op jit(solution)/shard_map/ppermute | solution.py:187
  187.0 4.4 %collective-permute-done.23 = bf16[112,784]{1,0:T(8,128)(2,1)S(1)} collective-permute-done((bf16[112,784]{1,0:T(8,128)(2,1)S(1)}, bf16[112,784]{1,0:T(8,128)(2,1)S(1)}, u32[]{:S(2)}, u32[]{:S(2)}) %collective-permute-start.23) | collective-permute-done | bytes 175648 | tf_op jit(solution)/shard_map/ppermute | solution.py:187
  191.4 4.4 %collective-permute-done.24 = bf16[112,784]{1,0:T(8,128)(2,1)S(1)} collective-permute-done((bf16[112,784]{1,0:T(8,128)(2,1)S(1)}, bf16[112,784]{1,0:T(8,128)(2,1)S(1)}, u32[]{:S(2)}, u32[]{:S(2)}) %collective-permute-start.24) | collective-permute-done | bytes 175648 | tf_op jit(solution)/shard_map/ppermute | solution.py:187
  (99 shorter events, 37.8 us)
Async XLA Ops:
  0.6 18.2 %collective-permute-start = (bf16[784,56]{0,1:T(8,128)(2,1)}, bf16[784,56]{0,1:T(8,128)(2,1)S(1)}, u32[]{:S(2)}, u32[]{:S(2)}) collective-permute-start(bf16[784,56]{0,1:T(8,128)(2,1)} %param.5), channel_id=1, source_target_pairs={{0,8},{1,9},{2,10},{3,11},{4,12},{5,13},{6,14},{7,15},{8,0},{9,1},... | collective-permute-start | bytes 263432 | tf_op jit(solution)/shard_map/ppermute | solution.py:187
  2.2 16.7 %collective-permute-start.1 = (bf16[784,56]{0,1:T(8,128)(2,1)}, bf16[784,56]{0,1:T(8,128)(2,1)S(1)}, u32[]{:S(2)}, u32[]{:S(2)}) collective-permute-start(bf16[784,56]{0,1:T(8,128)(2,1)} %param.5), channel_id=1, source_target_pairs={{0,16},{1,17},{2,18},{3,19},{4,20},{5,21},{6,22},{7,23},{8,24},{9,... | collective-permute-start | bytes 263432 | tf_op jit(solution)/shard_map/ppermute | solution.py:187
  3.7 15.2 %collective-permute-start.2 = (bf16[784,56]{0,1:T(8,128)(2,1)}, bf16[784,56]{0,1:T(8,128)(2,1)S(1)}, u32[]{:S(2)}, u32[]{:S(2)}) collective-permute-start(bf16[784,56]{0,1:T(8,128)(2,1)} %param.5), channel_id=1, source_target_pairs={{0,24},{1,25},{2,26},{3,27},{4,28},{5,29},{6,30},{7,31},{8,16},{9,... | collective-permute-start | bytes 263432 | tf_op jit(solution)/shard_map/ppermute | solution.py:187
  18.9 23.4 %collective-permute-start.3 = (bf16[2,112,2048]{2,1,0:T(8,128)(2,1)}, bf16[2,112,2048]{2,1,0:T(8,128)(2,1)}, u32[]{:S(2)}, u32[]{:S(2)}) collective-permute-start(bf16[2,112,2048]{2,1,0:T(8,128)(2,1)} %contract.3.refs_0_.own_ref), channel_id=1, source_target_pairs={{0,8},{1,9},{2,10},{3,11},{4,12},{5,13},{6,14},{7,15},{8,0},{9,1},... | collective-permute-start | bytes 2752520 | tf_op jit(solution)/shard_map/ppermute | solution.py:187
  20.4 21.8 %collective-permute-start.4 = (bf16[2,112,2048]{2,1,0:T(8,128)(2,1)}, bf16[2,112,2048]{2,1,0:T(8,128)(2,1)S(1)}, u32[]{:S(2)}, u32[]{:S(2)}) collective-permute-start(bf16[2,112,2048]{2,1,0:T(8,128)(2,1)} %contract.3.refs_0_.own_ref), channel_id=1, source_target_pairs={{0,16},{1,17},{2,18},{3,19},{4,20},{5,21},{6,22},{7,23},{8,24},{9,... | collective-permute-start | bytes 2752520 | tf_op jit(solution)/shard_map/ppermute | solution.py:187
  41.2 33.2 %collective-permute-start.6 = (bf16[2,168,2048]{2,1,0:T(8,128)(2,1)S(1)}, bf16[2,168,2048]{2,1,0:T(8,128)(2,1)S(1)}, u32[]{:S(2)}, u32[]{:S(2)}) collective-permute-start(bf16[2,168,2048]{2,1,0:T(8,128)(2,1)S(1)} %contract.4.refs_1_.own_ref), channel_id=1, source_target_pairs={{0,8},{1,9},{2,10},{3,11},{4,12},{5,13},{6,14},{7,15},{8,0},{9,1},... | collective-permute-start | bytes 4128776 | tf_op jit(solution)/shard_map/ppermute | solution.py:187
  41.8 33.2 %collective-permute-start.7 = (bf16[2,168,2048]{2,1,0:T(8,128)(2,1)S(1)}, bf16[2,168,2048]{2,1,0:T(8,128)(2,1)}, u32[]{:S(2)}, u32[]{:S(2)}) collective-permute-start(bf16[2,168,2048]{2,1,0:T(8,128)(2,1)S(1)} %contract.4.refs_1_.own_ref), channel_id=1, source_target_pairs={{0,16},{1,17},{2,18},{3,19},{4,20},{5,21},{6,22},{7,23},{8,24},{9,... | collective-permute-start | bytes 4128776 | tf_op jit(solution)/shard_map/ppermute | solution.py:187
  43.2 51.4 %collective-permute-start.5 = (bf16[2,112,2048]{2,1,0:T(8,128)(2,1)}, bf16[2,112,2048]{2,1,0:T(8,128)(2,1)}, u32[]{:S(2)}, u32[]{:S(2)}) collective-permute-start(bf16[2,112,2048]{2,1,0:T(8,128)(2,1)} %collective-permute-done.3.x_ref), channel_id=1, source_target_pairs={{0,16},{1,17},{2,18},{3,19},{4,20},{5,21},{6,22},{7,23},{8,24},{9,... | collective-permute-start | bytes 2752520 | tf_op jit(solution)/shard_map/ppermute | solution.py:187
  60.4 45.9 %collective-permute-start.13 = (bf16[2,112,2048]{2,1,0:T(8,128)(2,1)}, bf16[2,112,2048]{2,1,0:T(8,128)(2,1)}, u32[]{:S(2)}, u32[]{:S(2)}) collective-permute-start(bf16[2,112,2048]{2,1,0:T(8,128)(2,1)} %get-tuple-element.98.own_ref), channel_id=1, source_target_pairs={{0,8},{1,9},{2,10},{3,11},{4,12},{5,13},{6,14},{7,15},{8,0},{9,1},... | collective-permute-start | bytes 2752520 | tf_op jit(solution)/shard_map/ppermute | solution.py:187
  61.9 49.5 %collective-permute-start.14 = (bf16[2,112,2048]{2,1,0:T(8,128)(2,1)}, bf16[2,112,2048]{2,1,0:T(8,128)(2,1)}, u32[]{:S(2)}, u32[]{:S(2)}) collective-permute-start(bf16[2,112,2048]{2,1,0:T(8,128)(2,1)} %get-tuple-element.98.own_ref), channel_id=1, source_target_pairs={{0,16},{1,17},{2,18},{3,19},{4,20},{5,21},{6,22},{7,23},{8,24},{9,... | collective-permute-start | bytes 2752520 | tf_op jit(solution)/shard_map/ppermute | solution.py:187
  75.0 46.0 %collective-permute-start.8 = (bf16[2,168,2048]{2,1,0:T(8,128)(2,1)}, bf16[2,168,2048]{2,1,0:T(8,128)(2,1)}, u32[]{:S(2)}, u32[]{:S(2)}) collective-permute-start(bf16[2,168,2048]{2,1,0:T(8,128)(2,1)} %collective-permute-done.7.y_ref), channel_id=1, source_target_pairs={{0,8},{1,9},{2,10},{3,11},{4,12},{5,13},{6,14},{7,15},{8,0},{9,1},... | collective-permute-start | bytes 4128776 | tf_op jit(solution)/shard_map/ppermute | solution.py:187
  111.4 24.7 %collective-permute-start.15 = (bf16[2,112,2048]{2,1,0:T(8,128)(2,1)}, bf16[2,112,2048]{2,1,0:T(8,128)(2,1)}, u32[]{:S(2)}, u32[]{:S(2)}) collective-permute-start(bf16[2,112,2048]{2,1,0:T(8,128)(2,1)} %collective-permute-done.13.x_ref), channel_id=1, source_target_pairs={{0,16},{1,17},{2,18},{3,19},{4,20},{5,21},{6,22},{7,23},{8,24},{9,... | collective-permute-start | bytes 2752520 | tf_op jit(solution)/shard_map/ppermute | solution.py:187
  114.4 21.0 %collective-permute-start.10 = (bf16[112,784]{1,0:T(8,128)(2,1)S(1)}, bf16[112,784]{1,0:T(8,128)(2,1)S(1)}, u32[]{:S(2)}, u32[]{:S(2)}) collective-permute-start(bf16[112,784]{1,0:T(8,128)(2,1)S(1)} %get-tuple-element.91), channel_id=1, source_target_pairs={{0,2},{1,3},{2,0},{3,1},{4,6},{5,7},{6,4},{7,5},{8,10},{9,11},{10,... | collective-permute-start | bytes 526856 | tf_op jit(solution)/shard_map/ppermute | solution.py:187
  114.9 20.5 %collective-permute-start.11 = (bf16[112,784]{1,0:T(8,128)(2,1)S(1)}, bf16[112,784]{1,0:T(8,128)(2,1)S(1)}, u32[]{:S(2)}, u32[]{:S(2)}) collective-permute-start(bf16[112,784]{1,0:T(8,128)(2,1)S(1)} %get-tuple-element.92), channel_id=1, source_target_pairs={{0,4},{1,5},{2,6},{3,7},{4,0},{5,1},{6,2},{7,3},{8,12},{9,13},{10,... | collective-permute-start | bytes 526856 | tf_op jit(solution)/shard_map/ppermute | solution.py:187
  117.5 17.9 %collective-permute-start.12 = (bf16[112,784]{1,0:T(8,128)(2,1)S(1)}, bf16[112,784]{1,0:T(8,128)(2,1)S(1)}, u32[]{:S(2)}, u32[]{:S(2)}) collective-permute-start(bf16[112,784]{1,0:T(8,128)(2,1)S(1)} %get-tuple-element.93), channel_id=1, source_target_pairs={{0,6},{1,7},{2,4},{3,5},{4,2},{5,3},{6,0},{7,1},{8,14},{9,15},{10,... | collective-permute-start | bytes 526856 | tf_op jit(solution)/shard_map/ppermute | solution.py:187
  140.1 13.7 %collective-permute-start.17 = (bf16[168,784]{1,0:T(8,128)(2,1)S(1)}, bf16[168,784]{1,0:T(8,128)(2,1)S(1)}, u32[]{:S(2)}, u32[]{:S(2)}) collective-permute-start(bf16[168,784]{1,0:T(8,128)(2,1)S(1)} %get-tuple-element.110), channel_id=1, source_target_pairs={{0,2},{1,3},{2,0},{3,1},{4,6},{5,7},{6,4},{7,5},{8,10},{9,11},{10,... | collective-permute-start | bytes 790280 | tf_op jit(solution)/shard_map/ppermute | solution.py:187
  140.6 23.0 %collective-permute-start.18 = (bf16[168,784]{1,0:T(8,128)(2,1)S(1)}, bf16[168,784]{1,0:T(8,128)(2,1)S(1)}, u32[]{:S(2)}, u32[]{:S(2)}) collective-permute-start(bf16[168,784]{1,0:T(8,128)(2,1)S(1)} %get-tuple-element.111), channel_id=1, source_target_pairs={{0,4},{1,5},{2,6},{3,7},{4,0},{5,1},{6,2},{7,3},{8,12},{9,13},{10,... | collective-permute-start | bytes 790280 | tf_op jit(solution)/shard_map/ppermute | solution.py:187
  143.2 26.7 %collective-permute-start.19 = (bf16[168,784]{1,0:T(8,128)(2,1)S(1)}, bf16[168,784]{1,0:T(8,128)(2,1)S(1)}, u32[]{:S(2)}, u32[]{:S(2)}) collective-permute-start(bf16[168,784]{1,0:T(8,128)(2,1)S(1)} %get-tuple-element.112), channel_id=1, source_target_pairs={{0,6},{1,7},{2,4},{3,5},{4,2},{5,3},{6,0},{7,1},{8,14},{9,15},{10,... | collective-permute-start | bytes 790280 | tf_op jit(solution)/shard_map/ppermute | solution.py:187
  174.1 8.9 %collective-permute-start.22 = (bf16[112,784]{1,0:T(8,128)(2,1)S(1)}, bf16[112,784]{1,0:T(8,128)(2,1)S(1)}, u32[]{:S(2)}, u32[]{:S(2)}) collective-permute-start(bf16[112,784]{1,0:T(8,128)(2,1)S(1)} %get-tuple-element.121), channel_id=1, source_target_pairs={{0,2},{1,3},{2,0},{3,1},{4,6},{5,7},{6,4},{7,5},{8,10},{9,11},{10,... | collective-permute-start | bytes 526856 | tf_op jit(solution)/shard_map/ppermute | solution.py:187
  174.2 17.2 %collective-permute-start.23 = (bf16[112,784]{1,0:T(8,128)(2,1)S(1)}, bf16[112,784]{1,0:T(8,128)(2,1)S(1)}, u32[]{:S(2)}, u32[]{:S(2)}) collective-permute-start(bf16[112,784]{1,0:T(8,128)(2,1)S(1)} %get-tuple-element.123), channel_id=1, source_target_pairs={{0,4},{1,5},{2,6},{3,7},{4,0},{5,1},{6,2},{7,3},{8,12},{9,13},{10,... | collective-permute-start | bytes 526856 | tf_op jit(solution)/shard_map/ppermute | solution.py:187
  177.2 18.6 %collective-permute-start.24 = (bf16[112,784]{1,0:T(8,128)(2,1)S(1)}, bf16[112,784]{1,0:T(8,128)(2,1)S(1)}, u32[]{:S(2)}, u32[]{:S(2)}) collective-permute-start(bf16[112,784]{1,0:T(8,128)(2,1)S(1)} %get-tuple-element.124), channel_id=1, source_target_pairs={{0,6},{1,7},{2,4},{3,5},{4,2},{5,3},{6,0},{7,1},{8,14},{9,15},{10,... | collective-permute-start | bytes 526856 | tf_op jit(solution)/shard_map/ppermute | solution.py:187
  183.0 14.1 %collective-permute-start.25 = (f32[8,128]{1,0:T(8,128)S(1)}, f32[8,128]{1,0:T(8,128)S(1)}, u32[]{:S(2)}, u32[]{:S(2)}) collective-permute-start(f32[8,128]{1,0:T(8,128)S(1)} %broadcast_add_fusion), channel_id=1, source_target_pairs={{0,2},{1,3},{2,0},{3,1},{4,6},{5,7},{6,4},{7,5},{8,10},{9,11},{10,... | collective-permute-start | bytes 12296 | tf_op jit(solution)/shard_map/ppermute | solution.py:187
  185.5 11.6 %collective-permute-start.26 = (f32[8,128]{1,0:T(8,128)S(1)}, f32[8,128]{1,0:T(8,128)S(1)}, u32[]{:S(2)}, u32[]{:S(2)}) collective-permute-start(f32[8,128]{1,0:T(8,128)S(1)} %broadcast_add_fusion), channel_id=1, source_target_pairs={{0,4},{1,5},{2,6},{3,7},{4,0},{5,1},{6,2},{7,3},{8,12},{9,13},{10,... | collective-permute-start | bytes 12296 | tf_op jit(solution)/shard_map/ppermute | solution.py:187
  185.8 11.3 %collective-permute-start.27 = (f32[8,128]{1,0:T(8,128)S(1)}, f32[8,128]{1,0:T(8,128)S(1)}, u32[]{:S(2)}, u32[]{:S(2)}) collective-permute-start(f32[8,128]{1,0:T(8,128)S(1)} %broadcast_add_fusion), channel_id=1, source_target_pairs={{0,6},{1,7},{2,4},{3,5},{4,2},{5,3},{6,0},{7,1},{8,14},{9,15},{10,... | collective-permute-start | bytes 12296 | tf_op jit(solution)/shard_map/ppermute | solution.py:187
  (21 other events, 154.5 us)

commit v5 on v4

--- a/solution.py
+++ b/solution.py
@@ -16,10 +16,17 @@
 ROUTES = "yxy"
 XY_DUE = ()
 Z_DUE = ()
-Z_SEND = (1, 2)
-XY_SEND = (0,)
+Z_PARTS = {1: (1, 2, 3), 2: (1, 2)}
+XY_SEND = ()
 D_SEND = (1,)
 GATE = True
+MAPS_AT = 1
+LAST_VMEM = 52
+TIE = False
+X_AFTER = ()
+PAIRED = (0, 1, 2)
+DUE_GRAM = {}
+DUE_SEND = {}
 GRAM_VMEM = 20
 GRAM_FLOPS = 4_000_000_000
 MERGE_VMEM = 8
@@ -70,7 +77,7 @@
         product_rows(p_ref, q_ref, rows, cols, scale, store)
 
 
-def contract(p4, q_factor, cuts, maps):
+def contract(p4, q_factor, cuts, truncation):
     _, half_i, bonds, columns = p4.shape
     bond = q_factor.shape[0]
     scale = 1.0 / math.sqrt(bonds)
@@ -87,6 +94,9 @@
         pl.BlockSpec((bond, bonds, tile), lambda c: (0, 0, c)),
     ]
     chunks = []
+    maps = None
+    if not TIE:
+        maps = [truncation] + [move(truncation, to) for to in (to_x, to_y, to_diagonal)]
     for lo, hi in zip(cuts, cuts[1:]):
         last = hi == cuts[-1]
         rows = (hi - lo) * bond
@@ -98,24 +108,31 @@
             in_specs=factor_specs + [row_spec(e.shape[1]) for e in earlier],
             out_specs=[row_spec(rows)] + ([row_spec(half_i * bond)] if last else []),
             out_shape=[row_shape(rows)] + ([row_shape(half_i * bond)] if last else []),
-            compiler_params=pltpu.CompilerParams(vmem_limit_bytes=52 << 20),
+            compiler_params=pltpu.CompilerParams(vmem_limit_bytes=(LAST_VMEM if last else 52) << 20),
             cost_estimate=pl.CostEstimate(flops=CONTRACT_FLOPS, bytes_accessed=1000, transcendentals=0),
             name="contract",
         )(p4, q_factor, *earlier)
         own = found[0]
         if not last:
-            q_factor, own, maps = lax.optimization_barrier((q_factor, own, maps))
+            q_factor, own = lax.optimization_barrier((q_factor, own))
+            if TIE and not chunks:
+                truncation, own = lax.optimization_barrier((truncation, own))
+                maps = [truncation] + [move(truncation, to) for to in (to_x, to_y, to_diagonal)]
+            if len(chunks) == MAPS_AT:
+                q_factor, maps = lax.optimization_barrier((q_factor, maps))
         chunks.append(own)
     return found[1], chunks, maps
 
 
-def gram_kernel(core_ref, own_ref, x_ref, y_ref, d_ref, s_ref, t_ref, *refs):
+def gram_kernel(parts, core_ref, own_ref, x_ref, y_ref, *refs):
+    diagonal, (s_ref, t_ref), refs = refs[:parts], refs[parts : parts + 2], refs[parts + 2 :]
     keep_ref, send_ref, sum_ref = refs[-3:]
     core = core_ref[0]
     rows = x_ref.shape[1]
     terms = []
-    for k, block in enumerate((own_ref, x_ref, y_ref, d_ref)):
-        left = block[...].reshape(2 * rows, block.shape[2])
+    for k, block in enumerate(((own_ref,), (x_ref,), (y_ref,), diagonal)):
+        left = [part[...].reshape(-1, part.shape[2]) for part in block]
+        left = left[0] if len(left) == 1 else jnp.concatenate(left, axis=0)
         value = lax.dot_general(
             left, s_ref[...], (((1,), (1,)), ((), ())), preferred_element_type=F32
         ).astype(BF16)
@@ -142,7 +159,7 @@
     vmem = pl.BlockSpec(memory_space=pltpu.VMEM)
     args = (*blocks, slab, maps) + (() if running is None else (running,))
     return pl.pallas_call(
-        gram_kernel,
+        functools.partial(gram_kernel, len(blocks) - 3),
         in_specs=[pl.BlockSpec(memory_space=pltpu.SMEM)] + [vmem] * len(args),
         out_specs=[vmem] * 3,
         out_shape=[out, out, jax.ShapeDtypeStruct((maps.shape[1], columns), F32)],
@@ -227,20 +244,25 @@
     place = jnp.stack([outer, lax.axis_index("inner") // 2]).astype(jnp.int32)
     p4 = p_factor.reshape(2, half_i, bonds, columns)
 
-    maps = [truncation] + [move(truncation, to) for to in (to_x, to_y, to_diagonal)]
-    slab, chunks, maps = contract(p4, q_factor, CUTS, maps)
+    slab, chunks, maps = contract(p4, q_factor, CUTS, truncation)
     maps = jnp.stack(maps).reshape(4, 2, half_rows, truncation.shape[1])
     slab = slab.reshape(2 * half_rows, columns)
 
     moved = []
     for t, own in enumerate(chunks):
-        x = move(own, to_x)
+        source = own
+        if t in X_AFTER:
+            source, moved[t - 1][1] = lax.optimization_barrier((own, moved[t - 1][1]))
+        x = move(source, to_x)
         y = move(own, to_y)
-        x, y = lax.optimization_barrier((x, y))
+        if t in PAIRED:
+            x, y = lax.optimization_barrier((x, y))
         if ROUTES[t] == "y":
             d = move(x, to_y)
         elif ROUTES[t] == "x":
             d = move(y, to_x)
+        elif ROUTES[t] == "s":
+            d = (move(x[:1], to_y), move(y[1:], to_x))
         else:
             d = move(own, to_diagonal)
         moved.append([x, y, d])
@@ -249,6 +271,8 @@
     absorbed = None
     for t, own in enumerate(chunks):
         row0, row1 = CUTS[t] * bond, CUTS[t + 1] * bond
+        for chunk, which in DUE_GRAM.get(t, ()):
+            moved[t][2], moved[chunk][which] = lax.optimization_barrier((moved[t][2], moved[chunk][which]))
         if t in XY_DUE:
             moved[t][2], moved[t + 1][0], moved[t + 1][1] = lax.optimization_barrier(
                 (moved[t][2], moved[t + 1][0], moved[t + 1][1])
@@ -258,9 +282,11 @@
             moved[t][2], *due = lax.optimization_barrier((moved[t][2], *due))
             sums[-1][: len(due)] = due
         part = maps[:, :, row0:row1].reshape(4, 2 * (row1 - row0), -1).swapaxes(1, 2)
-        keep, send, absorbed = gram_chunk(core_vec, (own, *moved[t]), slab, part, absorbed)
-        if t in Z_SEND:
-            send, *sums[-1] = lax.optimization_barrier((send, *sums[-1]))
+        keep, send, absorbed = gram_chunk(core_vec, (own, *jax.tree.leaves(moved[t])), slab, part, absorbed)
+        for part in Z_PARTS.get(t, ()):
+            send, sums[-1][part] = lax.optimization_barrier((send, sums[-1][part]))
+        for chunk, which in DUE_SEND.get(t, ()):
+            send, moved[chunk][which] = lax.optimization_barrier((send, moved[chunk][which]))
         if t in XY_SEND:
             send, moved[t + 1][0], moved[t + 1][1] = lax.optimization_barrier(
                 (send, moved[t + 1][0], moved[t + 1][1])

time: 201 us -> 198 us (0.985)
  waiting for transfers between devices: 67.3 us -> 64.2 us
    ppermute x28, waiting for transfers between devices: 67.3 us -> 64.2 us  [move(): return lax.ppermute(value, AXES, pairs(target))]
    unnamed x37 -> x33, local copies, waits for them, and re-layouts: 13.9 us -> 12.4 us
  transfers between devices with their start and end apart: 28 -> 28, of which waited for: 12 -> 11; matrix products, arithmetic and copies ran while one was open for 5% -> 5% of each run, Pallas kernels for 38% -> 39%
where the time goes in v5:
time: 198 us; the launch traced here: 196 us
  Pallas kernels  78.2 us (39%)
  waiting for transfers between devices  64.2 us (32%)
  starting transfers between devices  29.5 us (15%)
  local copies, waits for them, and re-layouts  18.5 us (9%)
  other arithmetic  3.79 us (2%)
    ppermute x28, waiting for transfers between devices, move(): return lax.ppermute(value, AXES, pairs(target))  64.2 us
    pallas_call x3, Pallas kernels, contract(): pl.pallas_call(functools.partial(last_kernel, cuts, scale) if last else f...  49.5 us
    ppermute x28, starting transfers between devices, move(): return lax.ppermute(value, AXES, pairs(target))  29.5 us
    pallas_call x3, Pallas kernels, gram_chunk(): pl.pallas_call(functools.partial(gram_kernel, len(blocks) - 3), in_specs=...  26.4 us
    unnamed x33, local copies, waits for them, and re-layouts  12.4 us
  transfers between devices with their start and end apart: 28, of which 11 were waited for; matrix products, arithmetic and copies ran while one was open for 5% of the time, Pallas kernels for 39%

profile of v5, /device:TPU:8, one launch (start us, length us, event | category | flops | bytes accessed | tf_op | source)
XLA Modules:
  0.0 195.8 jit_solution(2470571577601688211)
XLA Ops:
  0.6 1.6 collective-permute-start.6
  4.2 14.7 %contract.3.refs_0_.own_ref = bf16[2,112,2048]{2,1,0:T(8,128)(2,1)} custom-call(bf16[2,7,56,2048]{3,2,1,0:T(8,128)(2,1)} %bitcast.31, bf16[56,56,2048]{2,1,0:T(8,128)(2,1)} %q_ref.3), custom_call_target="tpu_custom_call" | custom-call | flops 30000001024 | bytes 1000 | tf_op jit(solution)/shard_map/contract/pallas_call | solution.py:105
  21.9 19.2 %contract.4.refs_1_.own_ref = bf16[2,168,2048]{2,1,0:T(8,128)(2,1)S(1)} custom-call(bf16[2,7,56,2048]{3,2,1,0:T(8,128)(2,1)} %bitcast.32, bf16[56,56,2048]{2,1,0:T(8,128)(2,1)} %q_ref.3), custom_call_target="tpu_custom_call" | custom-call | flops 30000001024 | bytes 1000 | tf_op jit(solution)/shard_map/contract/pallas_call | solution.py:105
  42.2 1.6 collective-permute-start.5
  43.8 15.7 %contract.5 = (bf16[2,112,2048]{2,1,0:T(8,128)(2,1)}, bf16[2,392,2048]{2,1,0:T(8,128)(2,1)}) custom-call(bf16[2,7,56,2048]{3,2,1,0:T(8,128)(2,1)} %bitcast.33, bf16[56,56,2048]{2,1,0:T(8,128)(2,1)} %q_ref.3, bf16[2,112,2048]{2,1,0:T(8,128)(2,1)} %contract.3.refs_0_.own_ref, bf16[2,168,2048]{2,1,0:T(8,128)(2,1)} %copy-done), custom_call_target="tpu_custom_call" | custom-call | flops 30000001024 | bytes 1000 | tf_op jit(solution)/shard_map/contract/pallas_call | solution.py:105
  64.3 10.0 %collective-permute-done.x_ref = bf16[2,168,2048]{2,1,0:T(8,128)(2,1)S(1)} collective-permute-done((bf16[2,168,2048]{2,1,0:T(8,128)(2,1)S(1)}, bf16[2,168,2048]{2,1,0:T(8,128)(2,1)S(1)}, u32[]{:S(2)}, u32[]{:S(2)}) %collective-permute-start) | collective-permute-done | bytes 1376288 | tf_op jit(solution)/shard_map/ppermute | solution.py:204
  77.1 1.9 fusion.1
  79.1 15.5 %collective-permute-done.5.refs_0_ = bf16[2,112,2048]{2,1,0:T(8,128)(2,1)} collective-permute-done((bf16[2,112,2048]{2,1,0:T(8,128)(2,1)}, bf16[2,112,2048]{2,1,0:T(8,128)(2,1)}, u32[]{:S(2)}, u32[]{:S(2)}) %collective-permute-start.5) | collective-permute-done | bytes 917536 | tf_op jit(solution)/shard_map/ppermute | solution.py:204
  94.6 1.9 copy-done.4
  96.5 8.0 %gram.3 = (bf16[4,112,784]{2,1,0:T(8,128)(2,1)S(1)}, bf16[4,112,784]{2,1,0:T(8,128)(2,1)S(1)}, f32[56,2048]{1,0:T(8,128)S(1)}) custom-call(s32[1]{0:T(128)} %bitcast.3.core_ref, bf16[2,112,2048]{2,1,0:T(8,128)(2,1)} %contract.3.refs_0_.own_ref, bf16[2,112,2048]{2,1,0:T(8,128)(2,1)} %collective-permute-done.3.x_ref, ...), custom_call_target="tpu_custom_call" | custom-call | flops 4000000000 | bytes 1000 | tf_op jit(solution)/shard_map/gram/pallas_call | solution.py:161
  105.3 6.1 %collective-permute-done.14.y_ref = bf16[2,112,2048]{2,1,0:T(8,128)(2,1)} collective-permute-done((bf16[2,112,2048]{2,1,0:T(8,128)(2,1)}, bf16[2,112,2048]{2,1,0:T(8,128)(2,1)}, u32[]{:S(2)}, u32[]{:S(2)}) %collective-permute-start.14) | collective-permute-done | bytes 917536 | tf_op jit(solution)/shard_map/ppermute | solution.py:204
  114.8 2.6 %collective-permute-start.11 = (bf16[112,784]{1,0:T(8,128)(2,1)S(1)}, bf16[112,784]{1,0:T(8,128)(2,1)S(1)}, u32[]{:S(2)}, u32[]{:S(2)}) collective-permute-start(bf16[112,784]{1,0:T(8,128)(2,1)S(1)} %get-tuple-element.82), channel_id=1, source_target_pairs={{0,4},{1,5},{2,6},{3,7},{4,0},{5,1},{6,2},{7,3},{8,12},{9,13},{10,... | collective-permute-start | bytes 526856 | tf_op jit(solution)/shard_map/ppermute | solution.py:204
  117.8 3.1 %collective-permute-done.2.refs_0_ = bf16[2,168,2048]{2,1,0:T(8,128)(2,1)} collective-permute-done((bf16[2,168,2048]{2,1,0:T(8,128)(2,1)}, bf16[2,168,2048]{2,1,0:T(8,128)(2,1)}, u32[]{:S(2)}, u32[]{:S(2)}) %collective-permute-start.2) | collective-permute-done | bytes 1376288 | tf_op jit(solution)/shard_map/ppermute | solution.py:204
  122.3 1.9 copy-done.5
  125.2 10.1 %gram.4 = (bf16[4,168,784]{2,1,0:T(8,128)(2,1)S(1)}, bf16[4,168,784]{2,1,0:T(8,128)(2,1)}, f32[56,2048]{1,0:T(8,128)S(1)}) custom-call(s32[1]{0:T(128)} %bitcast.3.core_ref, bf16[2,168,2048]{2,1,0:T(8,128)(2,1)S(1)} %copy-done.1, bf16[2,168,2048]{2,1,0:T(8,128)(2,1)S(1)} %copy-done.3, bf16[2,168,2048]{2,1,0:T(8,128)(2,1)} %collective-permute-done.1.y_ref, ...), custom_call_target="tpu_custom_call" | custom-call | flops 4000000000 | bytes 1000 | tf_op jit(solution)/shard_map/gram/pallas_call | solution.py:161
  136.8 3.0 %collective-permute-done.16.recv_ref = bf16[4,168,784]{2,1,0:T(8,128)(2,1)S(1)} collective-permute-done((bf16[4,168,784]{2,1,0:T(8,128)(2,1)}, bf16[4,168,784]{2,1,0:T(8,128)(2,1)S(1)}, u32[]{:S(2)}, u32[]{:S(2)}) %collective-permute-start.16) | collective-permute-done | bytes 1053728 | tf_op jit(solution)/shard_map/ppermute | solution.py:204
  141.2 2.6 %collective-permute-start.18 = (bf16[168,784]{1,0:T(8,128)(2,1)S(1)}, bf16[168,784]{1,0:T(8,128)(2,1)S(1)}, u32[]{:S(2)}, u32[]{:S(2)}) collective-permute-start(bf16[168,784]{1,0:T(8,128)(2,1)S(1)} %get-tuple-element.102), channel_id=1, source_target_pairs={{0,4},{1,5},{2,6},{3,7},{4,0},{5,1},{6,2},{7,3},{8,12},{9,13},{10,... | collective-permute-start | bytes 790280 | tf_op jit(solution)/shard_map/ppermute | solution.py:204
  143.8 1.9 copy-done.6
  145.7 8.2 %gram.5 = (bf16[4,112,784]{2,1,0:T(8,128)(2,1)S(1)}, bf16[4,112,784]{2,1,0:T(8,128)(2,1)S(1)}, f32[56,2048]{1,0:T(8,128)S(1)}) custom-call(s32[1]{0:T(128)} %bitcast.3.core_ref, bf16[2,112,2048]{2,1,0:T(8,128)(2,1)} %get-tuple-element.88.own_ref, bf16[2,112,2048]{2,1,0:T(8,128)(2,1)} %collective-permute-done.13.x_ref, ...), custom_call_target="tpu_custom_call" | custom-call | flops 4000000000 | bytes 1000 | tf_op jit(solution)/shard_map/gram/pallas_call | solution.py:161
  154.2 3.3 %collective-permute-done.18 = bf16[168,784]{1,0:T(8,128)(2,1)S(1)} collective-permute-done((bf16[168,784]{1,0:T(8,128)(2,1)S(1)}, bf16[168,784]{1,0:T(8,128)(2,1)S(1)}, u32[]{:S(2)}, u32[]{:S(2)}) %collective-permute-start.18) | collective-permute-done | bytes 263456 | tf_op jit(solution)/shard_map/ppermute | solution.py:204
  161.6 3.4 %collective-permute-start.22 = (bf16[112,784]{1,0:T(8,128)(2,1)S(1)}, bf16[112,784]{1,0:T(8,128)(2,1)S(1)}, u32[]{:S(2)}, u32[]{:S(2)}) collective-permute-start(bf16[112,784]{1,0:T(8,128)(2,1)S(1)} %get-tuple-element.109), channel_id=1, source_target_pairs={{0,2},{1,3},{2,0},{3,1},{4,6},{5,7},{6,4},{7,5},{8,10},{9,11},{10,... | collective-permute-start | bytes 526856 | tf_op jit(solution)/shard_map/ppermute | solution.py:204
  166.6 17.9 %collective-permute-done.19 = bf16[168,784]{1,0:T(8,128)(2,1)S(1)} collective-permute-done((bf16[168,784]{1,0:T(8,128)(2,1)S(1)}, bf16[168,784]{1,0:T(8,128)(2,1)S(1)}, u32[]{:S(2)}, u32[]{:S(2)}) %collective-permute-start.19) | collective-permute-done | bytes 263456 | tf_op jit(solution)/shard_map/ppermute | solution.py:204
  185.8 2.5 %collective-permute-start.27 = (f32[8,128]{1,0:T(8,128)S(1)}, f32[8,128]{1,0:T(8,128)S(1)}, u32[]{:S(2)}, u32[]{:S(2)}) collective-permute-start(f32[8,128]{1,0:T(8,128)S(1)} %broadcast_add_fusion), channel_id=1, source_target_pairs={{0,6},{1,7},{2,4},{3,5},{4,2},{5,3},{6,0},{7,1},{8,14},{9,15},{10,... | collective-permute-start | bytes 12296 | tf_op jit(solution)/shard_map/ppermute | solution.py:204
  188.3 4.2 %collective-permute-done.24 = bf16[112,784]{1,0:T(8,128)(2,1)S(1)} collective-permute-done((bf16[112,784]{1,0:T(8,128)(2,1)S(1)}, bf16[112,784]{1,0:T(8,128)(2,1)S(1)}, u32[]{:S(2)}, u32[]{:S(2)}) %collective-permute-start.24) | collective-permute-done | bytes 175648 | tf_op jit(solution)/shard_map/ppermute | solution.py:204
  (95 shorter events, 33.6 us)
Async XLA Ops:
  0.6 40.4 %collective-permute-start.6 = (bf16[784,56]{0,1:T(8,128)(2,1)}, bf16[784,56]{0,1:T(8,128)(2,1)S(1)}, u32[]{:S(2)}, u32[]{:S(2)}) collective-permute-start(bf16[784,56]{0,1:T(8,128)(2,1)} %param.5), channel_id=1, source_target_pairs={{0,8},{1,9},{2,10},{3,11},{4,12},{5,13},{6,14},{7,15},{8,0},{9,1},... | collective-permute-start | bytes 263432 | tf_op jit(solution)/shard_map/ppermute | solution.py:204
  2.2 39.5 %collective-permute-start.7 = (bf16[784,56]{0,1:T(8,128)(2,1)}, bf16[784,56]{0,1:T(8,128)(2,1)S(1)}, u32[]{:S(2)}, u32[]{:S(2)}) collective-permute-start(bf16[784,56]{0,1:T(8,128)(2,1)} %param.5), channel_id=1, source_target_pairs={{0,16},{1,17},{2,18},{3,19},{4,20},{5,21},{6,22},{7,23},{8,24},{9,... | collective-permute-start | bytes 263432 | tf_op jit(solution)/shard_map/ppermute | solution.py:204
  3.7 38.5 %collective-permute-start.8 = (bf16[784,56]{0,1:T(8,128)(2,1)}, bf16[784,56]{0,1:T(8,128)(2,1)S(1)}, u32[]{:S(2)}, u32[]{:S(2)}) collective-permute-start(bf16[784,56]{0,1:T(8,128)(2,1)} %param.5), channel_id=1, source_target_pairs={{0,24},{1,25},{2,26},{3,27},{4,28},{5,29},{6,30},{7,31},{8,16},{9,... | collective-permute-start | bytes 263432 | tf_op jit(solution)/shard_map/ppermute | solution.py:204
  18.9 23.4 %collective-permute-start.3 = (bf16[2,112,2048]{2,1,0:T(8,128)(2,1)}, bf16[2,112,2048]{2,1,0:T(8,128)(2,1)}, u32[]{:S(2)}, u32[]{:S(2)}) collective-permute-start(bf16[2,112,2048]{2,1,0:T(8,128)(2,1)} %contract.3.refs_0_.own_ref), channel_id=1, source_target_pairs={{0,8},{1,9},{2,10},{3,11},{4,12},{5,13},{6,14},{7,15},{8,0},{9,1},... | collective-permute-start | bytes 2752520 | tf_op jit(solution)/shard_map/ppermute | solution.py:204
  20.3 21.9 %collective-permute-start.4 = (bf16[2,112,2048]{2,1,0:T(8,128)(2,1)}, bf16[2,112,2048]{2,1,0:T(8,128)(2,1)}, u32[]{:S(2)}, u32[]{:S(2)}) collective-permute-start(bf16[2,112,2048]{2,1,0:T(8,128)(2,1)} %contract.3.refs_0_.own_ref), channel_id=1, source_target_pairs={{0,16},{1,17},{2,18},{3,19},{4,20},{5,21},{6,22},{7,23},{8,24},{9,... | collective-permute-start | bytes 2752520 | tf_op jit(solution)/shard_map/ppermute | solution.py:204
  41.1 33.2 %collective-permute-start = (bf16[2,168,2048]{2,1,0:T(8,128)(2,1)S(1)}, bf16[2,168,2048]{2,1,0:T(8,128)(2,1)S(1)}, u32[]{:S(2)}, u32[]{:S(2)}) collective-permute-start(bf16[2,168,2048]{2,1,0:T(8,128)(2,1)S(1)} %contract.4.refs_1_.own_ref), channel_id=1, source_target_pairs={{0,8},{1,9},{2,10},{3,11},{4,12},{5,13},{6,14},{7,15},{8,0},{9,1},... | collective-permute-start | bytes 4128776 | tf_op jit(solution)/shard_map/ppermute | solution.py:204
  41.7 33.2 %collective-permute-start.1 = (bf16[2,168,2048]{2,1,0:T(8,128)(2,1)S(1)}, bf16[2,168,2048]{2,1,0:T(8,128)(2,1)}, u32[]{:S(2)}, u32[]{:S(2)}) collective-permute-start(bf16[2,168,2048]{2,1,0:T(8,128)(2,1)S(1)} %contract.4.refs_1_.own_ref), channel_id=1, source_target_pairs={{0,16},{1,17},{2,18},{3,19},{4,20},{5,21},{6,22},{7,23},{8,24},{9,... | collective-permute-start | bytes 4128776 | tf_op jit(solution)/shard_map/ppermute | solution.py:204
  42.2 52.4 %collective-permute-start.5 = (bf16[2,112,2048]{2,1,0:T(8,128)(2,1)}, bf16[2,112,2048]{2,1,0:T(8,128)(2,1)}, u32[]{:S(2)}, u32[]{:S(2)}) collective-permute-start(bf16[2,112,2048]{2,1,0:T(8,128)(2,1)} %collective-permute-done.3.x_ref), channel_id=1, source_target_pairs={{0,16},{1,17},{2,18},{3,19},{4,20},{5,21},{6,22},{7,23},{8,24},{9,... | collective-permute-start | bytes 2752520 | tf_op jit(solution)/shard_map/ppermute | solution.py:204
  59.5 45.8 %collective-permute-start.13 = (bf16[2,112,2048]{2,1,0:T(8,128)(2,1)}, bf16[2,112,2048]{2,1,0:T(8,128)(2,1)}, u32[]{:S(2)}, u32[]{:S(2)}) collective-permute-start(bf16[2,112,2048]{2,1,0:T(8,128)(2,1)} %get-tuple-element.88.own_ref), channel_id=1, source_target_pairs={{0,8},{1,9},{2,10},{3,11},{4,12},{5,13},{6,14},{7,15},{8,0},{9,1},... | collective-permute-start | bytes 2752520 | tf_op jit(solution)/shard_map/ppermute | solution.py:204
  61.0 50.4 %collective-permute-start.14 = (bf16[2,112,2048]{2,1,0:T(8,128)(2,1)}, bf16[2,112,2048]{2,1,0:T(8,128)(2,1)}, u32[]{:S(2)}, u32[]{:S(2)}) collective-permute-start(bf16[2,112,2048]{2,1,0:T(8,128)(2,1)} %get-tuple-element.88.own_ref), channel_id=1, source_target_pairs={{0,16},{1,17},{2,18},{3,19},{4,20},{5,21},{6,22},{7,23},{8,24},{9,... | collective-permute-start | bytes 2752520 | tf_op jit(solution)/shard_map/ppermute | solution.py:204
  74.9 46.0 %collective-permute-start.2 = (bf16[2,168,2048]{2,1,0:T(8,128)(2,1)}, bf16[2,168,2048]{2,1,0:T(8,128)(2,1)}, u32[]{:S(2)}, u32[]{:S(2)}) collective-permute-start(bf16[2,168,2048]{2,1,0:T(8,128)(2,1)} %collective-permute-done.1.y_ref), channel_id=1, source_target_pairs={{0,8},{1,9},{2,10},{3,11},{4,12},{5,13},{6,14},{7,15},{8,0},{9,1},... | collective-permute-start | bytes 4128776 | tf_op jit(solution)/shard_map/ppermute | solution.py:204
  105.3 8.3 %collective-permute-start.9 = (bf16[4,112,784]{2,1,0:T(8,128)(2,1)S(1)}, bf16[4,112,784]{2,1,0:T(8,128)(2,1)S(1)}, u32[]{:S(2)}, u32[]{:S(2)}) collective-permute-start(bf16[4,112,784]{2,1,0:T(8,128)(2,1)S(1)} %get-tuple-element.72), channel_id=1, source_target_pairs={{0,1},{1,0},{2,3},{3,2},{4,5},{5,4},{6,7},{7,6},{8,9},{9,8},{10,11... | collective-permute-start | bytes 2107400 | tf_op jit(solution)/shard_map/ppermute | solution.py:204
  111.4 25.4 %collective-permute-start.15 = (bf16[2,112,2048]{2,1,0:T(8,128)(2,1)}, bf16[2,112,2048]{2,1,0:T(8,128)(2,1)}, u32[]{:S(2)}, u32[]{:S(2)}) collective-permute-start(bf16[2,112,2048]{2,1,0:T(8,128)(2,1)} %collective-permute-done.13.x_ref), channel_id=1, source_target_pairs={{0,16},{1,17},{2,18},{3,19},{4,20},{5,21},{6,22},{7,23},{8,24},{9,... | collective-permute-start | bytes 2752520 | tf_op jit(solution)/shard_map/ppermute | solution.py:204
  114.3 21.0 %collective-permute-start.10 = (bf16[112,784]{1,0:T(8,128)(2,1)S(1)}, bf16[112,784]{1,0:T(8,128)(2,1)S(1)}, u32[]{:S(2)}, u32[]{:S(2)}) collective-permute-start(bf16[112,784]{1,0:T(8,128)(2,1)S(1)} %get-tuple-element.79), channel_id=1, source_target_pairs={{0,2},{1,3},{2,0},{3,1},{4,6},{5,7},{6,4},{7,5},{8,10},{9,11},{10,... | collective-permute-start | bytes 526856 | tf_op jit(solution)/shard_map/ppermute | solution.py:204
  114.8 20.5 %collective-permute-start.11 = (bf16[112,784]{1,0:T(8,128)(2,1)S(1)}, bf16[112,784]{1,0:T(8,128)(2,1)S(1)}, u32[]{:S(2)}, u32[]{:S(2)}) collective-permute-start(bf16[112,784]{1,0:T(8,128)(2,1)S(1)} %get-tuple-element.82), channel_id=1, source_target_pairs={{0,4},{1,5},{2,6},{3,7},{4,0},{5,1},{6,2},{7,3},{8,12},{9,13},{10,... | collective-permute-start | bytes 526856 | tf_op jit(solution)/shard_map/ppermute | solution.py:204
  117.4 17.9 %collective-permute-start.12 = (bf16[112,784]{1,0:T(8,128)(2,1)S(1)}, bf16[112,784]{1,0:T(8,128)(2,1)S(1)}, u32[]{:S(2)}, u32[]{:S(2)}) collective-permute-start(bf16[112,784]{1,0:T(8,128)(2,1)S(1)} %get-tuple-element.85), channel_id=1, source_target_pairs={{0,6},{1,7},{2,4},{3,5},{4,2},{5,3},{6,0},{7,1},{8,14},{9,15},{10,... | collective-permute-start | bytes 526856 | tf_op jit(solution)/shard_map/ppermute | solution.py:204
  140.6 13.6 %collective-permute-start.17 = (bf16[168,784]{1,0:T(8,128)(2,1)S(1)}, bf16[168,784]{1,0:T(8,128)(2,1)S(1)}, u32[]{:S(2)}, u32[]{:S(2)}) collective-permute-start(bf16[168,784]{1,0:T(8,128)(2,1)S(1)} %get-tuple-element.99), channel_id=1, source_target_pairs={{0,2},{1,3},{2,0},{3,1},{4,6},{5,7},{6,4},{7,5},{8,10},{9,11},{10,... | collective-permute-start | bytes 790280 | tf_op jit(solution)/shard_map/ppermute | solution.py:204
  141.2 16.3 %collective-permute-start.18 = (bf16[168,784]{1,0:T(8,128)(2,1)S(1)}, bf16[168,784]{1,0:T(8,128)(2,1)S(1)}, u32[]{:S(2)}, u32[]{:S(2)}) collective-permute-start(bf16[168,784]{1,0:T(8,128)(2,1)S(1)} %get-tuple-element.102), channel_id=1, source_target_pairs={{0,4},{1,5},{2,6},{3,7},{4,0},{5,1},{6,2},{7,3},{8,12},{9,13},{10,... | collective-permute-start | bytes 790280 | tf_op jit(solution)/shard_map/ppermute | solution.py:204
  159.4 25.1 %collective-permute-start.19 = (bf16[168,784]{1,0:T(8,128)(2,1)S(1)}, bf16[168,784]{1,0:T(8,128)(2,1)S(1)}, u32[]{:S(2)}, u32[]{:S(2)}) collective-permute-start(bf16[168,784]{1,0:T(8,128)(2,1)S(1)} %get-tuple-element.104), channel_id=1, source_target_pairs={{0,6},{1,7},{2,4},{3,5},{4,2},{5,3},{6,0},{7,1},{8,14},{9,15},{10,... | collective-permute-start | bytes 790280 | tf_op jit(solution)/shard_map/ppermute | solution.py:204
  161.6 23.1 %collective-permute-start.22 = (bf16[112,784]{1,0:T(8,128)(2,1)S(1)}, bf16[112,784]{1,0:T(8,128)(2,1)S(1)}, u32[]{:S(2)}, u32[]{:S(2)}) collective-permute-start(bf16[112,784]{1,0:T(8,128)(2,1)S(1)} %get-tuple-element.109), channel_id=1, source_target_pairs={{0,2},{1,3},{2,0},{3,1},{4,6},{5,7},{6,4},{7,5},{8,10},{9,11},{10,... | collective-permute-start | bytes 526856 | tf_op jit(solution)/shard_map/ppermute | solution.py:204
  165.1 23.2 %collective-permute-start.23 = (bf16[112,784]{1,0:T(8,128)(2,1)S(1)}, bf16[112,784]{1,0:T(8,128)(2,1)S(1)}, u32[]{:S(2)}, u32[]{:S(2)}) collective-permute-start(bf16[112,784]{1,0:T(8,128)(2,1)S(1)} %get-tuple-element.111), channel_id=1, source_target_pairs={{0,4},{1,5},{2,6},{3,7},{4,0},{5,1},{6,2},{7,3},{8,12},{9,13},{10,... | collective-permute-start | bytes 526856 | tf_op jit(solution)/shard_map/ppermute | solution.py:204
  165.1 27.4 %collective-permute-start.24 = (bf16[112,784]{1,0:T(8,128)(2,1)S(1)}, bf16[112,784]{1,0:T(8,128)(2,1)S(1)}, u32[]{:S(2)}, u32[]{:S(2)}) collective-permute-start(bf16[112,784]{1,0:T(8,128)(2,1)S(1)} %get-tuple-element.112), channel_id=1, source_target_pairs={{0,6},{1,7},{2,4},{3,5},{4,2},{5,3},{6,0},{7,1},{8,14},{9,15},{10,... | collective-permute-start | bytes 526856 | tf_op jit(solution)/shard_map/ppermute | solution.py:204
  184.7 9.0 %collective-permute-start.25 = (f32[8,128]{1,0:T(8,128)S(1)}, f32[8,128]{1,0:T(8,128)S(1)}, u32[]{:S(2)}, u32[]{:S(2)}) collective-permute-start(f32[8,128]{1,0:T(8,128)S(1)} %broadcast_add_fusion), channel_id=1, source_target_pairs={{0,2},{1,3},{2,0},{3,1},{4,6},{5,7},{6,4},{7,5},{8,10},{9,11},{10,... | collective-permute-start | bytes 12296 | tf_op jit(solution)/shard_map/ppermute | solution.py:204
  184.8 9.0 %collective-permute-start.26 = (f32[8,128]{1,0:T(8,128)S(1)}, f32[8,128]{1,0:T(8,128)S(1)}, u32[]{:S(2)}, u32[]{:S(2)}) collective-permute-start(f32[8,128]{1,0:T(8,128)S(1)} %broadcast_add_fusion), channel_id=1, source_target_pairs={{0,4},{1,5},{2,6},{3,7},{4,0},{5,1},{6,2},{7,3},{8,12},{9,13},{10,... | collective-permute-start | bytes 12296 | tf_op jit(solution)/shard_map/ppermute | solution.py:204
  (19 other events, 126.8 us)

commit v6 on v5

--- a/solution.py
+++ b/solution.py
@@ -19,7 +19,7 @@
 Z_PARTS = {1: (1, 2, 3), 2: (1, 2)}
 XY_SEND = ()
 D_SEND = (1,)
-GATE = True
+GATE = False
 MAPS_AT = 1
 LAST_VMEM = 52
 TIE = False

time: 198 us -> 197 us (level)
  local copies, waits for them, and re-layouts: 18.5 us -> 15.8 us
  waiting for transfers between devices: 64.2 us -> 66.6 us
    ppermute x28, waiting for transfers between devices: 64.2 us -> 66.6 us  [move(): return lax.ppermute(value, AXES, pairs(target))]
    unnamed x33 -> x37, local copies, waits for them, and re-layouts: 12.4 us -> 10.5 us
  transfers between devices with their start and end apart: 28 -> 28, of which waited for: 11 -> 11; matrix products, arithmetic and copies ran while one was open for 5% -> 4% of each run, Pallas kernels for 39% -> 40%
where the time goes in v6:
time: 197 us; the launch traced here: 196 us
  Pallas kernels  78.3 us (40%)
  waiting for transfers between devices  66.6 us (34%)
  starting transfers between devices  28.8 us (15%)
  local copies, waits for them, and re-layouts  15.8 us (8%)
  other arithmetic  4.44 us (2%)
    ppermute x28, waiting for transfers between devices, move(): return lax.ppermute(value, AXES, pairs(target))  66.6 us
    pallas_call x3, Pallas kernels, contract(): pl.pallas_call(functools.partial(last_kernel, cuts, scale) if last else f...  49.5 us
    ppermute x28, starting transfers between devices, move(): return lax.ppermute(value, AXES, pairs(target))  28.8 us
    pallas_call x3, Pallas kernels, gram_chunk(): pl.pallas_call(functools.partial(gram_kernel, len(blocks) - 3), in_specs=...  26.5 us
    unnamed x37, local copies, waits for them, and re-layouts  10.5 us
  transfers between devices with their start and end apart: 28, of which 11 were waited for; matrix products, arithmetic and copies ran while one was open for 4% of the time, Pallas kernels for 40%

profile of v6, /device:TPU:8, one launch (start us, length us, event | category | flops | bytes accessed | tf_op | source)
XLA Modules:
  0.0 195.5 jit_solution(2025758351563651455)
XLA Ops:
  4.2 14.7 %contract.3.refs_0_.own_ref = bf16[2,112,2048]{2,1,0:T(8,128)(2,1)} custom-call(bf16[2,7,56,2048]{3,2,1,0:T(8,128)(2,1)} %bitcast.31, bf16[56,56,2048]{2,1,0:T(8,128)(2,1)} %q_ref.3), custom_call_target="tpu_custom_call" | custom-call | flops 30000001024 | bytes 1000 | tf_op jit(solution)/shard_map/contract/pallas_call | solution.py:105
  21.9 19.2 %contract.4.refs_1_.own_ref = bf16[2,168,2048]{2,1,0:T(8,128)(2,1)S(1)} custom-call(bf16[2,7,56,2048]{3,2,1,0:T(8,128)(2,1)} %bitcast.32, bf16[56,56,2048]{2,1,0:T(8,128)(2,1)} %q_ref.3), custom_call_target="tpu_custom_call" | custom-call | flops 30000001024 | bytes 1000 | tf_op jit(solution)/shard_map/contract/pallas_call | solution.py:105
  42.2 1.6 collective-permute-start.5
  43.8 15.7 %contract.5 = (bf16[2,112,2048]{2,1,0:T(8,128)(2,1)}, bf16[2,392,2048]{2,1,0:T(8,128)(2,1)}) custom-call(bf16[2,7,56,2048]{3,2,1,0:T(8,128)(2,1)} %bitcast.33, bf16[56,56,2048]{2,1,0:T(8,128)(2,1)} %q_ref.3, bf16[2,112,2048]{2,1,0:T(8,128)(2,1)} %contract.3.refs_0_.own_ref, bf16[2,168,2048]{2,1,0:T(8,128)(2,1)} %copy-done), custom_call_target="tpu_custom_call" | custom-call | flops 30000001024 | bytes 1000 | tf_op jit(solution)/shard_map/contract/pallas_call | solution.py:105
  63.3 11.0 %collective-permute-done.x_ref = bf16[2,168,2048]{2,1,0:T(8,128)(2,1)S(1)} collective-permute-done((bf16[2,168,2048]{2,1,0:T(8,128)(2,1)S(1)}, bf16[2,168,2048]{2,1,0:T(8,128)(2,1)S(1)}, u32[]{:S(2)}, u32[]{:S(2)}) %collective-permute-start) | collective-permute-done | bytes 1376288 | tf_op jit(solution)/shard_map/ppermute | solution.py:204
  77.5 17.1 %collective-permute-done.5.refs_0_ = bf16[2,112,2048]{2,1,0:T(8,128)(2,1)} collective-permute-done((bf16[2,112,2048]{2,1,0:T(8,128)(2,1)}, bf16[2,112,2048]{2,1,0:T(8,128)(2,1)}, u32[]{:S(2)}, u32[]{:S(2)}) %collective-permute-start.5) | collective-permute-done | bytes 917536 | tf_op jit(solution)/shard_map/ppermute | solution.py:204
  94.6 1.9 copy-done.4
  96.5 8.0 %gram.3 = (bf16[4,112,784]{2,1,0:T(8,128)(2,1)S(1)}, bf16[4,112,784]{2,1,0:T(8,128)(2,1)S(1)}, f32[56,2048]{1,0:T(8,128)S(1)}) custom-call(s32[1]{0:T(128)} %bitcast.3.core_ref, bf16[2,112,2048]{2,1,0:T(8,128)(2,1)} %contract.3.refs_0_.own_ref, bf16[2,112,2048]{2,1,0:T(8,128)(2,1)} %collective-permute-done.3.x_ref, ...), custom_call_target="tpu_custom_call" | custom-call | flops 4000000000 | bytes 1000 | tf_op jit(solution)/shard_map/gram/pallas_call | solution.py:161
  105.3 6.1 %collective-permute-done.14.y_ref = bf16[2,112,2048]{2,1,0:T(8,128)(2,1)} collective-permute-done((bf16[2,112,2048]{2,1,0:T(8,128)(2,1)}, bf16[2,112,2048]{2,1,0:T(8,128)(2,1)}, u32[]{:S(2)}, u32[]{:S(2)}) %collective-permute-start.14) | collective-permute-done | bytes 917536 | tf_op jit(solution)/shard_map/ppermute | solution.py:204
  114.8 2.6 %collective-permute-start.11 = (bf16[112,784]{1,0:T(8,128)(2,1)S(1)}, bf16[112,784]{1,0:T(8,128)(2,1)S(1)}, u32[]{:S(2)}, u32[]{:S(2)}) collective-permute-start(bf16[112,784]{1,0:T(8,128)(2,1)S(1)} %get-tuple-element.80), channel_id=1, source_target_pairs={{0,4},{1,5},{2,6},{3,7},{4,0},{5,1},{6,2},{7,3},{8,12},{9,13},{10,... | collective-permute-start | bytes 526856 | tf_op jit(solution)/shard_map/ppermute | solution.py:204
  117.9 3.1 %collective-permute-done.2.refs_0_ = bf16[2,168,2048]{2,1,0:T(8,128)(2,1)} collective-permute-done((bf16[2,168,2048]{2,1,0:T(8,128)(2,1)}, bf16[2,168,2048]{2,1,0:T(8,128)(2,1)}, u32[]{:S(2)}, u32[]{:S(2)}) %collective-permute-start.2) | collective-permute-done | bytes 1376288 | tf_op jit(solution)/shard_map/ppermute | solution.py:204
  122.3 1.9 copy-done.5
  125.2 10.2 %gram.4 = (bf16[4,168,784]{2,1,0:T(8,128)(2,1)S(1)}, bf16[4,168,784]{2,1,0:T(8,128)(2,1)}, f32[56,2048]{1,0:T(8,128)S(1)}) custom-call(s32[1]{0:T(128)} %bitcast.3.core_ref, bf16[2,168,2048]{2,1,0:T(8,128)(2,1)S(1)} %copy-done.1, bf16[2,168,2048]{2,1,0:T(8,128)(2,1)S(1)} %copy-done.3, bf16[2,168,2048]{2,1,0:T(8,128)(2,1)} %collective-permute-done.1.y_ref, ...), custom_call_target="tpu_custom_call" | custom-call | flops 4000000000 | bytes 1000 | tf_op jit(solution)/shard_map/gram/pallas_call | solution.py:161
  136.9 3.0 %collective-permute-done.16.recv_ref = bf16[4,168,784]{2,1,0:T(8,128)(2,1)S(1)} collective-permute-done((bf16[4,168,784]{2,1,0:T(8,128)(2,1)}, bf16[4,168,784]{2,1,0:T(8,128)(2,1)S(1)}, u32[]{:S(2)}, u32[]{:S(2)}) %collective-permute-start.16) | collective-permute-done | bytes 1053728 | tf_op jit(solution)/shard_map/ppermute | solution.py:204
  141.3 2.6 %collective-permute-start.18 = (bf16[168,784]{1,0:T(8,128)(2,1)S(1)}, bf16[168,784]{1,0:T(8,128)(2,1)S(1)}, u32[]{:S(2)}, u32[]{:S(2)}) collective-permute-start(bf16[168,784]{1,0:T(8,128)(2,1)S(1)} %get-tuple-element.100), channel_id=1, source_target_pairs={{0,4},{1,5},{2,6},{3,7},{4,0},{5,1},{6,2},{7,3},{8,12},{9,13},{10,... | collective-permute-start | bytes 790280 | tf_op jit(solution)/shard_map/ppermute | solution.py:204
  143.8 1.9 copy-done.6
  145.8 8.3 %gram.5 = (bf16[4,112,784]{2,1,0:T(8,128)(2,1)S(1)}, bf16[4,112,784]{2,1,0:T(8,128)(2,1)S(1)}, f32[56,2048]{1,0:T(8,128)S(1)}) custom-call(s32[1]{0:T(128)} %bitcast.3.core_ref, bf16[2,112,2048]{2,1,0:T(8,128)(2,1)} %get-tuple-element.86.own_ref, bf16[2,112,2048]{2,1,0:T(8,128)(2,1)} %collective-permute-done.13.x_ref, ...), custom_call_target="tpu_custom_call" | custom-call | flops 4000000000 | bytes 1000 | tf_op jit(solution)/shard_map/gram/pallas_call | solution.py:161
  157.3 1.6 collective-permute-start.25
  161.5 1.9 collective-permute-done.26
  166.9 1.7 collective-permute-start.21
  168.6 2.4 %collective-permute-start.22 = (bf16[112,784]{1,0:T(8,128)(2,1)S(1)}, bf16[112,784]{1,0:T(8,128)(2,1)S(1)}, u32[]{:S(2)}, u32[]{:S(2)}) collective-permute-start(bf16[112,784]{1,0:T(8,128)(2,1)S(1)} %get-tuple-element.107), channel_id=1, source_target_pairs={{0,4},{1,5},{2,6},{3,7},{4,0},{5,1},{6,2},{7,3},{8,12},{9,13},{10,... | collective-permute-start | bytes 526856 | tf_op jit(solution)/shard_map/ppermute | solution.py:204
  171.5 12.5 %collective-permute-done.19 = bf16[168,784]{1,0:T(8,128)(2,1)S(1)} collective-permute-done((bf16[168,784]{1,0:T(8,128)(2,1)S(1)}, bf16[168,784]{1,0:T(8,128)(2,1)S(1)}, u32[]{:S(2)}, u32[]{:S(2)}) %collective-permute-start.19) | collective-permute-done | bytes 263456 | tf_op jit(solution)/shard_map/ppermute | solution.py:204
  184.1 4.3 %collective-permute-done.22 = bf16[112,784]{1,0:T(8,128)(2,1)S(1)} collective-permute-done((bf16[112,784]{1,0:T(8,128)(2,1)S(1)}, bf16[112,784]{1,0:T(8,128)(2,1)S(1)}, u32[]{:S(2)}, u32[]{:S(2)}) %collective-permute-start.22) | collective-permute-done | bytes 175648 | tf_op jit(solution)/shard_map/ppermute | solution.py:204
  188.4 5.9 %collective-permute-done.23 = bf16[112,784]{1,0:T(8,128)(2,1)S(1)} collective-permute-done((bf16[112,784]{1,0:T(8,128)(2,1)S(1)}, bf16[112,784]{1,0:T(8,128)(2,1)S(1)}, u32[]{:S(2)}, u32[]{:S(2)}) %collective-permute-start.23) | collective-permute-done | bytes 175648 | tf_op jit(solution)/shard_map/ppermute | solution.py:204
  (99 shorter events, 35.0 us)
Async XLA Ops:
  0.6 40.5 %collective-permute-start.6 = (bf16[784,56]{0,1:T(8,128)(2,1)}, bf16[784,56]{0,1:T(8,128)(2,1)S(1)}, u32[]{:S(2)}, u32[]{:S(2)}) collective-permute-start(bf16[784,56]{0,1:T(8,128)(2,1)} %param.5), channel_id=1, source_target_pairs={{0,8},{1,9},{2,10},{3,11},{4,12},{5,13},{6,14},{7,15},{8,0},{9,1},... | collective-permute-start | bytes 263432 | tf_op jit(solution)/shard_map/ppermute | solution.py:204
  2.2 39.5 %collective-permute-start.7 = (bf16[784,56]{0,1:T(8,128)(2,1)}, bf16[784,56]{0,1:T(8,128)(2,1)S(1)}, u32[]{:S(2)}, u32[]{:S(2)}) collective-permute-start(bf16[784,56]{0,1:T(8,128)(2,1)} %param.5), channel_id=1, source_target_pairs={{0,16},{1,17},{2,18},{3,19},{4,20},{5,21},{6,22},{7,23},{8,24},{9,... | collective-permute-start | bytes 263432 | tf_op jit(solution)/shard_map/ppermute | solution.py:204
  3.7 38.5 %collective-permute-start.8 = (bf16[784,56]{0,1:T(8,128)(2,1)}, bf16[784,56]{0,1:T(8,128)(2,1)S(1)}, u32[]{:S(2)}, u32[]{:S(2)}) collective-permute-start(bf16[784,56]{0,1:T(8,128)(2,1)} %param.5), channel_id=1, source_target_pairs={{0,24},{1,25},{2,26},{3,27},{4,28},{5,29},{6,30},{7,31},{8,16},{9,... | collective-permute-start | bytes 263432 | tf_op jit(solution)/shard_map/ppermute | solution.py:204
  18.9 23.4 %collective-permute-start.3 = (bf16[2,112,2048]{2,1,0:T(8,128)(2,1)}, bf16[2,112,2048]{2,1,0:T(8,128)(2,1)}, u32[]{:S(2)}, u32[]{:S(2)}) collective-permute-start(bf16[2,112,2048]{2,1,0:T(8,128)(2,1)} %contract.3.refs_0_.own_ref), channel_id=1, source_target_pairs={{0,8},{1,9},{2,10},{3,11},{4,12},{5,13},{6,14},{7,15},{8,0},{9,1},... | collective-permute-start | bytes 2752520 | tf_op jit(solution)/shard_map/ppermute | solution.py:204
  20.4 21.9 %collective-permute-start.4 = (bf16[2,112,2048]{2,1,0:T(8,128)(2,1)}, bf16[2,112,2048]{2,1,0:T(8,128)(2,1)}, u32[]{:S(2)}, u32[]{:S(2)}) collective-permute-start(bf16[2,112,2048]{2,1,0:T(8,128)(2,1)} %contract.3.refs_0_.own_ref), channel_id=1, source_target_pairs={{0,16},{1,17},{2,18},{3,19},{4,20},{5,21},{6,22},{7,23},{8,24},{9,... | collective-permute-start | bytes 2752520 | tf_op jit(solution)/shard_map/ppermute | solution.py:204
  41.1 33.2 %collective-permute-start = (bf16[2,168,2048]{2,1,0:T(8,128)(2,1)S(1)}, bf16[2,168,2048]{2,1,0:T(8,128)(2,1)S(1)}, u32[]{:S(2)}, u32[]{:S(2)}) collective-permute-start(bf16[2,168,2048]{2,1,0:T(8,128)(2,1)S(1)} %contract.4.refs_1_.own_ref), channel_id=1, source_target_pairs={{0,8},{1,9},{2,10},{3,11},{4,12},{5,13},{6,14},{7,15},{8,0},{9,1},... | collective-permute-start | bytes 4128776 | tf_op jit(solution)/shard_map/ppermute | solution.py:204
  41.7 33.2 %collective-permute-start.1 = (bf16[2,168,2048]{2,1,0:T(8,128)(2,1)S(1)}, bf16[2,168,2048]{2,1,0:T(8,128)(2,1)}, u32[]{:S(2)}, u32[]{:S(2)}) collective-permute-start(bf16[2,168,2048]{2,1,0:T(8,128)(2,1)S(1)} %contract.4.refs_1_.own_ref), channel_id=1, source_target_pairs={{0,16},{1,17},{2,18},{3,19},{4,20},{5,21},{6,22},{7,23},{8,24},{9,... | collective-permute-start | bytes 4128776 | tf_op jit(solution)/shard_map/ppermute | solution.py:204
  42.2 52.4 %collective-permute-start.5 = (bf16[2,112,2048]{2,1,0:T(8,128)(2,1)}, bf16[2,112,2048]{2,1,0:T(8,128)(2,1)}, u32[]{:S(2)}, u32[]{:S(2)}) collective-permute-start(bf16[2,112,2048]{2,1,0:T(8,128)(2,1)} %collective-permute-done.3.x_ref), channel_id=1, source_target_pairs={{0,16},{1,17},{2,18},{3,19},{4,20},{5,21},{6,22},{7,23},{8,24},{9,... | collective-permute-start | bytes 2752520 | tf_op jit(solution)/shard_map/ppermute | solution.py:204
  59.5 45.8 %collective-permute-start.13 = (bf16[2,112,2048]{2,1,0:T(8,128)(2,1)}, bf16[2,112,2048]{2,1,0:T(8,128)(2,1)}, u32[]{:S(2)}, u32[]{:S(2)}) collective-permute-start(bf16[2,112,2048]{2,1,0:T(8,128)(2,1)} %get-tuple-element.86.own_ref), channel_id=1, source_target_pairs={{0,8},{1,9},{2,10},{3,11},{4,12},{5,13},{6,14},{7,15},{8,0},{9,1},... | collective-permute-start | bytes 2752520 | tf_op jit(solution)/shard_map/ppermute | solution.py:204
  61.0 50.4 %collective-permute-start.14 = (bf16[2,112,2048]{2,1,0:T(8,128)(2,1)}, bf16[2,112,2048]{2,1,0:T(8,128)(2,1)}, u32[]{:S(2)}, u32[]{:S(2)}) collective-permute-start(bf16[2,112,2048]{2,1,0:T(8,128)(2,1)} %get-tuple-element.86.own_ref), channel_id=1, source_target_pairs={{0,16},{1,17},{2,18},{3,19},{4,20},{5,21},{6,22},{7,23},{8,24},{9,... | collective-permute-start | bytes 2752520 | tf_op jit(solution)/shard_map/ppermute | solution.py:204
  74.9 46.0 %collective-permute-start.2 = (bf16[2,168,2048]{2,1,0:T(8,128)(2,1)}, bf16[2,168,2048]{2,1,0:T(8,128)(2,1)}, u32[]{:S(2)}, u32[]{:S(2)}) collective-permute-start(bf16[2,168,2048]{2,1,0:T(8,128)(2,1)} %collective-permute-done.1.y_ref), channel_id=1, source_target_pairs={{0,8},{1,9},{2,10},{3,11},{4,12},{5,13},{6,14},{7,15},{8,0},{9,1},... | collective-permute-start | bytes 4128776 | tf_op jit(solution)/shard_map/ppermute | solution.py:204
  105.3 8.3 %collective-permute-start.9 = (bf16[4,112,784]{2,1,0:T(8,128)(2,1)S(1)}, bf16[4,112,784]{2,1,0:T(8,128)(2,1)S(1)}, u32[]{:S(2)}, u32[]{:S(2)}) collective-permute-start(bf16[4,112,784]{2,1,0:T(8,128)(2,1)S(1)} %get-tuple-element.70), channel_id=1, source_target_pairs={{0,1},{1,0},{2,3},{3,2},{4,5},{5,4},{6,7},{7,6},{8,9},{9,8},{10,11... | collective-permute-start | bytes 2107400 | tf_op jit(solution)/shard_map/ppermute | solution.py:204
  111.4 25.4 %collective-permute-start.15 = (bf16[2,112,2048]{2,1,0:T(8,128)(2,1)}, bf16[2,112,2048]{2,1,0:T(8,128)(2,1)}, u32[]{:S(2)}, u32[]{:S(2)}) collective-permute-start(bf16[2,112,2048]{2,1,0:T(8,128)(2,1)} %collective-permute-done.13.x_ref), channel_id=1, source_target_pairs={{0,16},{1,17},{2,18},{3,19},{4,20},{5,21},{6,22},{7,23},{8,24},{9,... | collective-permute-start | bytes 2752520 | tf_op jit(solution)/shard_map/ppermute | solution.py:204
  114.3 21.1 %collective-permute-start.10 = (bf16[112,784]{1,0:T(8,128)(2,1)S(1)}, bf16[112,784]{1,0:T(8,128)(2,1)S(1)}, u32[]{:S(2)}, u32[]{:S(2)}) collective-permute-start(bf16[112,784]{1,0:T(8,128)(2,1)S(1)} %get-tuple-element.77), channel_id=1, source_target_pairs={{0,2},{1,3},{2,0},{3,1},{4,6},{5,7},{6,4},{7,5},{8,10},{9,11},{10,... | collective-permute-start | bytes 526856 | tf_op jit(solution)/shard_map/ppermute | solution.py:204
  114.8 20.6 %collective-permute-start.11 = (bf16[112,784]{1,0:T(8,128)(2,1)S(1)}, bf16[112,784]{1,0:T(8,128)(2,1)S(1)}, u32[]{:S(2)}, u32[]{:S(2)}) collective-permute-start(bf16[112,784]{1,0:T(8,128)(2,1)S(1)} %get-tuple-element.80), channel_id=1, source_target_pairs={{0,4},{1,5},{2,6},{3,7},{4,0},{5,1},{6,2},{7,3},{8,12},{9,13},{10,... | collective-permute-start | bytes 526856 | tf_op jit(solution)/shard_map/ppermute | solution.py:204
  117.4 18.0 %collective-permute-start.12 = (bf16[112,784]{1,0:T(8,128)(2,1)S(1)}, bf16[112,784]{1,0:T(8,128)(2,1)S(1)}, u32[]{:S(2)}, u32[]{:S(2)}) collective-permute-start(bf16[112,784]{1,0:T(8,128)(2,1)S(1)} %get-tuple-element.83), channel_id=1, source_target_pairs={{0,6},{1,7},{2,4},{3,5},{4,2},{5,3},{6,0},{7,1},{8,14},{9,15},{10,... | collective-permute-start | bytes 526856 | tf_op jit(solution)/shard_map/ppermute | solution.py:204
  140.7 20.1 %collective-permute-start.17 = (bf16[168,784]{1,0:T(8,128)(2,1)S(1)}, bf16[168,784]{1,0:T(8,128)(2,1)S(1)}, u32[]{:S(2)}, u32[]{:S(2)}) collective-permute-start(bf16[168,784]{1,0:T(8,128)(2,1)S(1)} %get-tuple-element.97), channel_id=1, source_target_pairs={{0,2},{1,3},{2,0},{3,1},{4,6},{5,7},{6,4},{7,5},{8,10},{9,11},{10,... | collective-permute-start | bytes 790280 | tf_op jit(solution)/shard_map/ppermute | solution.py:204
  141.3 19.6 %collective-permute-start.18 = (bf16[168,784]{1,0:T(8,128)(2,1)S(1)}, bf16[168,784]{1,0:T(8,128)(2,1)S(1)}, u32[]{:S(2)}, u32[]{:S(2)}) collective-permute-start(bf16[168,784]{1,0:T(8,128)(2,1)S(1)} %get-tuple-element.100), channel_id=1, source_target_pairs={{0,4},{1,5},{2,6},{3,7},{4,0},{5,1},{6,2},{7,3},{8,12},{9,13},{10,... | collective-permute-start | bytes 790280 | tf_op jit(solution)/shard_map/ppermute | solution.py:204
  158.9 4.5 %collective-permute-start.26 = (f32[8,128]{1,0:T(8,128)S(1)}, f32[8,128]{1,0:T(8,128)S(1)}, u32[]{:S(2)}, u32[]{:S(2)}) collective-permute-start(f32[8,128]{1,0:T(8,128)S(1)} %broadcast_add_fusion), channel_id=1, source_target_pairs={{0,4},{1,5},{2,6},{3,7},{4,0},{5,1},{6,2},{7,3},{8,12},{9,13},{10,... | collective-permute-start | bytes 12296 | tf_op jit(solution)/shard_map/ppermute | solution.py:204
  160.8 5.3 %collective-permute-start.20 = (bf16[4,112,784]{2,1,0:T(8,128)(2,1)S(1)}, bf16[4,112,784]{2,1,0:T(8,128)(2,1)S(1)}, u32[]{:S(2)}, u32[]{:S(2)}) collective-permute-start(bf16[4,112,784]{2,1,0:T(8,128)(2,1)S(1)} %get-tuple-element.104), channel_id=1, source_target_pairs={{0,1},{1,0},{2,3},{3,2},{4,5},{5,4},{6,7},{7,6},{8,9},{9,8},{10,11... | collective-permute-start | bytes 2107400 | tf_op jit(solution)/shard_map/ppermute | solution.py:204
  161.0 23.0 %collective-permute-start.19 = (bf16[168,784]{1,0:T(8,128)(2,1)S(1)}, bf16[168,784]{1,0:T(8,128)(2,1)S(1)}, u32[]{:S(2)}, u32[]{:S(2)}) collective-permute-start(bf16[168,784]{1,0:T(8,128)(2,1)S(1)} %get-tuple-element.102), channel_id=1, source_target_pairs={{0,6},{1,7},{2,4},{3,5},{4,2},{5,3},{6,0},{7,1},{8,14},{9,15},{10,... | collective-permute-start | bytes 790280 | tf_op jit(solution)/shard_map/ppermute | solution.py:204
  166.9 17.2 %collective-permute-start.21 = (bf16[112,784]{1,0:T(8,128)(2,1)S(1)}, bf16[112,784]{1,0:T(8,128)(2,1)S(1)}, u32[]{:S(2)}, u32[]{:S(2)}) collective-permute-start(bf16[112,784]{1,0:T(8,128)(2,1)S(1)} %get-tuple-element.106), channel_id=1, source_target_pairs={{0,2},{1,3},{2,0},{3,1},{4,6},{5,7},{6,4},{7,5},{8,10},{9,11},{10,... | collective-permute-start | bytes 526856 | tf_op jit(solution)/shard_map/ppermute | solution.py:204
  168.6 19.8 %collective-permute-start.22 = (bf16[112,784]{1,0:T(8,128)(2,1)S(1)}, bf16[112,784]{1,0:T(8,128)(2,1)S(1)}, u32[]{:S(2)}, u32[]{:S(2)}) collective-permute-start(bf16[112,784]{1,0:T(8,128)(2,1)S(1)} %get-tuple-element.107), channel_id=1, source_target_pairs={{0,4},{1,5},{2,6},{3,7},{4,0},{5,1},{6,2},{7,3},{8,12},{9,13},{10,... | collective-permute-start | bytes 526856 | tf_op jit(solution)/shard_map/ppermute | solution.py:204
  171.0 23.3 %collective-permute-start.23 = (bf16[112,784]{1,0:T(8,128)(2,1)S(1)}, bf16[112,784]{1,0:T(8,128)(2,1)S(1)}, u32[]{:S(2)}, u32[]{:S(2)}) collective-permute-start(bf16[112,784]{1,0:T(8,128)(2,1)S(1)} %get-tuple-element.108), channel_id=1, source_target_pairs={{0,6},{1,7},{2,4},{3,5},{4,2},{5,3},{6,0},{7,1},{8,14},{9,15},{10,... | collective-permute-start | bytes 526856 | tf_op jit(solution)/shard_map/ppermute | solution.py:204
  (21 other events, 160.9 us)

commit v7 on v6

--- a/solution.py
+++ b/solution.py
@@ -11,7 +11,7 @@
 F32 = jnp.float32
 BF16 = jnp.bfloat16
 AXES = ("outer", "inner")
-COLUMN_TILE = 256
+COLUMN_TILE = 128
 CUTS = (0, 2, 5, 7)
 ROUTES = "yxy"
 XY_DUE = ()

time: 197 us -> 201 us (1.020)
  Pallas kernels: 78.3 us -> 85.8 us
  waiting for transfers between devices: 66.6 us -> 63.3 us
    pallas_call x3, Pallas kernels: 49.5 us -> 56.9 us  [contract(): pl.pallas_call(functools.partial(last_kernel, cuts, scale) if last else f...]
    ppermute x28, waiting for transfers between devices: 66.6 us -> 63.3 us  [move(): return lax.ppermute(value, AXES, pairs(target))]
  transfers between devices with their start and end apart: 28 -> 28, of which waited for: 11 -> 11; matrix products, arithmetic and copies ran while one was open for 4% -> 4% of each run, Pallas kernels for 40% -> 43%
where the time goes in v7:
time: 201 us; the launch traced here: 200 us
  Pallas kernels  85.8 us (43%)
  waiting for transfers between devices  63.3 us (31%)
  starting transfers between devices  28.7 us (14%)
  local copies, waits for them, and re-layouts  15.8 us (8%)
  other arithmetic  4.44 us (2%)
    ppermute x28, waiting for transfers between devices, move(): return lax.ppermute(value, AXES, pairs(target))  63.3 us
    pallas_call x3, Pallas kernels, contract(): pl.pallas_call(functools.partial(last_kernel, cuts, scale) if last else f...  56.9 us
    ppermute x28, starting transfers between devices, move(): return lax.ppermute(value, AXES, pairs(target))  28.7 us
    pallas_call x3, Pallas kernels, gram_chunk(): pl.pallas_call(functools.partial(gram_kernel, len(blocks) - 3), in_specs=...  26.5 us
    unnamed x37, local copies, waits for them, and re-layouts  10.5 us
  transfers between devices with their start and end apart: 28, of which 11 were waited for; matrix products, arithmetic and copies ran while one was open for 4% of the time, Pallas kernels for 43%

profile of v7, /device:TPU:8, one launch (start us, length us, event | category | flops | bytes accessed | tf_op | source)
XLA Modules:
  0.0 199.6 jit_solution(8205211065218492929)
XLA Ops:
  4.2 17.9 %contract.3.refs_0_.own_ref = bf16[2,112,2048]{2,1,0:T(8,128)(2,1)} custom-call(bf16[2,7,56,2048]{3,2,1,0:T(8,128)(2,1)} %bitcast.31, bf16[56,56,2048]{2,1,0:T(8,128)(2,1)} %q_ref.3), custom_call_target="tpu_custom_call" | custom-call | flops 30000001024 | bytes 1000 | tf_op jit(solution)/shard_map/contract/pallas_call | solution.py:105
  25.1 20.0 %contract.4.refs_1_.own_ref = bf16[2,168,2048]{2,1,0:T(8,128)(2,1)S(1)} custom-call(bf16[2,7,56,2048]{3,2,1,0:T(8,128)(2,1)} %bitcast.32, bf16[56,56,2048]{2,1,0:T(8,128)(2,1)} %q_ref.3), custom_call_target="tpu_custom_call" | custom-call | flops 30000001024 | bytes 1000 | tf_op jit(solution)/shard_map/contract/pallas_call | solution.py:105
  46.3 1.6 collective-permute-start.5
  47.9 19.0 %contract.5 = (bf16[2,112,2048]{2,1,0:T(8,128)(2,1)}, bf16[2,392,2048]{2,1,0:T(8,128)(2,1)}) custom-call(bf16[2,7,56,2048]{3,2,1,0:T(8,128)(2,1)} %bitcast.33, bf16[56,56,2048]{2,1,0:T(8,128)(2,1)} %q_ref.3, bf16[2,112,2048]{2,1,0:T(8,128)(2,1)} %contract.3.refs_0_.own_ref, bf16[2,168,2048]{2,1,0:T(8,128)(2,1)} %copy-done), custom_call_target="tpu_custom_call" | custom-call | flops 30000001024 | bytes 1000 | tf_op jit(solution)/shard_map/contract/pallas_call | solution.py:105
  70.8 7.6 %collective-permute-done.x_ref = bf16[2,168,2048]{2,1,0:T(8,128)(2,1)S(1)} collective-permute-done((bf16[2,168,2048]{2,1,0:T(8,128)(2,1)S(1)}, bf16[2,168,2048]{2,1,0:T(8,128)(2,1)S(1)}, u32[]{:S(2)}, u32[]{:S(2)}) %collective-permute-start) | collective-permute-done | bytes 1376288 | tf_op jit(solution)/shard_map/ppermute | solution.py:204
  81.6 17.1 %collective-permute-done.5.refs_0_ = bf16[2,112,2048]{2,1,0:T(8,128)(2,1)} collective-permute-done((bf16[2,112,2048]{2,1,0:T(8,128)(2,1)}, bf16[2,112,2048]{2,1,0:T(8,128)(2,1)}, u32[]{:S(2)}, u32[]{:S(2)}) %collective-permute-start.5) | collective-permute-done | bytes 917536 | tf_op jit(solution)/shard_map/ppermute | solution.py:204
  98.7 1.9 copy-done.4
  100.6 8.0 %gram.3 = (bf16[4,112,784]{2,1,0:T(8,128)(2,1)S(1)}, bf16[4,112,784]{2,1,0:T(8,128)(2,1)S(1)}, f32[56,2048]{1,0:T(8,128)S(1)}) custom-call(s32[1]{0:T(128)} %bitcast.3.core_ref, bf16[2,112,2048]{2,1,0:T(8,128)(2,1)} %contract.3.refs_0_.own_ref, bf16[2,112,2048]{2,1,0:T(8,128)(2,1)} %collective-permute-done.3.x_ref, ...), custom_call_target="tpu_custom_call" | custom-call | flops 4000000000 | bytes 1000 | tf_op jit(solution)/shard_map/gram/pallas_call | solution.py:161
  109.4 6.1 %collective-permute-done.14.y_ref = bf16[2,112,2048]{2,1,0:T(8,128)(2,1)} collective-permute-done((bf16[2,112,2048]{2,1,0:T(8,128)(2,1)}, bf16[2,112,2048]{2,1,0:T(8,128)(2,1)}, u32[]{:S(2)}, u32[]{:S(2)}) %collective-permute-start.14) | collective-permute-done | bytes 917536 | tf_op jit(solution)/shard_map/ppermute | solution.py:204
  118.7 2.8 %collective-permute-start.11 = (bf16[112,784]{1,0:T(8,128)(2,1)S(1)}, bf16[112,784]{1,0:T(8,128)(2,1)S(1)}, u32[]{:S(2)}, u32[]{:S(2)}) collective-permute-start(bf16[112,784]{1,0:T(8,128)(2,1)S(1)} %get-tuple-element.80), channel_id=1, source_target_pairs={{0,4},{1,5},{2,6},{3,7},{4,0},{5,1},{6,2},{7,3},{8,12},{9,13},{10,... | collective-permute-start | bytes 526856 | tf_op jit(solution)/shard_map/ppermute | solution.py:204
  121.9 3.2 %collective-permute-done.2.refs_0_ = bf16[2,168,2048]{2,1,0:T(8,128)(2,1)} collective-permute-done((bf16[2,168,2048]{2,1,0:T(8,128)(2,1)}, bf16[2,168,2048]{2,1,0:T(8,128)(2,1)}, u32[]{:S(2)}, u32[]{:S(2)}) %collective-permute-start.2) | collective-permute-done | bytes 1376288 | tf_op jit(solution)/shard_map/ppermute | solution.py:204
  126.4 1.9 copy-done.5
  129.3 10.2 %gram.4 = (bf16[4,168,784]{2,1,0:T(8,128)(2,1)S(1)}, bf16[4,168,784]{2,1,0:T(8,128)(2,1)}, f32[56,2048]{1,0:T(8,128)S(1)}) custom-call(s32[1]{0:T(128)} %bitcast.3.core_ref, bf16[2,168,2048]{2,1,0:T(8,128)(2,1)S(1)} %copy-done.1, bf16[2,168,2048]{2,1,0:T(8,128)(2,1)S(1)} %copy-done.3, bf16[2,168,2048]{2,1,0:T(8,128)(2,1)} %collective-permute-done.1.y_ref, ...), custom_call_target="tpu_custom_call" | custom-call | flops 4000000000 | bytes 1000 | tf_op jit(solution)/shard_map/gram/pallas_call | solution.py:161
  141.0 3.0 %collective-permute-done.16.recv_ref = bf16[4,168,784]{2,1,0:T(8,128)(2,1)S(1)} collective-permute-done((bf16[4,168,784]{2,1,0:T(8,128)(2,1)}, bf16[4,168,784]{2,1,0:T(8,128)(2,1)S(1)}, u32[]{:S(2)}, u32[]{:S(2)}) %collective-permute-start.16) | collective-permute-done | bytes 1053728 | tf_op jit(solution)/shard_map/ppermute | solution.py:204
  145.4 2.6 %collective-permute-start.18 = (bf16[168,784]{1,0:T(8,128)(2,1)S(1)}, bf16[168,784]{1,0:T(8,128)(2,1)S(1)}, u32[]{:S(2)}, u32[]{:S(2)}) collective-permute-start(bf16[168,784]{1,0:T(8,128)(2,1)S(1)} %get-tuple-element.100), channel_id=1, source_target_pairs={{0,4},{1,5},{2,6},{3,7},{4,0},{5,1},{6,2},{7,3},{8,12},{9,13},{10,... | collective-permute-start | bytes 790280 | tf_op jit(solution)/shard_map/ppermute | solution.py:204
  148.0 1.9 copy-done.6
  149.9 8.3 %gram.5 = (bf16[4,112,784]{2,1,0:T(8,128)(2,1)S(1)}, bf16[4,112,784]{2,1,0:T(8,128)(2,1)S(1)}, f32[56,2048]{1,0:T(8,128)S(1)}) custom-call(s32[1]{0:T(128)} %bitcast.3.core_ref, bf16[2,112,2048]{2,1,0:T(8,128)(2,1)} %get-tuple-element.86.own_ref, bf16[2,112,2048]{2,1,0:T(8,128)(2,1)} %collective-permute-done.13.x_ref, ...), custom_call_target="tpu_custom_call" | custom-call | flops 4000000000 | bytes 1000 | tf_op jit(solution)/shard_map/gram/pallas_call | solution.py:161
  161.4 1.6 collective-permute-start.25
  165.6 1.9 collective-permute-done.26
  171.0 1.7 collective-permute-start.21
  172.7 2.4 %collective-permute-start.22 = (bf16[112,784]{1,0:T(8,128)(2,1)S(1)}, bf16[112,784]{1,0:T(8,128)(2,1)S(1)}, u32[]{:S(2)}, u32[]{:S(2)}) collective-permute-start(bf16[112,784]{1,0:T(8,128)(2,1)S(1)} %get-tuple-element.107), channel_id=1, source_target_pairs={{0,4},{1,5},{2,6},{3,7},{4,0},{5,1},{6,2},{7,3},{8,12},{9,13},{10,... | collective-permute-start | bytes 526856 | tf_op jit(solution)/shard_map/ppermute | solution.py:204
  175.6 12.5 %collective-permute-done.19 = bf16[168,784]{1,0:T(8,128)(2,1)S(1)} collective-permute-done((bf16[168,784]{1,0:T(8,128)(2,1)S(1)}, bf16[168,784]{1,0:T(8,128)(2,1)S(1)}, u32[]{:S(2)}, u32[]{:S(2)}) %collective-permute-start.19) | collective-permute-done | bytes 263456 | tf_op jit(solution)/shard_map/ppermute | solution.py:204
  188.2 4.3 %collective-permute-done.22 = bf16[112,784]{1,0:T(8,128)(2,1)S(1)} collective-permute-done((bf16[112,784]{1,0:T(8,128)(2,1)S(1)}, bf16[112,784]{1,0:T(8,128)(2,1)S(1)}, u32[]{:S(2)}, u32[]{:S(2)}) %collective-permute-start.22) | collective-permute-done | bytes 175648 | tf_op jit(solution)/shard_map/ppermute | solution.py:204
  192.5 5.8 %collective-permute-done.23 = bf16[112,784]{1,0:T(8,128)(2,1)S(1)} collective-permute-done((bf16[112,784]{1,0:T(8,128)(2,1)S(1)}, bf16[112,784]{1,0:T(8,128)(2,1)S(1)}, u32[]{:S(2)}, u32[]{:S(2)}) %collective-permute-start.23) | collective-permute-done | bytes 175648 | tf_op jit(solution)/shard_map/ppermute | solution.py:204
  (99 shorter events, 34.7 us)
Async XLA Ops:
  0.6 44.6 %collective-permute-start.6 = (bf16[784,56]{0,1:T(8,128)(2,1)}, bf16[784,56]{0,1:T(8,128)(2,1)S(1)}, u32[]{:S(2)}, u32[]{:S(2)}) collective-permute-start(bf16[784,56]{0,1:T(8,128)(2,1)} %param.5), channel_id=1, source_target_pairs={{0,8},{1,9},{2,10},{3,11},{4,12},{5,13},{6,14},{7,15},{8,0},{9,1},... | collective-permute-start | bytes 263432 | tf_op jit(solution)/shard_map/ppermute | solution.py:204
  2.2 43.6 %collective-permute-start.7 = (bf16[784,56]{0,1:T(8,128)(2,1)}, bf16[784,56]{0,1:T(8,128)(2,1)S(1)}, u32[]{:S(2)}, u32[]{:S(2)}) collective-permute-start(bf16[784,56]{0,1:T(8,128)(2,1)} %param.5), channel_id=1, source_target_pairs={{0,16},{1,17},{2,18},{3,19},{4,20},{5,21},{6,22},{7,23},{8,24},{9,... | collective-permute-start | bytes 263432 | tf_op jit(solution)/shard_map/ppermute | solution.py:204
  3.7 42.6 %collective-permute-start.8 = (bf16[784,56]{0,1:T(8,128)(2,1)}, bf16[784,56]{0,1:T(8,128)(2,1)S(1)}, u32[]{:S(2)}, u32[]{:S(2)}) collective-permute-start(bf16[784,56]{0,1:T(8,128)(2,1)} %param.5), channel_id=1, source_target_pairs={{0,24},{1,25},{2,26},{3,27},{4,28},{5,29},{6,30},{7,31},{8,16},{9,... | collective-permute-start | bytes 263432 | tf_op jit(solution)/shard_map/ppermute | solution.py:204
  22.1 24.2 %collective-permute-start.3 = (bf16[2,112,2048]{2,1,0:T(8,128)(2,1)}, bf16[2,112,2048]{2,1,0:T(8,128)(2,1)}, u32[]{:S(2)}, u32[]{:S(2)}) collective-permute-start(bf16[2,112,2048]{2,1,0:T(8,128)(2,1)} %contract.3.refs_0_.own_ref), channel_id=1, source_target_pairs={{0,8},{1,9},{2,10},{3,11},{4,12},{5,13},{6,14},{7,15},{8,0},{9,1},... | collective-permute-start | bytes 2752520 | tf_op jit(solution)/shard_map/ppermute | solution.py:204
  23.6 22.7 %collective-permute-start.4 = (bf16[2,112,2048]{2,1,0:T(8,128)(2,1)}, bf16[2,112,2048]{2,1,0:T(8,128)(2,1)}, u32[]{:S(2)}, u32[]{:S(2)}) collective-permute-start(bf16[2,112,2048]{2,1,0:T(8,128)(2,1)} %contract.3.refs_0_.own_ref), channel_id=1, source_target_pairs={{0,16},{1,17},{2,18},{3,19},{4,20},{5,21},{6,22},{7,23},{8,24},{9,... | collective-permute-start | bytes 2752520 | tf_op jit(solution)/shard_map/ppermute | solution.py:204
  45.2 33.2 %collective-permute-start = (bf16[2,168,2048]{2,1,0:T(8,128)(2,1)S(1)}, bf16[2,168,2048]{2,1,0:T(8,128)(2,1)S(1)}, u32[]{:S(2)}, u32[]{:S(2)}) collective-permute-start(bf16[2,168,2048]{2,1,0:T(8,128)(2,1)S(1)} %contract.4.refs_1_.own_ref), channel_id=1, source_target_pairs={{0,8},{1,9},{2,10},{3,11},{4,12},{5,13},{6,14},{7,15},{8,0},{9,1},... | collective-permute-start | bytes 4128776 | tf_op jit(solution)/shard_map/ppermute | solution.py:204
  45.8 33.2 %collective-permute-start.1 = (bf16[2,168,2048]{2,1,0:T(8,128)(2,1)S(1)}, bf16[2,168,2048]{2,1,0:T(8,128)(2,1)}, u32[]{:S(2)}, u32[]{:S(2)}) collective-permute-start(bf16[2,168,2048]{2,1,0:T(8,128)(2,1)S(1)} %contract.4.refs_1_.own_ref), channel_id=1, source_target_pairs={{0,16},{1,17},{2,18},{3,19},{4,20},{5,21},{6,22},{7,23},{8,24},{9,... | collective-permute-start | bytes 4128776 | tf_op jit(solution)/shard_map/ppermute | solution.py:204
  46.3 52.4 %collective-permute-start.5 = (bf16[2,112,2048]{2,1,0:T(8,128)(2,1)}, bf16[2,112,2048]{2,1,0:T(8,128)(2,1)}, u32[]{:S(2)}, u32[]{:S(2)}) collective-permute-start(bf16[2,112,2048]{2,1,0:T(8,128)(2,1)} %collective-permute-done.3.x_ref), channel_id=1, source_target_pairs={{0,16},{1,17},{2,18},{3,19},{4,20},{5,21},{6,22},{7,23},{8,24},{9,... | collective-permute-start | bytes 2752520 | tf_op jit(solution)/shard_map/ppermute | solution.py:204
  66.9 42.5 %collective-permute-start.13 = (bf16[2,112,2048]{2,1,0:T(8,128)(2,1)}, bf16[2,112,2048]{2,1,0:T(8,128)(2,1)}, u32[]{:S(2)}, u32[]{:S(2)}) collective-permute-start(bf16[2,112,2048]{2,1,0:T(8,128)(2,1)} %get-tuple-element.86.own_ref), channel_id=1, source_target_pairs={{0,8},{1,9},{2,10},{3,11},{4,12},{5,13},{6,14},{7,15},{8,0},{9,1},... | collective-permute-start | bytes 2752520 | tf_op jit(solution)/shard_map/ppermute | solution.py:204
  68.4 47.0 %collective-permute-start.14 = (bf16[2,112,2048]{2,1,0:T(8,128)(2,1)}, bf16[2,112,2048]{2,1,0:T(8,128)(2,1)}, u32[]{:S(2)}, u32[]{:S(2)}) collective-permute-start(bf16[2,112,2048]{2,1,0:T(8,128)(2,1)} %get-tuple-element.86.own_ref), channel_id=1, source_target_pairs={{0,16},{1,17},{2,18},{3,19},{4,20},{5,21},{6,22},{7,23},{8,24},{9,... | collective-permute-start | bytes 2752520 | tf_op jit(solution)/shard_map/ppermute | solution.py:204
  79.0 46.0 %collective-permute-start.2 = (bf16[2,168,2048]{2,1,0:T(8,128)(2,1)}, bf16[2,168,2048]{2,1,0:T(8,128)(2,1)}, u32[]{:S(2)}, u32[]{:S(2)}) collective-permute-start(bf16[2,168,2048]{2,1,0:T(8,128)(2,1)} %collective-permute-done.1.y_ref), channel_id=1, source_target_pairs={{0,8},{1,9},{2,10},{3,11},{4,12},{5,13},{6,14},{7,15},{8,0},{9,1},... | collective-permute-start | bytes 4128776 | tf_op jit(solution)/shard_map/ppermute | solution.py:204
  109.4 8.2 %collective-permute-start.9 = (bf16[4,112,784]{2,1,0:T(8,128)(2,1)S(1)}, bf16[4,112,784]{2,1,0:T(8,128)(2,1)S(1)}, u32[]{:S(2)}, u32[]{:S(2)}) collective-permute-start(bf16[4,112,784]{2,1,0:T(8,128)(2,1)S(1)} %get-tuple-element.70), channel_id=1, source_target_pairs={{0,1},{1,0},{2,3},{3,2},{4,5},{5,4},{6,7},{7,6},{8,9},{9,8},{10,11... | collective-permute-start | bytes 2107400 | tf_op jit(solution)/shard_map/ppermute | solution.py:204
  115.5 25.4 %collective-permute-start.15 = (bf16[2,112,2048]{2,1,0:T(8,128)(2,1)}, bf16[2,112,2048]{2,1,0:T(8,128)(2,1)}, u32[]{:S(2)}, u32[]{:S(2)}) collective-permute-start(bf16[2,112,2048]{2,1,0:T(8,128)(2,1)} %collective-permute-done.13.x_ref), channel_id=1, source_target_pairs={{0,16},{1,17},{2,18},{3,19},{4,20},{5,21},{6,22},{7,23},{8,24},{9,... | collective-permute-start | bytes 2752520 | tf_op jit(solution)/shard_map/ppermute | solution.py:204
  118.3 21.2 %collective-permute-start.10 = (bf16[112,784]{1,0:T(8,128)(2,1)S(1)}, bf16[112,784]{1,0:T(8,128)(2,1)S(1)}, u32[]{:S(2)}, u32[]{:S(2)}) collective-permute-start(bf16[112,784]{1,0:T(8,128)(2,1)S(1)} %get-tuple-element.77), channel_id=1, source_target_pairs={{0,2},{1,3},{2,0},{3,1},{4,6},{5,7},{6,4},{7,5},{8,10},{9,11},{10,... | collective-permute-start | bytes 526856 | tf_op jit(solution)/shard_map/ppermute | solution.py:204
  118.7 20.9 %collective-permute-start.11 = (bf16[112,784]{1,0:T(8,128)(2,1)S(1)}, bf16[112,784]{1,0:T(8,128)(2,1)S(1)}, u32[]{:S(2)}, u32[]{:S(2)}) collective-permute-start(bf16[112,784]{1,0:T(8,128)(2,1)S(1)} %get-tuple-element.80), channel_id=1, source_target_pairs={{0,4},{1,5},{2,6},{3,7},{4,0},{5,1},{6,2},{7,3},{8,12},{9,13},{10,... | collective-permute-start | bytes 526856 | tf_op jit(solution)/shard_map/ppermute | solution.py:204
  121.4 18.1 %collective-permute-start.12 = (bf16[112,784]{1,0:T(8,128)(2,1)S(1)}, bf16[112,784]{1,0:T(8,128)(2,1)S(1)}, u32[]{:S(2)}, u32[]{:S(2)}) collective-permute-start(bf16[112,784]{1,0:T(8,128)(2,1)S(1)} %get-tuple-element.83), channel_id=1, source_target_pairs={{0,6},{1,7},{2,4},{3,5},{4,2},{5,3},{6,0},{7,1},{8,14},{9,15},{10,... | collective-permute-start | bytes 526856 | tf_op jit(solution)/shard_map/ppermute | solution.py:204
  144.8 20.1 %collective-permute-start.17 = (bf16[168,784]{1,0:T(8,128)(2,1)S(1)}, bf16[168,784]{1,0:T(8,128)(2,1)S(1)}, u32[]{:S(2)}, u32[]{:S(2)}) collective-permute-start(bf16[168,784]{1,0:T(8,128)(2,1)S(1)} %get-tuple-element.97), channel_id=1, source_target_pairs={{0,2},{1,3},{2,0},{3,1},{4,6},{5,7},{6,4},{7,5},{8,10},{9,11},{10,... | collective-permute-start | bytes 790280 | tf_op jit(solution)/shard_map/ppermute | solution.py:204
  145.4 19.6 %collective-permute-start.18 = (bf16[168,784]{1,0:T(8,128)(2,1)S(1)}, bf16[168,784]{1,0:T(8,128)(2,1)S(1)}, u32[]{:S(2)}, u32[]{:S(2)}) collective-permute-start(bf16[168,784]{1,0:T(8,128)(2,1)S(1)} %get-tuple-element.100), channel_id=1, source_target_pairs={{0,4},{1,5},{2,6},{3,7},{4,0},{5,1},{6,2},{7,3},{8,12},{9,13},{10,... | collective-permute-start | bytes 790280 | tf_op jit(solution)/shard_map/ppermute | solution.py:204
  163.0 4.5 %collective-permute-start.26 = (f32[8,128]{1,0:T(8,128)S(1)}, f32[8,128]{1,0:T(8,128)S(1)}, u32[]{:S(2)}, u32[]{:S(2)}) collective-permute-start(f32[8,128]{1,0:T(8,128)S(1)} %broadcast_add_fusion), channel_id=1, source_target_pairs={{0,4},{1,5},{2,6},{3,7},{4,0},{5,1},{6,2},{7,3},{8,12},{9,13},{10,... | collective-permute-start | bytes 12296 | tf_op jit(solution)/shard_map/ppermute | solution.py:204
  165.0 5.3 %collective-permute-start.20 = (bf16[4,112,784]{2,1,0:T(8,128)(2,1)S(1)}, bf16[4,112,784]{2,1,0:T(8,128)(2,1)S(1)}, u32[]{:S(2)}, u32[]{:S(2)}) collective-permute-start(bf16[4,112,784]{2,1,0:T(8,128)(2,1)S(1)} %get-tuple-element.104), channel_id=1, source_target_pairs={{0,1},{1,0},{2,3},{3,2},{4,5},{5,4},{6,7},{7,6},{8,9},{9,8},{10,11... | collective-permute-start | bytes 2107400 | tf_op jit(solution)/shard_map/ppermute | solution.py:204
  165.1 23.0 %collective-permute-start.19 = (bf16[168,784]{1,0:T(8,128)(2,1)S(1)}, bf16[168,784]{1,0:T(8,128)(2,1)S(1)}, u32[]{:S(2)}, u32[]{:S(2)}) collective-permute-start(bf16[168,784]{1,0:T(8,128)(2,1)S(1)} %get-tuple-element.102), channel_id=1, source_target_pairs={{0,6},{1,7},{2,4},{3,5},{4,2},{5,3},{6,0},{7,1},{8,14},{9,15},{10,... | collective-permute-start | bytes 790280 | tf_op jit(solution)/shard_map/ppermute | solution.py:204
  171.0 17.2 %collective-permute-start.21 = (bf16[112,784]{1,0:T(8,128)(2,1)S(1)}, bf16[112,784]{1,0:T(8,128)(2,1)S(1)}, u32[]{:S(2)}, u32[]{:S(2)}) collective-permute-start(bf16[112,784]{1,0:T(8,128)(2,1)S(1)} %get-tuple-element.106), channel_id=1, source_target_pairs={{0,2},{1,3},{2,0},{3,1},{4,6},{5,7},{6,4},{7,5},{8,10},{9,11},{10,... | collective-permute-start | bytes 526856 | tf_op jit(solution)/shard_map/ppermute | solution.py:204
  172.7 19.8 %collective-permute-start.22 = (bf16[112,784]{1,0:T(8,128)(2,1)S(1)}, bf16[112,784]{1,0:T(8,128)(2,1)S(1)}, u32[]{:S(2)}, u32[]{:S(2)}) collective-permute-start(bf16[112,784]{1,0:T(8,128)(2,1)S(1)} %get-tuple-element.107), channel_id=1, source_target_pairs={{0,4},{1,5},{2,6},{3,7},{4,0},{5,1},{6,2},{7,3},{8,12},{9,13},{10,... | collective-permute-start | bytes 526856 | tf_op jit(solution)/shard_map/ppermute | solution.py:204
  175.1 23.2 %collective-permute-start.23 = (bf16[112,784]{1,0:T(8,128)(2,1)S(1)}, bf16[112,784]{1,0:T(8,128)(2,1)S(1)}, u32[]{:S(2)}, u32[]{:S(2)}) collective-permute-start(bf16[112,784]{1,0:T(8,128)(2,1)S(1)} %get-tuple-element.108), channel_id=1, source_target_pairs={{0,6},{1,7},{2,4},{3,5},{4,2},{5,3},{6,0},{7,1},{8,14},{9,15},{10,... | collective-permute-start | bytes 526856 | tf_op jit(solution)/shard_map/ppermute | solution.py:204
  (21 other events, 167.7 us)
